TPU v7x, 32 devices: a whole 2x2x4 slice. The times are simulated.
32 devices in a mesh: size: 4 (over z), gz: 8 (over y, x, core).
Axes of the slice: x: 2, y: 2, z: 4, core: 2. Of those that a mesh axis runs over, the one named last changes fastest.
Arguments:
- tissue: int32 [256, 64, 128], P('gz'), may hold values from 0 to 2
- vessel_pressure: float32 [256, 64, 128], P('gz', 'size'), may hold values from -12 to 12
- cond_table: float32 [3], replicated, may hold values from 0.4 to 1.2
- leak_table: float32 [3], replicated, may hold values from 0.2 to 2
- bind_table: float32 [4, 3], P('size'), may hold values from 0.05 to 1
- hindrance: float32 [4], P('size'), may hold values from 0.2 to 1
- diffusivity: float32 [4], P('size'), may hold values from 0.1 to 0.6
- free_conc: float32 [4, 256, 64, 128], P('size', 'gz'), may hold values from 0 to 2
- bound_conc: float32 [4, 256, 64, 128], P('size', 'gz'), may hold values from 0 to 1
Outputs:
- pressure: float32 [256, 64, 128], P('gz', 'size')
- free_out: float32 [4, 256, 64, 128], P('size', 'gz')
- bound_out: float32 [4, 256, 64, 128], P('size', 'gz')
Inputs may be any that keep to these rules, and one draw needn't show every extreme that they name: 0 marks a vessel cell, 1 necrotic tissue, 2 viable tissue.
All inputs are finite; a program needn't handle non-finite values.
Results may differ from a plain program's by a relative error of at most 0.0001.
Values sent between devices are 32-bit elements; how exact they have to be, the bound alone decides.
No kernel may reach another device: no remote copies, remote signals or barrier semaphores. Data moves between devices by JAX's collectives and lax.ppermute only.
A program may use at most 128 MiB of HBM per device.

v0:
```python
import functools
import math
import jax
import jax.numpy as jnp
from jax import lax
from jax.experimental import pallas as pl
from jax.experimental.pallas import tpu as pltpu
from jax.sharding import PartitionSpec as P

TSTEPS = 2
HALO = TSTEPS + 1
DT = 0.1


def select(labels, values):
    return jnp.where(labels == 0, values[0], jnp.where(labels == 1, values[1], values[2]))


def following(cells, axis):
    return pltpu.roll(cells, cells.shape[axis] - 1, axis)


def preceding(cells, axis):
    return pltpu.roll(cells, 1, axis)


def edges(shape):
    row = lax.broadcasted_iota(jnp.int32, shape, 0)
    lane = lax.broadcasted_iota(jnp.int32, shape, 1)
    return (row == 0, row == shape[0] - 1), (lane == 0, lane == shape[1] - 1)


def inside():
    slab = lax.axis_index("gz")
    has_low = (slab > 0).astype(jnp.float32)
    has_high = (slab < lax.axis_size("gz") - 1).astype(jnp.float32)
    return has_low, has_high


def tables(cond_t, leak_t):
    cond = [cond_t[i] for i in range(3)]
    leak = [leak_t[i] for i in range(3)]
    diag = [6.0 * c * c + k for c, k in zip(cond, leak)]
    ratio = [k / d for k, d in zip(leak, diag)]
    gain = [c / d for c, d in zip(cond, diag)]
    return cond, leak, diag, ratio, gain


def image(layer, labels, valid, ends, gain, ratio, p0, scaled, u0):
    q = scaled[layer]
    around = scaled[layer - 1] + scaled[layer + 1]
    for axis in range(2):
        low, high = ends[axis]
        around = around + jnp.where(high, 0.0, following(q, axis))
        around = around + jnp.where(low, 0.0, preceding(q, axis))
    g = select(labels, gain)
    if valid is not None:
        g = g * valid
    u0[layer] = g * (6.0 * q - around) + select(labels, ratio) * p0[layer]


def products(first, count, totals, ends, tissue, leak, diag, p0, u0, cond):
    def body(i, carry):
        layer = i + HALO
        labels = tissue[i]
        p, u = p0[layer], u0[layer]
        d = select(labels, diag)
        du = d * u
        q = cond[layer] * u
        ahead = jnp.where(ends[0][1], 0.0, following(q, 0)) + jnp.where(ends[1][1], 0.0, following(q, 1))
        vertical = cond[layer - 1] * u0[layer - 1] + cond[layer + 1] * u0[layer + 1]
        energy = select(labels, leak) * u * u + q * (6.0 * q - 2.0 * ahead - vertical)
        terms = (d * p * p, du * p, du * u, energy)
        return tuple(a + t.reshape(-1, 8, t.shape[-1]).sum(0) for a, t in zip(carry, terms))

    return lax.fori_loop(first, first + count, body, totals)


def rim_kernel(parts, rim, cond_t, leak_t, bind_t, hinder_t, vp, *refs):
    outer = refs[: parts - 1]
    from_low, from_high, tissue, conc, p0, scaled, u0, cond, sums, kx, ky, kz, rate, wide = refs[parts - 1 :]
    layers, width, _ = vp.shape
    rows = tissue.shape[1]
    me = lax.axis_index("size")
    has_low, has_high = inside()
    cond_v, leak_v, diag_v, ratio_v, gain_v = tables(cond_t, leak_t)
    rate_v = [bind_t[0, i] * DT for i in range(3)]
    hinder = hinder_t[0] * DT
    tis_at = parts * HALO * width
    conc_at = tis_at + HALO * rows

    def place(layer, spot, pressure, labels):
        p = pressure * select(labels, ratio_v)
        p0[layer, spot, :] = p
        scaled[layer, spot, :] = select(labels, cond_v) * p

    for k in range(parts):
        spot = pl.ds(pl.multiple_of(lax.rem(me - k + parts, parts) * width, width), width)
        source = vp if k == 0 else outer[k - 1]
        top = layers - rim if k == 0 else rim

        def fill(i, carry):
            place(i + HALO, spot, source[i], tissue[i, spot, :])
            place(i + (layers - rim + HALO), spot, source[i + top], tissue[i + (layers - rim), spot, :])
            return carry

        lax.fori_loop(0, rim, fill, 0, unroll=2)
        for j in range(HALO):
            at = (k * HALO + j) * width
            for side, layer in ((from_low, j), (from_high, layers + HALO + j)):
                labels = side[pl.ds(pl.multiple_of(tis_at + j * rows + spot.start, width), width), :]
                place(layer, spot, side[at : at + width, :], labels)

    def halo_labels(side, j):
        return side[tis_at + j * rows : tis_at + (j + 1) * rows, :]

    for j in range(HALO):
        cond[j] = select(halo_labels(from_low, j), cond_v) * has_low
        cond[layers + HALO + j] = select(halo_labels(from_high, j), cond_v) * has_high
    for j in range(TSTEPS):
        wide[j] = from_low[conc_at + j * rows : conc_at + (j + 1) * rows, :]
        wide[layers + TSTEPS + j] = from_high[conc_at + j * rows : conc_at + (j + 1) * rows, :]
    rate[0] = select(halo_labels(from_low, HALO - 1), rate_v)
    rate[layers + 1] = select(halo_labels(from_high, 0), rate_v)

    def own(i, carry):
        labels = tissue[i]
        cond[i + HALO] = select(labels, cond_v)
        rate[i + 1] = select(labels, rate_v)
        wide[i + TSTEPS] = conc[i]
        return carry

    lax.fori_loop(0, layers, own, 0, unroll=2)
    ends = edges(tissue.shape[1:])

    def faces(i, carry):
        c = cond[i + 1]
        scaled_c = hinder * c
        kz[i] = scaled_c * cond[i + 2]
        kx[i] = jnp.where(ends[0][1], 0.0, scaled_c * following(c, 0))
        ky[i] = jnp.where(ends[1][1], 0.0, scaled_c * following(c, 1))
        return carry

    lax.fori_loop(0, layers + TSTEPS + 1, faces, 0)

    for j in range(1, HALO):
        image(j, halo_labels(from_low, j), has_low, ends, gain_v, ratio_v, p0, scaled, u0)
        back = HALO - 1 - j
        image(layers + HALO + back, halo_labels(from_high, back), has_high, ends, gain_v, ratio_v, p0, scaled, u0)

    def both(i, carry):
        image(i + HALO, tissue[i], None, ends, gain_v, ratio_v, p0, scaled, u0)
        j = layers - 1 - i
        image(j + HALO, tissue[j], None, ends, gain_v, ratio_v, p0, scaled, u0)
        return carry

    lax.fori_loop(0, rim - 1, both, 0)
    zero = jnp.zeros((8, tissue.shape[2]), jnp.float32)
    fixed = (ends, tissue, leak_v, diag_v, p0, u0, cond)
    totals = products(0, rim - 2, (zero,) * 4, *fixed)
    totals = products(layers - rim + 2, rim - 2, totals, *fixed)
    for i in range(4):
        sums[i] = totals[i]


def core_kernel(parts, rim, cond_t, leak_t, vp, *refs):
    inner = refs[: parts - 1]
    tissue, cond, part, _, _, _, p0, scaled, u0, sums = refs[parts - 1 :]
    layers, width, _ = vp.shape
    me = lax.axis_index("size")
    cond_v, leak_v, diag_v, ratio_v, gain_v = tables(cond_t, leak_t)
    for k in range(parts):
        spot = pl.ds(pl.multiple_of(lax.rem(me - k + parts, parts) * width, width), width)
        source = vp if k == 0 else inner[k - 1]
        start = rim if k == 0 else 0

        def fill(i, carry):
            labels = tissue[i + rim, spot, :]
            p = source[i + start] * select(labels, ratio_v)
            p0[i + (rim + HALO), spot, :] = p
            scaled[i + (rim + HALO), spot, :] = select(labels, cond_v) * p
            return carry

        lax.fori_loop(0, layers - 2 * rim, fill, 0, unroll=2)
    ends = edges(tissue.shape[1:])

    def middle(i, carry):
        image(i + HALO, tissue[i], None, ends, gain_v, ratio_v, p0, scaled, u0)
        return carry

    lax.fori_loop(rim - 1, layers - rim + 1, middle, 0, unroll=2)
    totals = tuple(part[i] for i in range(4))
    totals = products(rim - 2, layers - 2 * rim + 4, totals, ends, tissue, leak_v, diag_v, p0, u0, cond)
    sums[...] = jnp.concatenate([t.sum(0, keepdims=True) for t in totals] * 2, 0)


def transport_kernel(width, diffuse_t, mine, theirs, p0, u0, kx, ky, kz, rate, wide, bound, pressure, free_out, bound_out, first, *coef):
    layers, rows, lanes = bound.shape
    me = lax.axis_index("size")
    has_low, has_high = inside()
    sums = mine[...] + theirs[...]
    rho, drop, second, third = [jnp.sum(sums[i : i + 1, :], axis=1, keepdims=True) for i in range(4)]
    alpha = rho / drop
    rho_next = alpha * alpha * second - rho
    beta = rho_next / rho
    curve = drop - 2.0 * alpha * second + alpha * alpha * third - beta * rho_next / alpha
    alpha_next = rho_next / curve
    on_p = jnp.broadcast_to(alpha + alpha_next * (1.0 + beta), (8, lanes))[None]
    on_u = jnp.broadcast_to(-alpha_next * alpha, (8, lanes))[None]
    diffuse = diffuse_t[0] * DT

    def combine(p, u):
        shape = p.shape
        return (on_p * p.reshape(-1, 8, lanes) + on_u * u.reshape(-1, 8, lanes)).reshape(shape)

    spot = pl.ds(pl.multiple_of(me * width, width), width)

    def own(i, carry):
        pressure[i] = combine(p0[i + HALO, spot, :], u0[i + HALO, spot, :])
        return carry

    lax.fori_loop(0, layers, own, 0, unroll=4)
    ends = edges((rows, lanes))

    def halves(flow):
        out = jnp.maximum(flow, 0.0) + diffuse
        return out, out - flow

    def advance(i, carry):
        here, low_flow = carry
        above = combine(p0[i + HALO], u0[i + HALO])
        conc = wide[i + 1]
        high_flow = kz[i + 1] * (here - above)
        p_low, n_low = halves(low_flow)
        p_high, n_high = halves(high_flow)
        leave = p_high + n_low + rate[i]
        weights = [p_low, n_high]
        moved = p_low * wide[i] + n_high * wide[i + 2]
        for axis, face in ((0, kx), (1, ky)):
            at_low, at_high = ends[axis]
            flow = face[i + 1] * (here - following(here, axis))
            p_high, n_high = halves(flow)
            p_low, n_low = halves(preceding(flow, axis))
            leave = leave + (p_high + n_low)
            n_high = jnp.where(at_high, 0.0, n_high)
            p_low = jnp.where(at_low, 0.0, p_low)
            weights += [p_low, n_high]
            moved = moved + p_low * preceding(conc, axis) + n_high * following(conc, axis)
        stay = 1.0 - leave
        valid = jnp.where(i == 0, has_low, jnp.where(i == layers + 1, has_high, 1.0))
        first[i] = (stay * conc + moved) * valid
        slot = lax.rem(i, 2)
        for ref, weight in zip(coef, [stay] + weights):
            ref[slot] = weight
        return above, high_flow

    start = combine(p0[TSTEPS], u0[TSTEPS])
    carry = (start, kz[0] * (combine(p0[1], u0[1]) - start))
    carry = lax.fori_loop(0, 2, advance, carry)

    def body(i, carry):
        here = first[i - 1]
        slot = lax.rem(i - 1, 2)
        old = [ref[slot] for ref in coef]
        carry = advance(i, carry)
        stay, z_low, z_high, x_low, x_high, y_low, y_high = old
        result = stay * here + z_low * first[i - 2] + z_high * first[i]
        result = result + x_low * preceding(here, 0) + x_high * following(here, 0)
        free_out[i - 2] = result + y_low * preceding(here, 1) + y_high * following(here, 1)
        bound_out[i - 2] = bound[i - 2] + rate[i - 1] * (wide[i] + here)
        return carry

    lax.fori_loop(2, layers + 2, body, carry)


def shifts(array, axis):
    count = lax.axis_size(axis)
    moved = []
    for k in range(1, count):
        moved.append(lax.ppermute(array, axis, [(i, (i + k) % count) for i in range(count)]))
    return moved


def across(low, high):
    count = lax.axis_size("gz")
    from_low = lax.ppermute(high, "gz", [(i, i + 1) for i in range(count - 1)])
    from_high = lax.ppermute(low, "gz", [(i + 1, i) for i in range(count - 1)])
    return from_low, from_high


def total_over(array, axis):
    count = lax.axis_size(axis)
    step = 1
    while True:
        other = lax.ppermute(array, axis, [(i, i ^ step) for i in range(count)])
        step *= 2
        if step == count:
            return array, other
        array = array + other


def smem():
    return pl.BlockSpec(memory_space=pltpu.SMEM)


def vmem():
    return pl.BlockSpec(memory_space=pltpu.VMEM)


def f32(*shape):
    return jax.ShapeDtypeStruct(shape, jnp.float32)


def call(kernel, outs, scalars, arrays, scratch=(), aliases={}):
    size = sum(4 * math.prod(a.shape) for a in list(outs) + list(arrays) + list(scratch))
    return pl.pallas_call(
        kernel,
        out_shape=tuple(outs),
        in_specs=[smem()] * len(scalars) + [vmem()] * len(arrays),
        out_specs=(vmem(),) * len(outs),
        scratch_shapes=[pltpu.VMEM(s.shape, s.dtype) for s in scratch],
        input_output_aliases=aliases,
        compiler_params=pltpu.CompilerParams(vmem_limit_bytes=size + (4 << 20)),
    )(*scalars, *arrays)


def program(tissue, vessel_pressure, cond_table, leak_table, bind_table, hindrance, diffusivity, free_conc, bound_conc):
    layers, width, lanes = vessel_pressure.shape
    rows = tissue.shape[1]
    parts = rows // width
    rim = max(HALO, layers // 4)
    conc, bound = free_conc[0], bound_conc[0]
    rims = jnp.concatenate([vessel_pressure[:rim], vessel_pressure[layers - rim :]], 0)
    outer = shifts(rims, "size")
    inner = shifts(vessel_pressure[rim : layers - rim], "size")
    blocks = [rims] + outer

    def payload(pieces, labels, cells):
        arrays = pieces + [labels.astype(jnp.float32), cells]
        return jnp.concatenate([a.reshape(-1, lanes) for a in arrays], 0)

    low = payload([b[:HALO] for b in blocks], tissue[:HALO], conc[:TSTEPS])
    high = payload([b[2 * rim - HALO :] for b in blocks], tissue[layers - HALO :], conc[layers - TSTEPS :])
    from_low, from_high = across(low, high)
    extended = f32(layers + 2 * HALO, rows, lanes)
    stepped = f32(layers + 2, rows, lanes)
    faces = f32(layers + TSTEPS + 1, rows, lanes)
    p0, scaled, u0, cond, part, kx, ky, kz, rate, wide = call(
        functools.partial(rim_kernel, parts, rim),
        [extended] * 4 + [f32(4, 8, lanes), faces, faces, faces, stepped, f32(layers + 2 * TSTEPS, rows, lanes)],
        [cond_table, leak_table, bind_table, hindrance],
        [vessel_pressure, *outer, from_low, from_high, tissue, conc],
    )
    p0, scaled, u0, sums = call(
        functools.partial(core_kernel, parts, rim),
        [extended] * 3 + [f32(8, lanes)],
        [cond_table, leak_table],
        [vessel_pressure, *inner, tissue, cond, part, p0, scaled, u0],
        aliases={2 + parts + 3 + i: i for i in range(3)},
    )
    mine, theirs = total_over(sums, "gz")
    slab = f32(layers, rows, lanes)
    pressure, free, bound = call(
        functools.partial(transport_kernel, width),
        [f32(layers, width, lanes), slab, slab],
        [diffusivity],
        [mine, theirs, p0, u0, kx, ky, kz, rate, wide, bound],
        scratch=[stepped] + [f32(2, rows, lanes)] * 7,
    )
    return pressure, free[None], bound[None]


def solution(mesh):
    return jax.shard_map(
        program,
        mesh=mesh,
        in_specs=(
            P("gz", None, None),
            P("gz", "size", None),
            P(),
            P(),
            P("size", None),
            P("size"),
            P("size"),
            P("size", "gz", None, None),
            P("size", "gz", None, None),
        ),
        out_specs=(P("gz", "size", None), P("size", "gz", None, None), P("size", "gz", None, None)),
        check_vma=False,
    )
```

profile of v0, /device:TPU:8, one launch (start us, length us, event | category | flops | bytes accessed | tf_op | source)
XLA Modules:
  0.0 55.7 jit_solution(8108213933822486822)
XLA Ops:
  0.6 0.9 %fusion.2 = (f32[8,16,128]{2,1,0:T(8,128)S(1)}, f32[8,16,128]{2,1,0:T(8,128)S(1)}) fusion(f32[32,16,128]{2,1,0:T(8,128)} %vp.3), kind=kLoop, calls=%fused_computation.17 | loop fusion | bytes 262144 | tf_op jit(solution)/shard_map/slice | solution.py:333
  1.5 0.0 copy-start.1
  1.5 0.0 copy-start
  1.6 0.0 copy-start.2
  1.6 0.0 copy-start.4
  1.6 0.0 copy-start.5
  1.6 0.0 copy-start.6
  1.6 1.6 %collective-permute-start.3 = (f32[16,16,128]{2,1,0:T(8,128)S(1)}, f32[16,16,128]{2,1,0:T(8,128)S(1)}, u32[]{:S(2)}, u32[]{:S(2)}) collective-permute-start(f32[16,16,128]{2,1,0:T(8,128)S(1)} %pad_maximum_fusion), channel_id=1, source_target_pairs={{0,8},{8,16},{16,24},{24,0},{1,9},{9,17},{17,25},{25,1},{2,10},{10... | collective-permute-start | bytes 393224 | tf_op jit(solution)/shard_map/ppermute | solution.py:280
  3.2 1.1 %collective-permute-start.4 = (f32[16,16,128]{2,1,0:T(8,128)S(1)}, f32[16,16,128]{2,1,0:T(8,128)S(1)}, u32[]{:S(2)}, u32[]{:S(2)}) collective-permute-start(f32[16,16,128]{2,1,0:T(8,128)S(1)} %pad_maximum_fusion), channel_id=1, source_target_pairs={{0,16},{8,24},{16,0},{24,8},{1,17},{9,25},{17,1},{25,9},{2,18},{10... | collective-permute-start | bytes 393224 | tf_op jit(solution)/shard_map/ppermute | solution.py:280
  4.3 1.9 %collective-permute-start.5 = (f32[16,16,128]{2,1,0:T(8,128)S(1)}, f32[16,16,128]{2,1,0:T(8,128)S(1)}, u32[]{:S(2)}, u32[]{:S(2)}) collective-permute-start(f32[16,16,128]{2,1,0:T(8,128)S(1)} %pad_maximum_fusion), channel_id=1, source_target_pairs={{0,24},{8,0},{16,8},{24,16},{1,25},{9,1},{17,9},{25,17},{2,26},{10... | collective-permute-start | bytes 393224 | tf_op jit(solution)/shard_map/ppermute | solution.py:280
  6.3 0.8 %fusion.1 = (f32[3,16,128]{2,1,0:T(8,128)S(1)}, f32[3,16,128]{2,1,0:T(8,128)S(1)}) fusion(f32[32,16,128]{2,1,0:T(8,128)} %vp.3), kind=kLoop, calls=%fused_computation.16 | loop fusion | bytes 98304 | tf_op jit(solution)/shard_map/slice | solution.py:342
  7.0 1.0 %slice_convert_fusion = (f32[3,64,128]{2,1,0:T(8,128)S(1)}, f32[3,64,128]{2,1,0:T(8,128)S(1)}) fusion(s32[32,64,128]{2,1,0:T(8,128)} %refs_3_.1), kind=kLoop, calls=%fused_computation.1 | loop fusion | flops 49152 | bytes 393216 | tf_op jit(solution)/shard_map/convert_element_type | solution.py:339
  8.0 0.9 %fusion = (f32[1,2,64,128]{3,2,1,0:T(8,128)S(1)}, f32[1,2,64,128]{3,2,1,0:T(8,128)S(1)}) fusion(f32[1,32,64,128]{3,2,1,0:T(8,128)} %param.16), kind=kLoop, calls=%fused_computation.15 | loop fusion | bytes 262144 | tf_op jit(solution)/shard_map/slice | solution.py:342
  8.9 3.8 %collective-permute-done.3.refs_0_ = f32[16,16,128]{2,1,0:T(8,128)S(1)} collective-permute-done((f32[16,16,128]{2,1,0:T(8,128)S(1)}, f32[16,16,128]{2,1,0:T(8,128)S(1)}, u32[]{:S(2)}, u32[]{:S(2)}) %collective-permute-start.3) | collective-permute-done | bytes 131104 | tf_op jit(solution)/shard_map/ppermute | solution.py:280
  12.7 1.7 %collective-permute-done.4.refs_1_ = f32[16,16,128]{2,1,0:T(8,128)S(1)} collective-permute-done((f32[16,16,128]{2,1,0:T(8,128)S(1)}, f32[16,16,128]{2,1,0:T(8,128)S(1)}, u32[]{:S(2)}, u32[]{:S(2)}) %collective-permute-start.4) | collective-permute-done | bytes 131104 | tf_op jit(solution)/shard_map/ppermute | solution.py:280
  14.4 1.7 %collective-permute-done.5.refs_2_ = f32[16,16,128]{2,1,0:T(8,128)S(1)} collective-permute-done((f32[16,16,128]{2,1,0:T(8,128)S(1)}, f32[16,16,128]{2,1,0:T(8,128)S(1)}, u32[]{:S(2)}, u32[]{:S(2)}) %collective-permute-start.5) | collective-permute-done | bytes 131104 | tf_op jit(solution)/shard_map/ppermute | solution.py:280
  16.2 1.3 %collective-permute-start.7 = (f32[512,128]{1,0:T(8,128)S(1)}, f32[512,128]{1,0:T(8,128)S(1)}, u32[]{:S(2)}, u32[]{:S(2)}) collective-permute-start(f32[512,128]{1,0:T(8,128)S(1)} %constant_dynamic-update-slice_fusion.6), channel_id=1, source_target_pairs={{1,0},{2,1},{3,2},{4,3},{5,4},{6,5},{7,6},{9,8},{10,9},{11,10},{12... | collective-permute-start | bytes 786440 | tf_op jit(solution)/shard_map/ppermute | solution.py:287
  17.6 3.0 %collective-permute-start.6 = (f32[512,128]{1,0:T(8,128)S(1)}, f32[512,128]{1,0:T(8,128)S(1)}, u32[]{:S(2)}, u32[]{:S(2)}) collective-permute-start(f32[512,128]{1,0:T(8,128)S(1)} %constant_dynamic-update-slice_fusion), channel_id=1, source_target_pairs={{0,1},{1,2},{2,3},{3,4},{4,5},{5,6},{6,7},{8,9},{9,10},{10,11},{11... | collective-permute-start | bytes 786440 | tf_op jit(solution)/shard_map/ppermute | solution.py:286
  20.6 0.0 copy-done.1
  20.7 0.1 collective-permute-start
  20.7 1.7 %collective-permute-start.1 = (f32[16,16,128]{2,1,0:T(8,128)S(1)}, f32[16,16,128]{2,1,0:T(8,128)S(1)}, u32[]{:S(2)}, u32[]{:S(2)}) collective-permute-start(f32[16,16,128]{2,1,0:T(8,128)S(1)} %slice.49), channel_id=1, source_target_pairs={{0,16},{8,24},{16,0},{24,8},{1,17},{9,25},{17,1},{25,9},{2,18},{10... | collective-permute-start | bytes 393224 | tf_op jit(solution)/shard_map/ppermute | solution.py:280
  22.5 1.9 %collective-permute-start.2 = (f32[16,16,128]{2,1,0:T(8,128)S(1)}, f32[16,16,128]{2,1,0:T(8,128)S(1)}, u32[]{:S(2)}, u32[]{:S(2)}) collective-permute-start(f32[16,16,128]{2,1,0:T(8,128)S(1)} %slice.49), channel_id=1, source_target_pairs={{0,24},{8,0},{16,8},{24,16},{1,25},{9,1},{17,9},{25,17},{2,26},{10... | collective-permute-start | bytes 393224 | tf_op jit(solution)/shard_map/ppermute | solution.py:280
  25.1 0.0 collective-permute-done.7.refs_4_
  25.1 0.0 collective-permute-done.6.refs_3_
  25.1 0.0 copy-done
  25.1 0.0 copy-done.2
  25.1 0.0 copy-done.4
  25.1 0.0 copy-done.5
  25.1 0.0 copy-done.6
  25.1 5.9 %shard_map.112 = (f32[38,64,128]{2,1,0:T(8,128)S(1)}, f32[38,64,128]{2,1,0:T(8,128)S(1)}, f32[38,64,128]{2,1,0:T(8,128)S(1)}, f32[38,64,128]{2,1,0:T(8,128)S(1)}...) custom-call(f32[3]{0:T(128)S(1)} %copy-done.4, ...), custom_call_target="tpu_custom_call" | custom-call | tf_op jit(solution)/shard_map/pallas_call | solution.py:316
  31.0 0.0 collective-permute-done.refs_0_
  31.0 1.3 %collective-permute-done.1.refs_1_ = f32[16,16,128]{2,1,0:T(8,128)S(1)} collective-permute-done((f32[16,16,128]{2,1,0:T(8,128)S(1)}, f32[16,16,128]{2,1,0:T(8,128)S(1)}, u32[]{:S(2)}, u32[]{:S(2)}) %collective-permute-start.1) | collective-permute-done | bytes 131104 | tf_op jit(solution)/shard_map/ppermute | solution.py:280
  32.3 2.8 %collective-permute-done.2.refs_2_ = f32[16,16,128]{2,1,0:T(8,128)S(1)} collective-permute-done((f32[16,16,128]{2,1,0:T(8,128)S(1)}, f32[16,16,128]{2,1,0:T(8,128)S(1)}, u32[]{:S(2)}, u32[]{:S(2)}) %collective-permute-start.2) | collective-permute-done | bytes 131104 | tf_op jit(solution)/shard_map/ppermute | solution.py:280
  35.2 0.0 copy-start.3
  35.2 3.7 %shard_map.113 = (f32[38,64,128]{2,1,0:T(8,128)S(1)}, f32[38,64,128]{2,1,0:T(8,128)S(1)}, f32[38,64,128]{2,1,0:T(8,128)S(1)}, f32[8,128]{1,0:T(8,128)S(1)}) custom-call(f32[3]{0:T(128)S(1)} %copy-done.4, f32[3]{0:T(128)S(1)} %copy-done.5, f32[32,16,128]{2,1,0:T(8,128)S(1)} %copy-done.1, ...), custom_call_target="tpu_custom_call", output_to_operand_aliasing={{0}: (9, {}), {1}: (10, {}), {2}: (11, {})} | custom-call | tf_op jit(solution)/shard_map/pallas_call | solution.py:316
  38.9 0.2 collective-permute-start.8
  39.0 1.1 %collective-permute-done.8 = f32[8,128]{1,0:T(8,128)S(1)} collective-permute-done((f32[8,128]{1,0:T(8,128)S(1)}, f32[8,128]{1,0:T(8,128)S(1)}, u32[]{:S(2)}, u32[]{:S(2)}) %collective-permute-start.8) | collective-permute-done | bytes 4128 | tf_op jit(solution)/shard_map/ppermute | solution.py:295
  40.1 1.4 %collective-permute-start.9 = (f32[8,128]{1,0:T(8,128)S(1)}, f32[8,128]{1,0:T(8,128)S(1)}, u32[]{:S(2)}, u32[]{:S(2)}) collective-permute-start(f32[8,128]{1,0:T(8,128)S(1)} %add.6), channel_id=1, source_target_pairs={{0,2},{1,3},{2,0},{3,1},{4,6},{5,7},{6,4},{7,5},{8,10},{9,11},{10,... | collective-permute-start | bytes 12296 | tf_op jit(solution)/shard_map/ppermute | solution.py:295
  41.5 2.2 %collective-permute-done.9 = f32[8,128]{1,0:T(8,128)S(1)} collective-permute-done((f32[8,128]{1,0:T(8,128)S(1)}, f32[8,128]{1,0:T(8,128)S(1)}, u32[]{:S(2)}, u32[]{:S(2)}) %collective-permute-start.9) | collective-permute-done | bytes 4128 | tf_op jit(solution)/shard_map/ppermute | solution.py:295
  43.7 1.5 %collective-permute-start.10 = (f32[8,128]{1,0:T(8,128)S(1)}, f32[8,128]{1,0:T(8,128)S(1)}, u32[]{:S(2)}, u32[]{:S(2)}) collective-permute-start(f32[8,128]{1,0:T(8,128)S(1)} %add.7.mine), channel_id=1, source_target_pairs={{0,4},{1,5},{2,6},{3,7},{4,0},{5,1},{6,2},{7,3},{8,12},{9,13},{10,... | collective-permute-start | bytes 12296 | tf_op jit(solution)/shard_map/ppermute | solution.py:295
  45.9 1.4 %collective-permute-done.10.theirs = f32[8,128]{1,0:T(8,128)S(1)} collective-permute-done((f32[8,128]{1,0:T(8,128)S(1)}, f32[8,128]{1,0:T(8,128)S(1)}, u32[]{:S(2)}, u32[]{:S(2)}) %collective-permute-start.10) | collective-permute-done | bytes 4128 | tf_op jit(solution)/shard_map/ppermute | solution.py:295
  47.3 0.0 copy-done.3
  47.3 8.4 %shard_map.114 = (f32[32,16,128]{2,1,0:T(8,128)}, f32[32,64,128]{2,1,0:T(8,128)}, f32[32,64,128]{2,1,0:T(8,128)}) custom-call(f32[1]{0:T(128)S(6)} %copy.29.diffuse_t, f32[8,128]{1,0:T(8,128)S(1)} %add.7.mine, f32[8,128]{1,0:T(8,128)S(1)} %collective-permute-done.10.theirs, f32[38,64,128]{2,1,0:T(8,128)S(1)} %get-tuple-element.25.p0, ...), custom_call_target="tpu_custom_call" | custom-call | tf_op jit(solution)/shard_map/pallas_call | solution.py:316
  (19 shorter events, 0.1 us)
Async XLA Ops:
  1.5 19.1 %copy-start.1 = (f32[32,16,128]{2,1,0:T(8,128)S(1)}, f32[32,16,128]{2,1,0:T(8,128)}, u32[]{:S(2)}) copy-start(f32[32,16,128]{2,1,0:T(8,128)} %vp.3) | copy-start | bytes 786436
  1.5 23.6 %copy-start = (s32[32,64,128]{2,1,0:T(8,128)S(1)}, s32[32,64,128]{2,1,0:T(8,128)}, u32[]{:S(2)}) copy-start(s32[32,64,128]{2,1,0:T(8,128)} %refs_3_.1) | copy-start | bytes 3145732
  1.6 23.6 %copy-start.2 = (f32[1,32,64,128]{3,2,1,0:T(8,128)S(1)}, f32[1,32,64,128]{3,2,1,0:T(8,128)}, u32[]{:S(2)}) copy-start(f32[1,32,64,128]{3,2,1,0:T(8,128)} %param.16) | copy-start | bytes 3145732
  1.6 23.5 %copy-start.4 = (f32[3]{0:T(128)S(1)}, f32[3]{0:T(128)}, u32[]{:S(2)}) copy-start(f32[3]{0:T(128)} %cond_t.3) | copy-start | bytes 40
  1.6 23.5 %copy-start.5 = (f32[3]{0:T(128)S(1)}, f32[3]{0:T(128)}, u32[]{:S(2)}) copy-start(f32[3]{0:T(128)} %leak_t.3) | copy-start | bytes 40
  1.6 23.5 %copy-start.6 = (f32[1,3]{1,0:T(1,128)S(1)}, f32[1,3]{1,0:T(1,128)}, u32[]{:S(2)}) copy-start(f32[1,3]{1,0:T(1,128)} %bind_t.1) | copy-start | bytes 40
  1.6 11.1 %collective-permute-start.3 = (f32[16,16,128]{2,1,0:T(8,128)S(1)}, f32[16,16,128]{2,1,0:T(8,128)S(1)}, u32[]{:S(2)}, u32[]{:S(2)}) collective-permute-start(f32[16,16,128]{2,1,0:T(8,128)S(1)} %pad_maximum_fusion), channel_id=1, source_target_pairs={{0,8},{8,16},{16,24},{24,0},{1,9},{9,17},{17,25},{25,1},{2,10},{10... | collective-permute-start | bytes 393224 | tf_op jit(solution)/shard_map/ppermute | solution.py:280
  3.2 11.2 %collective-permute-start.4 = (f32[16,16,128]{2,1,0:T(8,128)S(1)}, f32[16,16,128]{2,1,0:T(8,128)S(1)}, u32[]{:S(2)}, u32[]{:S(2)}) collective-permute-start(f32[16,16,128]{2,1,0:T(8,128)S(1)} %pad_maximum_fusion), channel_id=1, source_target_pairs={{0,16},{8,24},{16,0},{24,8},{1,17},{9,25},{17,1},{25,9},{2,18},{10... | collective-permute-start | bytes 393224 | tf_op jit(solution)/shard_map/ppermute | solution.py:280
  4.3 11.8 %collective-permute-start.5 = (f32[16,16,128]{2,1,0:T(8,128)S(1)}, f32[16,16,128]{2,1,0:T(8,128)S(1)}, u32[]{:S(2)}, u32[]{:S(2)}) collective-permute-start(f32[16,16,128]{2,1,0:T(8,128)S(1)} %pad_maximum_fusion), channel_id=1, source_target_pairs={{0,24},{8,0},{16,8},{24,16},{1,25},{9,1},{17,9},{25,17},{2,26},{10... | collective-permute-start | bytes 393224 | tf_op jit(solution)/shard_map/ppermute | solution.py:280
  16.2 8.9 %collective-permute-start.7 = (f32[512,128]{1,0:T(8,128)S(1)}, f32[512,128]{1,0:T(8,128)S(1)}, u32[]{:S(2)}, u32[]{:S(2)}) collective-permute-start(f32[512,128]{1,0:T(8,128)S(1)} %constant_dynamic-update-slice_fusion.6), channel_id=1, source_target_pairs={{1,0},{2,1},{3,2},{4,3},{5,4},{6,5},{7,6},{9,8},{10,9},{11,10},{12... | collective-permute-start | bytes 786440 | tf_op jit(solution)/shard_map/ppermute | solution.py:287
  17.6 7.5 %collective-permute-start.6 = (f32[512,128]{1,0:T(8,128)S(1)}, f32[512,128]{1,0:T(8,128)S(1)}, u32[]{:S(2)}, u32[]{:S(2)}) collective-permute-start(f32[512,128]{1,0:T(8,128)S(1)} %constant_dynamic-update-slice_fusion), channel_id=1, source_target_pairs={{0,1},{1,2},{2,3},{3,4},{4,5},{5,6},{6,7},{8,9},{9,10},{10,11},{11... | collective-permute-start | bytes 786440 | tf_op jit(solution)/shard_map/ppermute | solution.py:286
  20.7 10.4 %collective-permute-start = (f32[16,16,128]{2,1,0:T(8,128)S(1)}, f32[16,16,128]{2,1,0:T(8,128)S(1)}, u32[]{:S(2)}, u32[]{:S(2)}) collective-permute-start(f32[16,16,128]{2,1,0:T(8,128)S(1)} %slice.49), channel_id=1, source_target_pairs={{0,8},{8,16},{16,24},{24,0},{1,9},{9,17},{17,25},{25,1},{2,10},{10... | collective-permute-start | bytes 393224 | tf_op jit(solution)/shard_map/ppermute | solution.py:280
  20.7 11.6 %collective-permute-start.1 = (f32[16,16,128]{2,1,0:T(8,128)S(1)}, f32[16,16,128]{2,1,0:T(8,128)S(1)}, u32[]{:S(2)}, u32[]{:S(2)}) collective-permute-start(f32[16,16,128]{2,1,0:T(8,128)S(1)} %slice.49), channel_id=1, source_target_pairs={{0,16},{8,24},{16,0},{24,8},{1,17},{9,25},{17,1},{25,9},{2,18},{10... | collective-permute-start | bytes 393224 | tf_op jit(solution)/shard_map/ppermute | solution.py:280
  22.5 12.7 %collective-permute-start.2 = (f32[16,16,128]{2,1,0:T(8,128)S(1)}, f32[16,16,128]{2,1,0:T(8,128)S(1)}, u32[]{:S(2)}, u32[]{:S(2)}) collective-permute-start(f32[16,16,128]{2,1,0:T(8,128)S(1)} %slice.49), channel_id=1, source_target_pairs={{0,24},{8,0},{16,8},{24,16},{1,25},{9,1},{17,9},{25,17},{2,26},{10... | collective-permute-start | bytes 393224 | tf_op jit(solution)/shard_map/ppermute | solution.py:280
  35.2 12.1 %copy-start.3 = (f32[1,32,64,128]{3,2,1,0:T(8,128)S(1)}, f32[1,32,64,128]{3,2,1,0:T(8,128)}, u32[]{:S(2)}) copy-start(f32[1,32,64,128]{3,2,1,0:T(8,128)} %param.17) | copy-start | bytes 3145732
  38.9 1.2 %collective-permute-start.8 = (f32[8,128]{1,0:T(8,128)S(1)}, f32[8,128]{1,0:T(8,128)S(1)}, u32[]{:S(2)}, u32[]{:S(2)}) collective-permute-start(f32[8,128]{1,0:T(8,128)S(1)} %get-tuple-element.24), channel_id=1, source_target_pairs={{0,1},{1,0},{2,3},{3,2},{4,5},{5,4},{6,7},{7,6},{8,9},{9,8},{10,11... | collective-permute-start | bytes 12296 | tf_op jit(solution)/shard_map/ppermute | solution.py:295
  40.1 3.6 %collective-permute-start.9 = (f32[8,128]{1,0:T(8,128)S(1)}, f32[8,128]{1,0:T(8,128)S(1)}, u32[]{:S(2)}, u32[]{:S(2)}) collective-permute-start(f32[8,128]{1,0:T(8,128)S(1)} %add.6), channel_id=1, source_target_pairs={{0,2},{1,3},{2,0},{3,1},{4,6},{5,7},{6,4},{7,5},{8,10},{9,11},{10,... | collective-permute-start | bytes 12296 | tf_op jit(solution)/shard_map/ppermute | solution.py:295
  43.7 3.6 %collective-permute-start.10 = (f32[8,128]{1,0:T(8,128)S(1)}, f32[8,128]{1,0:T(8,128)S(1)}, u32[]{:S(2)}, u32[]{:S(2)}) collective-permute-start(f32[8,128]{1,0:T(8,128)S(1)} %add.7.mine), channel_id=1, source_target_pairs={{0,4},{1,5},{2,6},{3,7},{4,0},{5,1},{6,2},{7,3},{8,12},{9,13},{10,... | collective-permute-start | bytes 12296 | tf_op jit(solution)/shard_map/ppermute | solution.py:295
where the time goes:
time: 56.1 us; the launch traced here: 55.7 us
  Pallas kernels  17.9 us (32%)
  waiting for transfers between devices  16.1 us (29%)
  starting transfers between devices  15.8 us (28%)
  local copies, waits for them, and re-layouts  2.66 us (5%)
  between operations  2.2 us (4%)
  other arithmetic  0.97 us (2%)
    pallas_call x3, Pallas kernels, call(): pl.pallas_call(kernel, out_shape=tuple(outs), in_specs=[smem()] * len(sca...  17.9 us
    ppermute x6, waiting for transfers between devices, shifts(): lax.ppermute(array, axis, [(i, (i + k) % count) for i in range(count)])  11.4 us
    ppermute x6, starting transfers between devices, shifts(): lax.ppermute(array, axis, [(i, (i + k) % count) for i in range(count)])  8.41 us
    ppermute x3, waiting for transfers between devices, total_over(): other = lax.ppermute(array, axis, [(i, i ^ step) for i in range(count)])  4.7 us
    ppermute x3, starting transfers between devices, total_over(): other = lax.ppermute(array, axis, [(i, i ^ step) for i in range(count)])  3.09 us
    ppermute x1, starting transfers between devices, across(): from_low = lax.ppermute(high, 'gz', [(i, i + 1) for i in range(count - 1)])  3.05 us
    slice x5, local copies, waits for them, and re-layouts, program(): low = payload([b[:HALO] for b in blocks], tissue[:HALO], conc[:TSTEPS])  1.66 us
    ppermute x1, starting transfers between devices, across(): from_high = lax.ppermute(low, 'gz', [(i + 1, i) for i in range(count - 1)])  1.29 us
  transfers between devices with their start and end apart: 11, of which 8 were waited for; matrix products, arithmetic and copies ran while one was open for 5% of the time, Pallas kernels for 11%

commit v1 on v0

v1 whole, which is shorter than its diff:
```python
import functools
import math
import jax
import jax.numpy as jnp
from jax import lax
from jax.experimental import pallas as pl
from jax.experimental.pallas import tpu as pltpu
from jax.sharding import PartitionSpec as P

TSTEPS = 2
HALO = TSTEPS + 1
DT = 0.1


def select(labels, values):
    return jnp.where(labels == 0, values[0], jnp.where(labels == 1, values[1], values[2]))


def following(cells, axis):
    return pltpu.roll(cells, cells.shape[axis] - 1, axis)


def preceding(cells, axis):
    return pltpu.roll(cells, 1, axis)


def edges(shape):
    row = lax.broadcasted_iota(jnp.int32, shape, 0)
    lane = lax.broadcasted_iota(jnp.int32, shape, 1)
    return (row == 0, row == shape[0] - 1), (lane == 0, lane == shape[1] - 1)


def inside():
    slab = lax.axis_index("gz")
    has_low = (slab > 0).astype(jnp.float32)
    has_high = (slab < lax.axis_size("gz") - 1).astype(jnp.float32)
    return has_low, has_high


def image(e, faces, inverse, p0, u0):
    kx, ky, kz = faces
    p = p0[e]
    pull = kz[e] * p0[e + 1] + kz[e - 1] * p0[e - 1]
    for axis, face in ((0, kx[e]), (1, ky[e])):
        pull = pull + (face * following(p, axis) + preceding(face * p, axis))
    u = p - inverse[e] * pull
    u0[e] = u
    return u


def products(e, u, u_next, totals, faces, diag, p0):
    kx, ky, kz = faces
    p = p0[e]
    d = diag[e - HALO]
    dp, du = d * p, d * u
    pull = kz[e] * u_next + kx[e] * following(u, 0) + ky[e] * following(u, 1)
    terms = (dp * p, dp * u, du * u, pull * u)
    return tuple(a + t.reshape(-1, 8, t.shape[-1]).sum(0) for a, t in zip(totals, terms))


def split_kernel(rim, vp, rims, inner):
    layers = vp.shape[0]
    rims[:rim] = vp[:rim]
    rims[rim:] = vp[layers - rim :]
    inner[...] = vp[rim : layers - rim]


def border_kernel(tissue, conc, low, high):
    layers, rows, _ = tissue.shape
    for j in range(HALO):
        low[j * rows : (j + 1) * rows, :] = tissue[j].astype(jnp.float32)
        high[j * rows : (j + 1) * rows, :] = tissue[layers - HALO + j].astype(jnp.float32)
    for j in range(TSTEPS):
        at = (HALO + j) * rows
        low[at : at + rows, :] = conc[j]
        high[at : at + rows, :] = conc[layers - TSTEPS + j]


def constants(cond_t, leak_t):
    cond_v = [cond_t[i] for i in range(3)]
    leak_v = [leak_t[i] for i in range(3)]
    diag_v = [6.0 * c * c + k for c, k in zip(cond_v, leak_v)]
    inverse_v = [1.0 / d for d in diag_v]
    ratio_v = [k / d for k, d in zip(leak_v, diag_v)]
    return cond_v, diag_v, inverse_v, ratio_v


def level(e, c, ends, kx, ky):
    kx[e] = jnp.where(ends[0][1], 0.0, c * following(c, 0))
    ky[e] = jnp.where(ends[1][1], 0.0, c * following(c, 1))


def prepare_kernel(cond_t, leak_t, bind_t, tissue, conc, kx, ky, kz, diag, inverse, ratio, rate, wide):
    layers, _, _ = tissue.shape
    cond_v, diag_v, inverse_v, ratio_v = constants(cond_t, leak_t)
    rate_v = [bind_t[0, i] * DT for i in range(3)]
    ends = edges(tissue.shape[1:])

    def own(i, before):
        e = i + HALO
        labels = tissue[i]
        c = select(labels, cond_v)
        diag[i] = select(labels, diag_v)
        inverse[e] = select(labels, inverse_v)
        ratio[i] = select(labels, ratio_v)
        rate[e] = select(labels, rate_v)
        wide[i + TSTEPS] = conc[i]
        level(e, c, ends, kx, ky)
        kz[e - 1] = before * c
        return c

    lax.fori_loop(0, layers, own, jnp.zeros(tissue.shape[1:], jnp.float32), unroll=2)


def rim_kernel(parts, rim, width, cond_t, leak_t, bind_t, *refs):
    blocks, refs = refs[0], refs[1:]
    from_low, from_high, tissue, diag, ratio = refs[:5]
    kx, ky, kz, inverse, rate, p0, u0, sums = refs[10:]
    layers, rows, _ = tissue.shape
    me = lax.axis_index("size")
    has_low, has_high = inside()
    cond_v, _, inverse_v, ratio_v = constants(cond_t, leak_t)
    rate_v = [bind_t[0, i] * DT for i in range(3)]
    tis_at = parts * HALO * width
    ends = edges(tissue.shape[1:])

    def halo(side, j, e, valid):
        at = tis_at + j * rows
        labels = side[at : at + rows, :]
        c = select(labels, cond_v) * valid
        level(e, c, ends, kx, ky)
        inverse[e] = select(labels, inverse_v)
        rate[e] = select(labels, rate_v)
        return c

    low = [halo(from_low, j, j, has_low) for j in range(HALO)] + [select(tissue[0], cond_v)]
    high = [select(tissue[layers - 1], cond_v)] + [halo(from_high, j, layers + HALO + j, has_high) for j in range(HALO)]
    for j in range(HALO):
        kz[j] = low[j] * low[j + 1]
        kz[layers + HALO - 1 + j] = high[j] * high[j + 1]

    for k in range(parts):
        column = pl.multiple_of((me ^ k) * width, width)
        spot = pl.ds(column, width)
        base = k * 2 * rim

        def fill(i, carry):
            high = i + (layers - rim)
            p0[i + HALO, spot, :] = blocks[i + base] * ratio[i, spot, :]
            p0[high + HALO, spot, :] = blocks[i + (base + rim)] * ratio[high, spot, :]
            return carry

        lax.fori_loop(0, rim, fill, 0)
        for j in range(HALO):
            at = (k * HALO + j) * width
            for side, e in ((from_low, j), (from_high, layers + HALO + j)):
                labels = side[pl.ds(pl.multiple_of(tis_at + j * rows + column, width), width), :]
                p0[e, spot, :] = side[at : at + width, :] * select(labels, ratio_v)

    faces = (kx, ky, kz)

    def both(e, carry):
        image(e, faces, inverse, p0, u0)
        image(layers + 2 * HALO - 1 - e, faces, inverse, p0, u0)
        return carry

    lax.fori_loop(1, rim + HALO - 1, both, 0)

    def sum_over(first, count, totals):
        def body(i, carry):
            e = i + HALO
            return products(e, u0[e], u0[e + 1], carry, faces, diag, p0)

        return lax.fori_loop(first, first + count, body, totals)

    zero = jnp.zeros((8, tissue.shape[2]), jnp.float32)
    totals = sum_over(0, rim - 2, (zero,) * 4)
    totals = sum_over(layers - rim + 1, rim - 1, totals)
    for i in range(4):
        sums[i] = totals[i]


def core_kernel(parts, rim, vp, *refs):
    inner = refs[: parts - 1]
    refs = refs[parts - 1 :]
    kx, ky, kz, diag, inverse, ratio, part, from_low, from_high = refs[:9]
    p0, u0, wide, sums = refs[12:]
    rows = wide.shape[1]
    for j in range(TSTEPS):
        at = from_low.shape[0] - (TSTEPS - j) * rows
        wide[j] = from_low[at : at + rows, :]
        wide[wide.shape[0] - TSTEPS + j] = from_high[at : at + rows, :]
    layers, width, _ = vp.shape
    me = lax.axis_index("size")
    for k in range(parts):
        spot = pl.ds(pl.multiple_of((me ^ k) * width, width), width)
        source = vp if k == 0 else inner[k - 1]
        start = rim if k == 0 else 0

        def fill(i, carry):
            p0[i + (rim + HALO), spot, :] = source[i + start] * ratio[i + rim, spot, :]
            return carry

        lax.fori_loop(0, layers - 2 * rim, fill, 0, unroll=2)
    faces = (kx, ky, kz)
    first = rim + HALO - 1
    last = layers - rim + HALO

    def body(e, carry):
        before, totals = carry
        here = image(e, faces, inverse, p0, u0)
        return here, products(e - 1, before, here, totals, faces, diag, p0)

    totals = tuple(part[i] for i in range(4))
    before, totals = lax.fori_loop(first, last + 1, body, (u0[first - 1], totals))
    totals = products(last, before, u0[last + 1], totals, faces, diag, p0)
    sums[...] = jnp.concatenate([t.sum(0, keepdims=True) for t in totals] * 2, 0)


def transport_kernel(width, hinder_t, diffuse_t, mine, theirs, p0, u0, kx, ky, kz, rate, wide, bound, pressure, free_out, bound_out, first, *coef):
    layers, rows, lanes = bound.shape
    me = lax.axis_index("size")
    has_low, has_high = inside()
    sums = mine[...] + theirs[...]
    rho, drop, second, shared = [jnp.sum(sums[i : i + 1, :], axis=1, keepdims=True) for i in range(4)]
    third = second - 2.0 * shared
    alpha = rho / drop
    rho_next = alpha * alpha * second - rho
    beta = rho_next / rho
    curve = drop - 2.0 * alpha * second + alpha * alpha * third - beta * rho_next / alpha
    alpha_next = rho_next / curve
    on_p = jnp.broadcast_to(alpha + alpha_next * (1.0 + beta), (8, lanes))[None]
    on_u = jnp.broadcast_to(-alpha_next * alpha, (8, lanes))[None]
    diffuse = diffuse_t[0] * DT
    hinder = hinder_t[0] * DT

    def combine(p, u, by_p, by_u):
        return (by_p * p.reshape(-1, 8, lanes) + by_u * u.reshape(-1, 8, lanes)).reshape(p.shape)

    spot = pl.ds(pl.multiple_of(me * width, width), width)

    def own(i, carry):
        pressure[i] = combine(p0[i + HALO, spot, :], u0[i + HALO, spot, :], on_p, on_u)
        return carry

    lax.fori_loop(0, layers, own, 0, unroll=4)
    drive_p, drive_u = hinder * on_p, hinder * on_u
    ends = edges((rows, lanes))

    def drive(e):
        return combine(p0[e], u0[e], drive_p, drive_u)

    def halves(flow):
        out = jnp.maximum(flow, 0.0) + diffuse
        return out, out - flow

    def advance(i, carry):
        here, low_flow = carry
        e = i + TSTEPS
        above = drive(e + 1)
        conc = wide[i + 1]
        high_flow = kz[e] * (here - above)
        p_low, n_low = halves(low_flow)
        p_high, n_high = halves(high_flow)
        leave = p_high + n_low + rate[e]
        weights = [p_low, n_high]
        moved = p_low * wide[i] + n_high * wide[i + 2]
        for axis, face in ((0, kx), (1, ky)):
            at_low, at_high = ends[axis]
            flow = face[e] * (here - following(here, axis))
            p_high, n_high = halves(flow)
            p_low, n_low = halves(preceding(flow, axis))
            leave = leave + (p_high + n_low)
            n_high = jnp.where(at_high, 0.0, n_high)
            p_low = jnp.where(at_low, 0.0, p_low)
            weights += [p_low, n_high]
            moved = moved + p_low * preceding(conc, axis) + n_high * following(conc, axis)
        stay = 1.0 - leave
        valid = jnp.where(i == 0, has_low, jnp.where(i == layers + 1, has_high, 1.0))
        first[i] = (stay * conc + moved) * valid
        slot = lax.rem(i, 2)
        for ref, weight in zip(coef, [stay] + weights):
            ref[slot] = weight
        return above, high_flow

    start = drive(TSTEPS)
    carry = (start, kz[TSTEPS - 1] * (drive(TSTEPS - 1) - start))
    carry = lax.fori_loop(0, 2, advance, carry)

    def body(i, carry):
        here = first[i - 1]
        slot = lax.rem(i - 1, 2)
        old = [ref[slot] for ref in coef]
        carry = advance(i, carry)
        stay, z_low, z_high, x_low, x_high, y_low, y_high = old
        result = stay * here + z_low * first[i - 2] + z_high * first[i]
        result = result + x_low * preceding(here, 0) + x_high * following(here, 0)
        free_out[i - 2] = result + y_low * preceding(here, 1) + y_high * following(here, 1)
        bound_out[i - 2] = bound[i - 2] + rate[i + 1] * (wide[i] + here)
        return carry

    lax.fori_loop(2, layers + 2, body, carry)


def swapped(array, axis, bit):
    count = lax.axis_size(axis)
    return lax.ppermute(array, axis, [(i, i ^ bit) for i in range(count)])


def butterfly(array, axis):
    bit = 1
    while bit < lax.axis_size(axis):
        array = jnp.concatenate([array, swapped(array, axis, bit)], 0)
        bit *= 2
    return array


def across(low, high):
    count = lax.axis_size("gz")
    from_low = lax.ppermute(high, "gz", [(i, i + 1) for i in range(count - 1)])
    from_high = lax.ppermute(low, "gz", [(i + 1, i) for i in range(count - 1)])
    return from_low, from_high


def total_over(array, axis):
    count = lax.axis_size(axis)
    step = 1
    while True:
        other = lax.ppermute(array, axis, [(i, i ^ step) for i in range(count)])
        step *= 2
        if step == count:
            return array, other
        array = array + other


def smem():
    return pl.BlockSpec(memory_space=pltpu.SMEM)


def vmem():
    return pl.BlockSpec(memory_space=pltpu.VMEM)


def f32(*shape):
    return jax.ShapeDtypeStruct(shape, jnp.float32)


def call(kernel, outs, scalars, arrays, scratch=(), aliases={}):
    size = sum(4 * math.prod(a.shape) for a in list(outs) + list(arrays) + list(scratch))
    return pl.pallas_call(
        kernel,
        out_shape=tuple(outs),
        in_specs=[smem()] * len(scalars) + [vmem()] * len(arrays),
        out_specs=(vmem(),) * len(outs),
        scratch_shapes=[pltpu.VMEM(s.shape, s.dtype) for s in scratch],
        input_output_aliases=aliases,
        compiler_params=pltpu.CompilerParams(vmem_limit_bytes=size + (4 << 20)),
    )(*scalars, *arrays)


def program(tissue, vessel_pressure, cond_table, leak_table, bind_table, hindrance, diffusivity, free_conc, bound_conc):
    layers, width, lanes = vessel_pressure.shape
    rows = tissue.shape[1]
    parts = rows // width
    rim = HALO
    conc, bound = free_conc[0], bound_conc[0]
    slab = f32(layers, rows, lanes)
    extended = f32(layers + 2 * HALO, rows, lanes)
    wider = f32(layers + 2 * TSTEPS, rows, lanes)
    rims, middle = call(
        functools.partial(split_kernel, rim),
        [f32(2 * rim, width, lanes), f32(layers - 2 * rim, width, lanes)],
        [],
        [vessel_pressure],
    )
    blocks = butterfly(rims, "size")
    inner = [swapped(middle, "size", k) for k in range(1, parts)]
    border = f32((HALO + TSTEPS) * rows, lanes)
    border_low, border_high = call(border_kernel, [border] * 2, [], [tissue, conc])

    def payload(first, border):
        pieces = [blocks[k * 2 * rim + first : k * 2 * rim + first + HALO] for k in range(parts)] + [border]
        return jnp.concatenate([a.reshape(-1, lanes) for a in pieces], 0)

    from_low, from_high = across(payload(0, border_low), payload(2 * rim - HALO, border_high))
    kx, ky, kz, diag, inverse, ratio, rate, wide = call(
        prepare_kernel,
        [extended] * 3 + [slab, extended, slab, extended, wider],
        [cond_table, leak_table, bind_table],
        [tissue, conc],
    )
    kx, ky, kz, inverse, rate, p0, u0, part = call(
        functools.partial(rim_kernel, parts, rim, width),
        [extended] * 7 + [f32(4, 8, lanes)],
        [cond_table, leak_table, bind_table],
        [blocks, from_low, from_high, tissue, diag, ratio, kx, ky, kz, inverse, rate],
        aliases={9 + i: i for i in range(5)},
    )
    p0, u0, wide, sums = call(
        functools.partial(core_kernel, parts, rim),
        [extended] * 2 + [wider, f32(8, lanes)],
        [],
        [vessel_pressure, *inner, kx, ky, kz, diag, inverse, ratio, part, from_low, from_high, p0, u0, wide],
        aliases={parts + 9 + i: i for i in range(3)},
    )
    mine, theirs = total_over(sums, "gz")
    pressure, free, bound = call(
        functools.partial(transport_kernel, width),
        [f32(layers, width, lanes), slab, slab],
        [hindrance, diffusivity],
        [mine, theirs, p0, u0, kx, ky, kz, rate, wide, bound],
        scratch=[f32(layers + 2, rows, lanes)] + [f32(2, rows, lanes)] * 7,
    )
    return pressure, free[None], bound[None]


def solution(mesh):
    return jax.shard_map(
        program,
        mesh=mesh,
        in_specs=(
            P("gz", None, None),
            P("gz", "size", None),
            P(),
            P(),
            P("size", None),
            P("size"),
            P("size"),
            P("size", "gz", None, None),
            P("size", "gz", None, None),
        ),
        out_specs=(P("gz", "size", None), P("size", "gz", None, None), P("size", "gz", None, None)),
        check_vma=False,
    )
```

time: 56.1 us -> 60 us (1.070)
  waiting for transfers between devices: 16.1 us -> 24.8 us
  Pallas kernels: 17.9 us -> 15.4 us
  starting transfers between devices: 15.8 us -> 13.8 us
  other arithmetic: 0.97 us -> 0.03 us
  local copies, waits for them, and re-layouts: 2.66 us -> 3.51 us
    ppermute x6 -> x5, waiting for transfers between devices: 11.4 us -> 20.4 us  [swapped(): return lax.ppermute(array, axis, [(i, i ^ bit) for i in range(count)])]
    unnamed x24 -> x28, local copies, waits for them, and re-layouts: 0.09 us -> 3.47 us
    slice x7 -> x3, local copies, waits for them, and re-layouts: 2.55 us -> 0.02 us  [payload(): blocks[k * 2 * rim + first:k * 2 * rim + first + HALO]]
    pallas_call x3 -> x6, Pallas kernels: 17.9 us -> 15.4 us  [call(): pl.pallas_call(kernel, out_shape=tuple(outs), in_specs=[smem()] * len(sca...]
    ppermute x6 -> x5, starting transfers between devices: 8.41 us -> 6.75 us  [swapped(): return lax.ppermute(array, axis, [(i, i ^ bit) for i in range(count)])]
    convert_element_type x1 -> x0, other arithmetic: 0.95 us -> none  [payload(): arrays = pieces + [labels.astype(jnp.float32), cells]]
  transfers between devices with their start and end apart: 11 -> 10, of which waited for: 8 -> 8; matrix products, arithmetic and copies ran while one was open for 5% -> 0% of each run, Pallas kernels for 11% -> 6%
where the time goes in v1:
time: 60 us; the launch traced here: 59.7 us
  waiting for transfers between devices  24.8 us (41%)
  Pallas kernels  15.4 us (26%)
  starting transfers between devices  13.8 us (23%)
  local copies, waits for them, and re-layouts  3.51 us (6%)
  between operations  2.15 us (4%)
    ppermute x5, waiting for transfers between devices, swapped(): return lax.ppermute(array, axis, [(i, i ^ bit) for i in range(count)])  20.4 us
    pallas_call x6, Pallas kernels, call(): pl.pallas_call(kernel, out_shape=tuple(outs), in_specs=[smem()] * len(sca...  15.4 us
    ppermute x5, starting transfers between devices, swapped(): return lax.ppermute(array, axis, [(i, i ^ bit) for i in range(count)])  6.75 us
    ppermute x3, waiting for transfers between devices, total_over(): other = lax.ppermute(array, axis, [(i, i ^ step) for i in range(count)])  4.38 us
    unnamed x28, local copies, waits for them, and re-layouts  3.47 us
    ppermute x1, starting transfers between devices, across(): from_low = lax.ppermute(high, 'gz', [(i, i + 1) for i in range(count - 1)])  3.05 us
    ppermute x3, starting transfers between devices, total_over(): other = lax.ppermute(array, axis, [(i, i ^ step) for i in range(count)])  2.76 us
    ppermute x1, starting transfers between devices, across(): from_high = lax.ppermute(low, 'gz', [(i + 1, i) for i in range(count - 1)])  1.29 us
  transfers between devices with their start and end apart: 10, of which 8 were waited for; matrix products, arithmetic and copies ran while one was open for 0% of the time, Pallas kernels for 6%

profile of v1, /device:TPU:8, one launch (start us, length us, event | category | flops | bytes accessed | tf_op | source)
XLA Modules:
  0.0 59.7 jit_solution(10348400378057440041)
XLA Ops:
  0.6 0.0 copy-start.5
  0.6 0.9 %copy-done.5 = f32[32,16,128]{2,1,0:T(8,128)S(1)} copy-done((f32[32,16,128]{2,1,0:T(8,128)S(1)}, f32[32,16,128]{2,1,0:T(8,128)}, u32[]{:S(2)}) %copy-start.5) | copy-done | bytes 262168
  1.6 0.1 collective-permute-start.3
  1.7 0.0 copy-start
  1.7 1.2 %copy-done = s32[32,64,128]{2,1,0:T(8,128)S(1)} copy-done((s32[32,64,128]{2,1,0:T(8,128)S(1)}, s32[32,64,128]{2,1,0:T(8,128)}, u32[]{:S(2)}) %copy-start) | copy-done | bytes 1048600
  2.9 0.0 copy-start.2
  3.0 1.2 %copy-done.2 = f32[1,32,64,128]{3,2,1,0:T(8,128)S(1)} copy-done((f32[1,32,64,128]{3,2,1,0:T(8,128)S(1)}, f32[1,32,64,128]{3,2,1,0:T(8,128)}, u32[]{:S(2)}) %copy-start.2) | copy-done | bytes 1048600
  4.2 0.0 copy-start.3
  4.2 0.0 copy-start.1
  4.2 0.0 copy-start.7
  4.2 0.0 copy-start.8
  4.2 0.0 copy-start.9
  4.2 1.5 %collective-permute-done.3 = f32[6,16,128]{2,1,0:T(8,128)S(1)} collective-permute-done((f32[6,16,128]{2,1,0:T(8,128)S(1)}, f32[6,16,128]{2,1,0:T(8,128)S(1)}, u32[]{:S(2)}, u32[]{:S(2)}) %collective-permute-start.3) | collective-permute-done | bytes 49184 | tf_op jit(solution)/shard_map/ppermute | solution.py:307
  5.8 2.7 %collective-permute-start.4 = (f32[12,16,128]{2,1,0:T(8,128)S(1)}, f32[12,16,128]{2,1,0:T(8,128)S(1)}, u32[]{:S(2)}, u32[]{:S(2)}) collective-permute-start(f32[12,16,128]{2,1,0:T(8,128)S(1)} %pad_maximum_fusion.1), channel_id=1, source_target_pairs={{0,16},{8,24},{16,0},{24,8},{1,17},{9,25},{17,1},{25,9},{2,18},{10... | collective-permute-start | bytes 294920 | tf_op jit(solution)/shard_map/ppermute | solution.py:307
  8.4 3.1 %collective-permute-done.4 = f32[12,16,128]{2,1,0:T(8,128)S(1)} collective-permute-done((f32[12,16,128]{2,1,0:T(8,128)S(1)}, f32[12,16,128]{2,1,0:T(8,128)S(1)}, u32[]{:S(2)}, u32[]{:S(2)}) %collective-permute-start.4) | collective-permute-done | bytes 98336 | tf_op jit(solution)/shard_map/ppermute | solution.py:307
  11.6 1.3 %collective-permute-start.6 = (f32[512,128]{1,0:T(8,128)S(1)}, f32[512,128]{1,0:T(8,128)S(1)}, u32[]{:S(2)}, u32[]{:S(2)}) collective-permute-start(f32[512,128]{1,0:T(8,128)S(1)} %constant_dynamic-update-slice_fusion.5), channel_id=1, source_target_pairs={{1,0},{2,1},{3,2},{4,3},{5,4},{6,5},{7,6},{9,8},{10,9},{11,10},{12... | collective-permute-start | bytes 786440 | tf_op jit(solution)/shard_map/ppermute | solution.py:321
  12.9 3.0 %collective-permute-start.5 = (f32[512,128]{1,0:T(8,128)S(1)}, f32[512,128]{1,0:T(8,128)S(1)}, u32[]{:S(2)}, u32[]{:S(2)}) collective-permute-start(f32[512,128]{1,0:T(8,128)S(1)} %constant_dynamic-update-slice_fusion), channel_id=1, source_target_pairs={{0,1},{1,2},{2,3},{3,4},{4,5},{5,6},{6,7},{8,9},{9,10},{10,11},{11... | collective-permute-start | bytes 786440 | tf_op jit(solution)/shard_map/ppermute | solution.py:320
  16.0 2.1 %collective-permute-start = (f32[26,16,128]{2,1,0:T(8,128)S(1)}, f32[26,16,128]{2,1,0:T(8,128)S(1)}, u32[]{:S(2)}, u32[]{:S(2)}) collective-permute-start(f32[26,16,128]{2,1,0:T(8,128)S(1)} %get-tuple-element.30), channel_id=1, source_target_pairs={{0,8},{8,0},{16,24},{24,16},{1,9},{9,1},{17,25},{25,17},{2,10},{10... | collective-permute-start | bytes 638984 | tf_op jit(solution)/shard_map/ppermute | solution.py:307
  18.1 1.4 %collective-permute-start.1 = (f32[26,16,128]{2,1,0:T(8,128)S(1)}, f32[26,16,128]{2,1,0:T(8,128)S(1)}, u32[]{:S(2)}, u32[]{:S(2)}) collective-permute-start(f32[26,16,128]{2,1,0:T(8,128)S(1)} %get-tuple-element.30), channel_id=1, source_target_pairs={{0,16},{8,24},{16,0},{24,8},{1,17},{9,25},{17,1},{25,9},{2,18},{10... | collective-permute-start | bytes 638984 | tf_op jit(solution)/shard_map/ppermute | solution.py:307
  19.5 0.5 collective-permute-start.2
  20.0 0.0 copy-done.3
  20.0 0.0 copy-done.1
  20.0 0.0 copy-done.7
  20.0 0.0 copy-done.8
  20.0 0.0 copy-done.9
  20.0 2.3 %shard_map.114 = (f32[38,64,128]{2,1,0:T(8,128)S(1)}, f32[38,64,128]{2,1,0:T(8,128)S(1)}, f32[38,64,128]{2,1,0:T(8,128)S(1)}, f32[32,64,128]{2,1,0:T(8,128)S(1)}...) custom-call(f32[3]{0:T(128)S(1)} %copy-done.7, ...), custom_call_target="tpu_custom_call" | custom-call | tf_op jit(solution)/shard_map/pallas_call | solution.py:350
  22.4 0.0 collective-permute-done.6.refs_2_.refs_11_
  22.4 0.0 collective-permute-done.5.refs_1_.refs_10_
  22.4 0.0 copy-start.6
  22.4 1.5 %shard_map.115 = (f32[38,64,128]{2,1,0:T(8,128)S(1)}, f32[38,64,128]{2,1,0:T(8,128)S(1)}, f32[38,64,128]{2,1,0:T(8,128)S(1)}, f32[38,64,128]{2,1,0:T(8,128)S(1)}...) custom-call(f32[3]{0:T(128)S(1)} %copy-done.7, ...), custom_call_target="tpu_custom_call", output_to_operand_aliasing={{0}: (9, {}), {1}: (10, {}), {2}: (11, {}), {3}: (12, {}), ... | custom-call | tf_op jit(solution)/shard_map/pallas_call | solution.py:350
  24.0 3.7 %collective-permute-done.refs_0_ = f32[26,16,128]{2,1,0:T(8,128)S(1)} collective-permute-done((f32[26,16,128]{2,1,0:T(8,128)S(1)}, f32[26,16,128]{2,1,0:T(8,128)S(1)}, u32[]{:S(2)}, u32[]{:S(2)}) %collective-permute-start) | collective-permute-done | bytes 213024 | tf_op jit(solution)/shard_map/ppermute | solution.py:307
  27.7 6.5 %collective-permute-done.1.refs_1_ = f32[26,16,128]{2,1,0:T(8,128)S(1)} collective-permute-done((f32[26,16,128]{2,1,0:T(8,128)S(1)}, f32[26,16,128]{2,1,0:T(8,128)S(1)}, u32[]{:S(2)}, u32[]{:S(2)}) %collective-permute-start.1) | collective-permute-done | bytes 213024 | tf_op jit(solution)/shard_map/ppermute | solution.py:307
  34.2 5.5 %collective-permute-done.2.refs_2_ = f32[26,16,128]{2,1,0:T(8,128)S(1)} collective-permute-done((f32[26,16,128]{2,1,0:T(8,128)S(1)}, f32[26,16,128]{2,1,0:T(8,128)S(1)}, u32[]{:S(2)}, u32[]{:S(2)}) %collective-permute-start.2) | collective-permute-done | bytes 213024 | tf_op jit(solution)/shard_map/ppermute | solution.py:307
  39.7 0.0 copy-done.6
  39.7 0.0 copy-start.4
  39.7 3.3 %shard_map.116 = (f32[38,64,128]{2,1,0:T(8,128)S(1)}, f32[38,64,128]{2,1,0:T(8,128)S(1)}, f32[36,64,128]{2,1,0:T(8,128)S(1)}, f32[8,128]{1,0:T(8,128)S(1)}) custom-call(f32[32,16,128]{2,1,0:T(8,128)S(1)} %copy-done.6, f32[26,16,128]{2,1,0:T(8,128)S(1)} %collective-permute-done.refs_0_, ...), custom_call_target="tpu_custom_call", output_to_operand_aliasing={{0}: (13, {}), {1}: (14, {}), {2}: (15, {})} | custom-call | tf_op jit(solution)/shard_map/pallas_call | solution.py:350
  43.1 0.2 collective-permute-start.7
  43.2 1.1 %collective-permute-done.7 = f32[8,128]{1,0:T(8,128)S(1)} collective-permute-done((f32[8,128]{1,0:T(8,128)S(1)}, f32[8,128]{1,0:T(8,128)S(1)}, u32[]{:S(2)}, u32[]{:S(2)}) %collective-permute-start.7) | collective-permute-done | bytes 4128 | tf_op jit(solution)/shard_map/ppermute | solution.py:329
  44.3 1.1 %collective-permute-start.8 = (f32[8,128]{1,0:T(8,128)S(1)}, f32[8,128]{1,0:T(8,128)S(1)}, u32[]{:S(2)}, u32[]{:S(2)}) collective-permute-start(f32[8,128]{1,0:T(8,128)S(1)} %add.6), channel_id=1, source_target_pairs={{0,2},{1,3},{2,0},{3,1},{4,6},{5,7},{6,4},{7,5},{8,10},{9,11},{10,... | collective-permute-start | bytes 12296 | tf_op jit(solution)/shard_map/ppermute | solution.py:329
  45.4 2.5 %collective-permute-done.8 = f32[8,128]{1,0:T(8,128)S(1)} collective-permute-done((f32[8,128]{1,0:T(8,128)S(1)}, f32[8,128]{1,0:T(8,128)S(1)}, u32[]{:S(2)}, u32[]{:S(2)}) %collective-permute-start.8) | collective-permute-done | bytes 4128 | tf_op jit(solution)/shard_map/ppermute | solution.py:329
  47.9 1.5 %collective-permute-start.9 = (f32[8,128]{1,0:T(8,128)S(1)}, f32[8,128]{1,0:T(8,128)S(1)}, u32[]{:S(2)}, u32[]{:S(2)}) collective-permute-start(f32[8,128]{1,0:T(8,128)S(1)} %add.7.mine), channel_id=1, source_target_pairs={{0,4},{1,5},{2,6},{3,7},{4,0},{5,1},{6,2},{7,3},{8,12},{9,13},{10,... | collective-permute-start | bytes 12296 | tf_op jit(solution)/shard_map/ppermute | solution.py:329
  50.7 0.8 %collective-permute-done.9.theirs = f32[8,128]{1,0:T(8,128)S(1)} collective-permute-done((f32[8,128]{1,0:T(8,128)S(1)}, f32[8,128]{1,0:T(8,128)S(1)}, u32[]{:S(2)}, u32[]{:S(2)}) %collective-permute-start.9) | collective-permute-done | bytes 4128 | tf_op jit(solution)/shard_map/ppermute | solution.py:329
  51.5 0.0 copy-done.4
  51.5 8.2 %shard_map.117 = (f32[32,16,128]{2,1,0:T(8,128)}, f32[32,64,128]{2,1,0:T(8,128)}, f32[32,64,128]{2,1,0:T(8,128)}) custom-call(f32[1]{0:T(128)S(6)} %copy.36.hinder_t, f32[1]{0:T(128)S(6)} %copy.37.diffuse_t, f32[8,128]{1,0:T(8,128)S(1)} %add.7.mine, f32[8,128]{1,0:T(8,128)S(1)} %collective-permute-done.9.theirs, f32[38,64,128]{2,1,0:T(8,128)S(1)} %get-tuple-element.50.p0, ...), custom_call_target="tpu_custom_call" | custom-call | tf_op jit(solution)/shard_map/pallas_call | solution.py:350
  (19 shorter events, 0.2 us)
Async XLA Ops:
  0.6 1.0 %copy-start.5 = (f32[32,16,128]{2,1,0:T(8,128)S(1)}, f32[32,16,128]{2,1,0:T(8,128)}, u32[]{:S(2)}) copy-start(f32[32,16,128]{2,1,0:T(8,128)} %vp.3) | copy-start | bytes 786436
  1.6 4.2 %collective-permute-start.3 = (f32[6,16,128]{2,1,0:T(8,128)S(1)}, f32[6,16,128]{2,1,0:T(8,128)S(1)}, u32[]{:S(2)}, u32[]{:S(2)}) collective-permute-start(f32[6,16,128]{2,1,0:T(8,128)S(1)} %get-tuple-element.31), channel_id=1, source_target_pairs={{0,8},{8,0},{16,24},{24,16},{1,9},{9,1},{17,25},{25,17},{2,10},{10... | collective-permute-start | bytes 147464 | tf_op jit(solution)/shard_map/ppermute | solution.py:307
  1.7 1.2 %copy-start = (s32[32,64,128]{2,1,0:T(8,128)S(1)}, s32[32,64,128]{2,1,0:T(8,128)}, u32[]{:S(2)}) copy-start(s32[32,64,128]{2,1,0:T(8,128)} %refs_3_.1) | copy-start | bytes 3145732
  2.9 1.2 %copy-start.2 = (f32[1,32,64,128]{3,2,1,0:T(8,128)S(1)}, f32[1,32,64,128]{3,2,1,0:T(8,128)}, u32[]{:S(2)}) copy-start(f32[1,32,64,128]{3,2,1,0:T(8,128)} %param.16) | copy-start | bytes 3145732
  4.2 15.8 %copy-start.3 = (f32[1,32,64,128]{3,2,1,0:T(8,128)S(1)}, f32[1,32,64,128]{3,2,1,0:T(8,128)}, u32[]{:S(2)}) copy-start(f32[1,32,64,128]{3,2,1,0:T(8,128)} %param.16) | copy-start | bytes 3145732
  4.2 15.8 %copy-start.1 = (s32[32,64,128]{2,1,0:T(8,128)S(1)}, s32[32,64,128]{2,1,0:T(8,128)}, u32[]{:S(2)}) copy-start(s32[32,64,128]{2,1,0:T(8,128)} %refs_3_.1) | copy-start | bytes 3145732
  4.2 15.8 %copy-start.7 = (f32[3]{0:T(128)S(1)}, f32[3]{0:T(128)}, u32[]{:S(2)}) copy-start(f32[3]{0:T(128)} %cond_t.3) | copy-start | bytes 40
  4.2 15.8 %copy-start.8 = (f32[3]{0:T(128)S(1)}, f32[3]{0:T(128)}, u32[]{:S(2)}) copy-start(f32[3]{0:T(128)} %leak_t.3) | copy-start | bytes 40
  4.2 15.8 %copy-start.9 = (f32[1,3]{1,0:T(1,128)S(1)}, f32[1,3]{1,0:T(1,128)}, u32[]{:S(2)}) copy-start(f32[1,3]{1,0:T(1,128)} %bind_t.3) | copy-start | bytes 40
  5.8 5.8 %collective-permute-start.4 = (f32[12,16,128]{2,1,0:T(8,128)S(1)}, f32[12,16,128]{2,1,0:T(8,128)S(1)}, u32[]{:S(2)}, u32[]{:S(2)}) collective-permute-start(f32[12,16,128]{2,1,0:T(8,128)S(1)} %pad_maximum_fusion.1), channel_id=1, source_target_pairs={{0,16},{8,24},{16,0},{24,8},{1,17},{9,25},{17,1},{25,9},{2,18},{10... | collective-permute-start | bytes 294920 | tf_op jit(solution)/shard_map/ppermute | solution.py:307
  11.6 10.8 %collective-permute-start.6 = (f32[512,128]{1,0:T(8,128)S(1)}, f32[512,128]{1,0:T(8,128)S(1)}, u32[]{:S(2)}, u32[]{:S(2)}) collective-permute-start(f32[512,128]{1,0:T(8,128)S(1)} %constant_dynamic-update-slice_fusion.5), channel_id=1, source_target_pairs={{1,0},{2,1},{3,2},{4,3},{5,4},{6,5},{7,6},{9,8},{10,9},{11,10},{12... | collective-permute-start | bytes 786440 | tf_op jit(solution)/shard_map/ppermute | solution.py:321
  12.9 9.5 %collective-permute-start.5 = (f32[512,128]{1,0:T(8,128)S(1)}, f32[512,128]{1,0:T(8,128)S(1)}, u32[]{:S(2)}, u32[]{:S(2)}) collective-permute-start(f32[512,128]{1,0:T(8,128)S(1)} %constant_dynamic-update-slice_fusion), channel_id=1, source_target_pairs={{0,1},{1,2},{2,3},{3,4},{4,5},{5,6},{6,7},{8,9},{9,10},{10,11},{11... | collective-permute-start | bytes 786440 | tf_op jit(solution)/shard_map/ppermute | solution.py:320
  16.0 11.7 %collective-permute-start = (f32[26,16,128]{2,1,0:T(8,128)S(1)}, f32[26,16,128]{2,1,0:T(8,128)S(1)}, u32[]{:S(2)}, u32[]{:S(2)}) collective-permute-start(f32[26,16,128]{2,1,0:T(8,128)S(1)} %get-tuple-element.30), channel_id=1, source_target_pairs={{0,8},{8,0},{16,24},{24,16},{1,9},{9,1},{17,25},{25,17},{2,10},{10... | collective-permute-start | bytes 638984 | tf_op jit(solution)/shard_map/ppermute | solution.py:307
  18.1 16.1 %collective-permute-start.1 = (f32[26,16,128]{2,1,0:T(8,128)S(1)}, f32[26,16,128]{2,1,0:T(8,128)S(1)}, u32[]{:S(2)}, u32[]{:S(2)}) collective-permute-start(f32[26,16,128]{2,1,0:T(8,128)S(1)} %get-tuple-element.30), channel_id=1, source_target_pairs={{0,16},{8,24},{16,0},{24,8},{1,17},{9,25},{17,1},{25,9},{2,18},{10... | collective-permute-start | bytes 638984 | tf_op jit(solution)/shard_map/ppermute | solution.py:307
  19.5 20.2 %collective-permute-start.2 = (f32[26,16,128]{2,1,0:T(8,128)S(1)}, f32[26,16,128]{2,1,0:T(8,128)S(1)}, u32[]{:S(2)}, u32[]{:S(2)}) collective-permute-start(f32[26,16,128]{2,1,0:T(8,128)S(1)} %get-tuple-element.30), channel_id=1, source_target_pairs={{0,24},{8,16},{16,8},{24,0},{1,25},{9,17},{17,9},{25,1},{2,26},{10... | collective-permute-start | bytes 638984 | tf_op jit(solution)/shard_map/ppermute | solution.py:307
  22.4 17.3 %copy-start.6 = (f32[32,16,128]{2,1,0:T(8,128)S(1)}, f32[32,16,128]{2,1,0:T(8,128)}, u32[]{:S(2)}) copy-start(f32[32,16,128]{2,1,0:T(8,128)} %vp.3) | copy-start | bytes 786436
  39.7 11.8 %copy-start.4 = (f32[1,32,64,128]{3,2,1,0:T(8,128)S(1)}, f32[1,32,64,128]{3,2,1,0:T(8,128)}, u32[]{:S(2)}) copy-start(f32[1,32,64,128]{3,2,1,0:T(8,128)} %param.17) | copy-start | bytes 3145732
  43.1 1.2 %collective-permute-start.7 = (f32[8,128]{1,0:T(8,128)S(1)}, f32[8,128]{1,0:T(8,128)S(1)}, u32[]{:S(2)}, u32[]{:S(2)}) collective-permute-start(f32[8,128]{1,0:T(8,128)S(1)} %get-tuple-element.49), channel_id=1, source_target_pairs={{0,1},{1,0},{2,3},{3,2},{4,5},{5,4},{6,7},{7,6},{8,9},{9,8},{10,11... | collective-permute-start | bytes 12296 | tf_op jit(solution)/shard_map/ppermute | solution.py:329
  44.3 3.6 %collective-permute-start.8 = (f32[8,128]{1,0:T(8,128)S(1)}, f32[8,128]{1,0:T(8,128)S(1)}, u32[]{:S(2)}, u32[]{:S(2)}) collective-permute-start(f32[8,128]{1,0:T(8,128)S(1)} %add.6), channel_id=1, source_target_pairs={{0,2},{1,3},{2,0},{3,1},{4,6},{5,7},{6,4},{7,5},{8,10},{9,11},{10,... | collective-permute-start | bytes 12296 | tf_op jit(solution)/shard_map/ppermute | solution.py:329
  47.9 3.6 %collective-permute-start.9 = (f32[8,128]{1,0:T(8,128)S(1)}, f32[8,128]{1,0:T(8,128)S(1)}, u32[]{:S(2)}, u32[]{:S(2)}) collective-permute-start(f32[8,128]{1,0:T(8,128)S(1)} %add.7.mine), channel_id=1, source_target_pairs={{0,4},{1,5},{2,6},{3,7},{4,0},{5,1},{6,2},{7,3},{8,12},{9,13},{10,... | collective-permute-start | bytes 12296 | tf_op jit(solution)/shard_map/ppermute | solution.py:329

commit v2 on v1

v2 whole, which is shorter than its diff:
```python
import functools
import math
import jax
import jax.numpy as jnp
from jax import lax
from jax.experimental import pallas as pl
from jax.experimental.pallas import tpu as pltpu
from jax.sharding import PartitionSpec as P

TSTEPS = 2
HALO = TSTEPS + 1
DT = 0.1


def select(labels, values):
    return jnp.where(labels == 0, values[0], jnp.where(labels == 1, values[1], values[2]))


def following(cells, axis):
    return pltpu.roll(cells, cells.shape[axis] - 1, axis)


def preceding(cells, axis):
    return pltpu.roll(cells, 1, axis)


def edges(shape):
    row = lax.broadcasted_iota(jnp.int32, shape, 0)
    lane = lax.broadcasted_iota(jnp.int32, shape, 1)
    return (row == 0, row == shape[0] - 1), (lane == 0, lane == shape[1] - 1)


def inside():
    slab = lax.axis_index("gz")
    has_low = (slab > 0).astype(jnp.float32)
    has_high = (slab < lax.axis_size("gz") - 1).astype(jnp.float32)
    return has_low, has_high


def at(ref, layer, rows, shift=0):
    if shift == 0:
        return ref[pl.ds(pl.multiple_of(layer * rows, 8), rows), :]
    view = ref.at[pl.ds(pl.multiple_of(layer * rows - 8, 8), rows + 16), :]
    return view[8 + shift : 8 + shift + rows, :]


def put(ref, layer, value):
    rows = value.shape[0]
    ref[pl.ds(pl.multiple_of(layer * rows, 8), rows), :] = value


def image(e, rows, faces, inverse, p0, u0, p_next):
    kx, ky, kz = faces
    p, y = at(p0, e, rows), at(ky, e, rows)
    ahead = following(p, 1)
    pull = at(kz, e, rows) * at(p0, e + 1, rows) + at(kz, e - 1, rows) * at(p0, e - 1, rows)
    pull = pull + (at(kx, e, rows) * at(p0, e, rows, 1) + at(kx, e, rows, -1) * at(p0, e, rows, -1))
    pull = pull + (y * ahead + preceding(y * p, 1))
    put(p_next, e, ahead)
    put(u0, e, p - at(inverse, e, rows) * pull)


def products(e, rows, totals, faces, diag, p0, u0, u_next):
    kx, ky, kz = faces
    p, u = at(p0, e, rows), at(u0, e, rows)
    d = at(diag, e - HALO, rows)
    dp, du = d * p, d * u
    ahead = following(u, 1)
    pull = at(kz, e, rows) * at(u0, e + 1, rows) + at(kx, e, rows) * at(u0, e, rows, 1) + at(ky, e, rows) * ahead
    put(u_next, e, ahead)
    terms = (dp * p, dp * u, du * u, pull * u)
    return tuple(a + t.reshape(-1, 8, t.shape[-1]).sum(0) for a, t in zip(totals, terms))


def split_kernel(rim, vp, rims, inner):
    layers = vp.shape[0]
    rims[:rim] = vp[:rim]
    rims[rim:] = vp[layers - rim :]
    inner[...] = vp[rim : layers - rim]


def border_kernel(tissue, conc, low, high):
    layers, rows, _ = tissue.shape
    for j in range(HALO):
        low[j * rows : (j + 1) * rows, :] = tissue[j].astype(jnp.float32)
        high[j * rows : (j + 1) * rows, :] = tissue[layers - HALO + j].astype(jnp.float32)
    for j in range(TSTEPS):
        at = (HALO + j) * rows
        low[at : at + rows, :] = conc[j]
        high[at : at + rows, :] = conc[layers - TSTEPS + j]


def constants(cond_t, leak_t):
    cond_v = [cond_t[i] for i in range(3)]
    leak_v = [leak_t[i] for i in range(3)]
    diag_v = [6.0 * c * c + k for c, k in zip(cond_v, leak_v)]
    inverse_v = [1.0 / d for d in diag_v]
    ratio_v = [k / d for k, d in zip(leak_v, diag_v)]
    return cond_v, diag_v, inverse_v, ratio_v


def level(e, c, ends, kx, ky):
    put(kx, e, jnp.where(ends[0][1], 0.0, c * following(c, 0)))
    put(ky, e, jnp.where(ends[1][1], 0.0, c * following(c, 1)))


def remaining(rate, diffuse, ends):
    stay = 1.0 - rate
    for low, high in ends:
        stay = stay - jnp.where(low, diffuse, 0.0) - jnp.where(high, diffuse, 0.0)
    return stay


def prepare_kernel(rows, cond_t, leak_t, bind_t, diffuse_t, tissue, conc, kx, ky, kz, diag, inverse, ratio, rate, keep, wide):
    shape = (rows, tissue.shape[1])
    layers = tissue.shape[0] // rows
    cond_v, diag_v, inverse_v, ratio_v = constants(cond_t, leak_t)
    rate_v = [bind_t[0, i] * DT for i in range(3)]
    ends = edges(shape)
    base = remaining(0.0, diffuse_t[0] * DT, ends)

    def own(i, before):
        e = i + HALO
        labels = at(tissue, i, rows)
        c = select(labels, cond_v)
        r = select(labels, rate_v)
        put(diag, i, select(labels, diag_v))
        put(inverse, e, select(labels, inverse_v))
        put(ratio, i, select(labels, ratio_v))
        put(rate, i, r)
        put(keep, i + 1, base - r)
        put(wide, i + TSTEPS, at(conc, i, rows))
        level(e, c, ends, kx, ky)
        put(kz, e - 1, before * c)
        return c

    lax.fori_loop(0, layers, own, jnp.zeros(shape, jnp.float32), unroll=2)


def rim_kernel(parts, rim, width, rows, cond_t, leak_t, bind_t, diffuse_t, blocks, from_low, from_high, tissue, diag, ratio, *refs):
    kx, ky, kz, inverse, keep, wide, p0, u0, p_next, u_next, sums = refs[6:]
    lanes = tissue.shape[1]
    layers = tissue.shape[0] // rows
    me = lax.axis_index("size")
    has_low, has_high = inside()
    cond_v, _, inverse_v, ratio_v = constants(cond_t, leak_t)
    rate_v = [bind_t[0, i] * DT for i in range(3)]
    tis_at = parts * HALO * width
    conc_at = tis_at + HALO * rows
    ends = edges((rows, lanes))

    def labels_of(side, j):
        return side[tis_at + j * rows : tis_at + (j + 1) * rows, :]

    def halo(side, j, e, valid):
        labels = labels_of(side, j)
        c = select(labels, cond_v) * valid
        level(e, c, ends, kx, ky)
        put(inverse, e, select(labels, inverse_v))
        return c

    low = [halo(from_low, j, j, has_low) for j in range(HALO)] + [select(at(tissue, 0, rows), cond_v)]
    high = [select(at(tissue, layers - 1, rows), cond_v)] + [halo(from_high, j, layers + HALO + j, has_high) for j in range(HALO)]
    for j in range(HALO):
        put(kz, j, low[j] * low[j + 1])
        put(kz, layers + HALO - 1 + j, high[j] * high[j + 1])
    for side, j, layer in ((from_low, HALO - 1, 0), (from_high, 0, layers + 1)):
        put(keep, layer, remaining(select(labels_of(side, j), rate_v), diffuse_t[0] * DT, ends))
    for j in range(TSTEPS):
        span = slice(conc_at + j * rows, conc_at + (j + 1) * rows)
        put(wide, j, from_low[span, :])
        put(wide, layers + TSTEPS + j, from_high[span, :])

    for k in range(parts):
        column = pl.multiple_of((me ^ k) * width, width)

        def spot(layer):
            return pl.ds(pl.multiple_of(layer * rows + column, width), width)

        for i in range(rim):
            top = i + (layers - rim)
            p0[spot(i + HALO), :] = blocks[k * 2 * rim + i] * ratio[spot(i), :]
            p0[spot(top + HALO), :] = blocks[k * 2 * rim + rim + i] * ratio[spot(top), :]
        for j in range(HALO):
            span = slice((k * HALO + j) * width, (k * HALO + j + 1) * width)
            for side, e in ((from_low, j), (from_high, layers + HALO + j)):
                labels = side[pl.ds(pl.multiple_of(tis_at + j * rows + column, width), width), :]
                p0[spot(e), :] = side[span, :] * select(labels, ratio_v)

    faces = (kx, ky, kz)

    def both(e, carry):
        image(e, rows, faces, inverse, p0, u0, p_next)
        image(layers + 2 * HALO - 1 - e, rows, faces, inverse, p0, u0, p_next)
        return carry

    lax.fori_loop(1, rim + HALO - 1, both, 0)
    for e in (HALO - 1, layers + HALO):
        put(u_next, e, following(at(u0, e, rows), 1))

    def sum_over(first, count, totals):
        def body(i, carry):
            return products(i + HALO, rows, carry, faces, diag, p0, u0, u_next)

        return lax.fori_loop(first, first + count, body, totals)

    zero = jnp.zeros((8, lanes), jnp.float32)
    totals = sum_over(0, rim - 2, (zero,) * 4)
    totals = sum_over(layers - rim + 1, rim - 1, totals)
    for i in range(4):
        sums[i] = totals[i]


def core_kernel(parts, rim, rows, vp, *refs):
    inner = refs[: parts - 1]
    refs = refs[parts - 1 :]
    kx, ky, kz, diag, inverse, ratio, part = refs[:7]
    p0, u0, p_next, u_next, sums = refs[11:]
    layers, width, _ = vp.shape
    me = lax.axis_index("size")
    for k in range(parts):
        column = pl.multiple_of((me ^ k) * width, width)
        source = vp if k == 0 else inner[k - 1]
        start = rim if k == 0 else 0

        def spot(layer):
            return pl.ds(pl.multiple_of(layer * rows + column, width), width)

        for i in range(layers - 2 * rim):
            p0[spot(i + (rim + HALO)), :] = source[i + start] * ratio[spot(i + rim), :]

    faces = (kx, ky, kz)
    first = rim + HALO - 1
    last = layers - rim + HALO

    def terms(e, totals):
        return products(e, rows, totals, faces, diag, p0, u0, u_next)

    def picture(e):
        image(e, rows, faces, inverse, p0, u0, p_next)

    def body(i, totals):
        e = first + 2 * i
        totals = terms(e - 2, terms(e - 3, totals))
        picture(e)
        picture(e + 1)
        return totals

    picture(first)
    picture(first + 1)
    pairs = (last + 1 - first) // 2
    totals = lax.fori_loop(1, pairs, body, tuple(part[i] for i in range(4)))
    done = first + 2 * pairs
    for e in range(done, last + 1):
        picture(e)
    for e in range(done - 3, last + 1):
        totals = terms(e, totals)
    sums[...] = jnp.concatenate([t.sum(0, keepdims=True) for t in totals] * 2, 0)


def slide_kernel(rows, wide, low, high):
    def body(i, carry):
        conc = at(wide, i + 1, rows)
        put(low, i, preceding(conc, 1))
        put(high, i, following(conc, 1))
        return carry

    lax.fori_loop(0, low.shape[0] // rows, body, 0, unroll=2)


def transport_kernel(width, rows, hinder_t, diffuse_t, mine, theirs, p0, u0, p_next, u_next, kx, ky, kz, rate, keep, wide, wide_low, wide_high, bound, pressure, free_out, bound_out, press, first, kept, zo, zb, xo, xb, yo, yb):
    lanes = bound.shape[1]
    layers = bound.shape[0] // rows
    me = lax.axis_index("size")
    has_low, has_high = inside()
    sums = mine[...] + theirs[...]
    rho, drop, second, shared = [jnp.sum(sums[i : i + 1, :], axis=1, keepdims=True) for i in range(4)]
    third = second - 2.0 * shared
    alpha = rho / drop
    rho_next = alpha * alpha * second - rho
    beta = rho_next / rho
    curve = drop - 2.0 * alpha * second + alpha * alpha * third - beta * rho_next / alpha
    alpha_next = rho_next / curve
    on_p = jnp.broadcast_to(alpha + alpha_next * (1.0 + beta), (8, lanes))[None]
    on_u = jnp.broadcast_to(-alpha_next * alpha, (8, lanes))[None]
    diffuse = diffuse_t[0] * DT
    hinder = hinder_t[0] * DT

    def combine(p, u, by_p, by_u):
        return (by_p * p.reshape(-1, 8, lanes) + by_u * u.reshape(-1, 8, lanes)).reshape(p.shape)

    def own(i, carry):
        spot = pl.ds(pl.multiple_of((i + HALO) * rows + me * width, width), width)
        put(pressure, i, combine(p0[spot, :], u0[spot, :], on_p, on_u))
        return carry

    lax.fori_loop(0, layers, own, 0, unroll=8)
    drive_p, drive_u = hinder * on_p, hinder * on_u

    def halves(flow, through):
        out = jnp.maximum(flow, 0.0) + through
        return out, out - flow

    def near(ref, layer, shift=0):
        return at(ref, layer, rows, shift)

    def store(ref, layer, value):
        put(ref, layer, value)

    def drive(e):
        store(press, e, combine(near(p0, e), near(u0, e), drive_p, drive_u))

    lane = lax.broadcasted_iota(jnp.int32, (rows, lanes), 1)
    row = lax.broadcasted_iota(jnp.int32, (rows, lanes), 0)
    along = jnp.where(row == rows - 1, 0.0, diffuse)
    rising = jnp.where(lane == lanes - 1, 0.0, diffuse)
    falling = jnp.where(lane == 0, 0.0, diffuse)

    def advance(i):
        e = i + TSTEPS
        here, conc = near(press, e), near(wide, i + 1)
        z_out, z_back = near(zo, i), near(zb, i)
        z_up, z_down = halves(near(kz, e) * (here - near(press, e + 1)), diffuse)
        stay = near(keep, i) - z_up - z_back
        moved = z_out * near(wide, i) + z_down * near(wide, i + 2)
        out, back = halves(near(kx, e) * (here - near(press, e, 1)), along)
        into = preceding(out, 0)
        stay = stay - out - preceding(back, 0)
        moved = moved + into * near(wide, i + 1, -1) + back * near(wide, i + 1, 1)
        flow = near(ky, e) * (here - combine(near(p_next, e), near(u_next, e), drive_p, drive_u))
        out, y_back = halves(flow, rising)
        y_into, y_low = halves(preceding(flow, 1), falling)
        stay = stay - out - y_low
        moved = moved + y_into * near(wide_low, i) + y_back * near(wide_high, i)
        drive(e + 2)
        for ref, value in ((zo, z_up), (zb, z_down), (xo, into), (xb, back), (yo, y_into), (yb, y_back), (kept, stay)):
            store(ref, i + 1, value)
        valid = jnp.where(i == 0, has_low, jnp.where(i == layers + 1, has_high, 1.0))
        store(first, i + 1, (stay * conc + moved) * valid)

    def finish(i):
        here = near(first, i + 1)
        result = near(kept, i + 1) * here + near(zo, i) * near(first, i) + near(zb, i + 1) * near(first, i + 2)
        result = result + near(xo, i + 1) * near(first, i + 1, -1) + near(xb, i + 1) * near(first, i + 1, 1)
        result = result + near(yo, i + 1) * preceding(here, 1) + near(yb, i + 1) * following(here, 1)
        store(free_out, i - 1, result)
        gain = near(rate, i - 1) * (near(wide, i + 1) + here)
        store(bound_out, i - 1, near(bound, i - 1) + gain)

    for e in range(TSTEPS - 1, TSTEPS + 2):
        drive(e)
    z_out, z_back = halves(near(kz, TSTEPS - 1) * (near(press, TSTEPS - 1) - near(press, TSTEPS)), diffuse)
    store(zo, 0, z_out)
    store(zb, 0, z_back)

    def begin(i, carry):
        advance(i)
        return carry

    lax.fori_loop(0, 3, begin, 0)

    def body(i, carry):
        finish(i - 2)
        advance(i)
        return carry

    lax.fori_loop(3, layers + 2, body, 0)
    finish(layers)


def swapped(array, axis, bit):
    count = lax.axis_size(axis)
    return lax.ppermute(array, axis, [(i, i ^ bit) for i in range(count)])


def butterfly(array, axis):
    bit = 1
    while bit < lax.axis_size(axis):
        array = jnp.concatenate([array, swapped(array, axis, bit)], 0)
        bit *= 2
    return array


def across(low, high):
    count = lax.axis_size("gz")
    from_low = lax.ppermute(high, "gz", [(i, i + 1) for i in range(count - 1)])
    from_high = lax.ppermute(low, "gz", [(i + 1, i) for i in range(count - 1)])
    return from_low, from_high


def total_over(array, axis):
    count = lax.axis_size(axis)
    step = 1
    while True:
        other = swapped(array, axis, step)
        step *= 2
        if step == count:
            return array, other
        array = array + other


def smem():
    return pl.BlockSpec(memory_space=pltpu.SMEM)


def vmem():
    return pl.BlockSpec(memory_space=pltpu.VMEM)


def f32(*shape):
    return jax.ShapeDtypeStruct(shape, jnp.float32)


def call(kernel, outs, scalars, arrays, scratch=(), aliases={}):
    size = sum(4 * math.prod(a.shape) for a in list(outs) + list(arrays) + list(scratch))
    return pl.pallas_call(
        kernel,
        out_shape=tuple(outs),
        in_specs=[smem()] * len(scalars) + [vmem()] * len(arrays),
        out_specs=(vmem(),) * len(outs),
        scratch_shapes=[pltpu.VMEM(s.shape, s.dtype) for s in scratch],
        input_output_aliases=aliases,
        compiler_params=pltpu.CompilerParams(vmem_limit_bytes=size + (4 << 20)),
    )(*scalars, *arrays)


def program(tissue, vessel_pressure, cond_table, leak_table, bind_table, hindrance, diffusivity, free_conc, bound_conc):
    layers, width, lanes = vessel_pressure.shape
    rows = tissue.shape[1]
    parts = rows // width
    rim = HALO
    conc, bound = free_conc[0], bound_conc[0]
    slab = f32(layers * rows, lanes)
    extended = f32((layers + 2 * HALO) * rows, lanes)
    stepped = f32((layers + 2) * rows, lanes)
    wider = f32((layers + 2 * TSTEPS) * rows, lanes)
    rims, middle = call(
        functools.partial(split_kernel, rim),
        [f32(2 * rim, width, lanes), f32(layers - 2 * rim, width, lanes)],
        [],
        [vessel_pressure],
    )
    blocks = butterfly(rims, "size")
    inner = [swapped(middle, "size", k) for k in range(1, parts)]
    border = f32((HALO + TSTEPS) * rows, lanes)
    border_low, border_high = call(border_kernel, [border] * 2, [], [tissue, conc])

    def payload(first, border):
        pieces = [blocks[k * 2 * rim + first : k * 2 * rim + first + HALO] for k in range(parts)] + [border]
        return jnp.concatenate([a.reshape(-1, lanes) for a in pieces], 0)

    from_low, from_high = across(payload(0, border_low), payload(2 * rim - HALO, border_high))
    tissue, conc, bound = (a.reshape(-1, lanes) for a in (tissue, conc, bound))
    kx, ky, kz, diag, inverse, ratio, rate, keep, wide = call(
        functools.partial(prepare_kernel, rows),
        [extended] * 3 + [slab, extended, slab, slab, stepped, wider],
        [cond_table, leak_table, bind_table, diffusivity],
        [tissue, conc],
    )
    kx, ky, kz, inverse, keep, wide, p0, u0, p_next, u_next, part = call(
        functools.partial(rim_kernel, parts, rim, width, rows),
        [extended] * 4 + [stepped, wider] + [extended] * 4 + [f32(4, 8, lanes)],
        [cond_table, leak_table, bind_table, diffusivity],
        [blocks, from_low, from_high, tissue, diag, ratio, kx, ky, kz, inverse, keep, wide],
        aliases={10 + i: i for i in range(6)},
    )
    p0, u0, p_next, u_next, sums = call(
        functools.partial(core_kernel, parts, rim, rows),
        [extended] * 4 + [f32(8, lanes)],
        [],
        [vessel_pressure, *inner, kx, ky, kz, diag, inverse, ratio, part, p0, u0, p_next, u_next],
        aliases={parts + 7 + i: i for i in range(4)},
    )
    wide_low, wide_high = call(functools.partial(slide_kernel, rows), [stepped] * 2, [], [wide])
    mine, theirs = total_over(sums, "gz")
    pressure, free, bound = call(
        functools.partial(transport_kernel, width, rows),
        [f32(layers * width, lanes), slab, slab],
        [hindrance, diffusivity],
        [mine, theirs, p0, u0, p_next, u_next, kx, ky, kz, rate, keep, wide, wide_low, wide_high, bound],
        scratch=[f32((layers + 2 * HALO + 1) * rows, lanes)] + [wider] * 8,
    )
    shape = (1, layers, rows, lanes)
    return pressure.reshape(layers, width, lanes), free.reshape(shape), bound.reshape(shape)


def solution(mesh):
    return jax.shard_map(
        program,
        mesh=mesh,
        in_specs=(
            P("gz", None, None),
            P("gz", "size", None),
            P(),
            P(),
            P("size", None),
            P("size"),
            P("size"),
            P("size", "gz", None, None),
            P("size", "gz", None, None),
        ),
        out_specs=(P("gz", "size", None), P("size", "gz", None, None), P("size", "gz", None, None)),
        check_vma=False,
    )
```

time: 60 us -> 56.6 us (0.943)
  Pallas kernels: 15.4 us -> 13.4 us
  waiting for transfers between devices: 24.8 us -> 23.3 us
    ppermute x3 -> x0, waiting for transfers between devices: 4.38 us -> none  [total_over(): other = lax.ppermute(array, axis, [(i, i ^ step) for i in range(count)])]
    ppermute x5 -> x8, waiting for transfers between devices: 20.4 us -> 23.3 us  [swapped(): return lax.ppermute(array, axis, [(i, i ^ bit) for i in range(count)])]
    ppermute x5 -> x8, starting transfers between devices: 6.75 us -> 9.51 us  [swapped(): return lax.ppermute(array, axis, [(i, i ^ bit) for i in range(count)])]
    ppermute x3 -> x0, starting transfers between devices: 2.76 us -> none  [total_over(): other = lax.ppermute(array, axis, [(i, i ^ step) for i in range(count)])]
    pallas_call x6 -> x7, Pallas kernels: 15.4 us -> 13.4 us  [call(): pl.pallas_call(kernel, out_shape=tuple(outs), in_specs=[smem()] * len(sca...]
  transfers between devices with their start and end apart: 10 -> 10, of which waited for: 8 -> 7; matrix products, arithmetic and copies ran while one was open for 0% -> 0% of each run, Pallas kernels for 6% -> 10%
where the time goes in v2:
time: 56.6 us; the launch traced here: 56.3 us
  waiting for transfers between devices  23.3 us (41%)
  starting transfers between devices  13.9 us (25%)
  Pallas kernels  13.4 us (24%)
  local copies, waits for them, and re-layouts  3.51 us (6%)
  between operations  2.21 us (4%)
    ppermute x8, waiting for transfers between devices, swapped(): return lax.ppermute(array, axis, [(i, i ^ bit) for i in range(count)])  23.3 us
    pallas_call x7, Pallas kernels, call(): pl.pallas_call(kernel, out_shape=tuple(outs), in_specs=[smem()] * len(sca...  13.4 us
    ppermute x8, starting transfers between devices, swapped(): return lax.ppermute(array, axis, [(i, i ^ bit) for i in range(count)])  9.51 us
    unnamed x28, local copies, waits for them, and re-layouts  3.47 us
    ppermute x1, starting transfers between devices, across(): from_low = lax.ppermute(high, 'gz', [(i, i + 1) for i in range(count - 1)])  3.05 us
    ppermute x1, starting transfers between devices, across(): from_high = lax.ppermute(low, 'gz', [(i + 1, i) for i in range(count - 1)])  1.29 us
  transfers between devices with their start and end apart: 10, of which 7 were waited for; matrix products, arithmetic and copies ran while one was open for 0% of the time, Pallas kernels for 10%

profile of v2, /device:TPU:8, one launch (start us, length us, event | category | flops | bytes accessed | tf_op | source)
XLA Modules:
  0.0 56.3 jit_solution(2050636826986237784)
XLA Ops:
  0.6 0.0 copy-start.5
  0.6 0.9 %copy-done.5 = f32[32,16,128]{2,1,0:T(8,128)S(1)} copy-done((f32[32,16,128]{2,1,0:T(8,128)S(1)}, f32[32,16,128]{2,1,0:T(8,128)}, u32[]{:S(2)}) %copy-start.5) | copy-done | bytes 262168
  1.6 0.1 collective-permute-start.3
  1.7 0.0 copy-start
  1.7 1.2 %copy-done = s32[32,64,128]{2,1,0:T(8,128)S(1)} copy-done((s32[32,64,128]{2,1,0:T(8,128)S(1)}, s32[32,64,128]{2,1,0:T(8,128)}, u32[]{:S(2)}) %copy-start) | copy-done | bytes 1048600
  2.9 0.0 copy-start.2
  3.0 1.2 %copy-done.2 = f32[1,32,64,128]{3,2,1,0:T(8,128)S(1)} copy-done((f32[1,32,64,128]{3,2,1,0:T(8,128)S(1)}, f32[1,32,64,128]{3,2,1,0:T(8,128)}, u32[]{:S(2)}) %copy-start.2) | copy-done | bytes 1048600
  4.2 0.0 copy-start.3
  4.2 0.0 copy-start.1
  4.2 0.0 copy-start.7
  4.2 0.0 copy-start.8
  4.2 0.0 copy-start.9
  4.2 1.5 %collective-permute-done.3 = f32[6,16,128]{2,1,0:T(8,128)S(1)} collective-permute-done((f32[6,16,128]{2,1,0:T(8,128)S(1)}, f32[6,16,128]{2,1,0:T(8,128)S(1)}, u32[]{:S(2)}, u32[]{:S(2)}) %collective-permute-start.3) | collective-permute-done | bytes 49184 | tf_op jit(solution)/shard_map/ppermute | solution.py:373
  5.8 2.7 %collective-permute-start.4 = (f32[12,16,128]{2,1,0:T(8,128)S(1)}, f32[12,16,128]{2,1,0:T(8,128)S(1)}, u32[]{:S(2)}, u32[]{:S(2)}) collective-permute-start(f32[12,16,128]{2,1,0:T(8,128)S(1)} %pad_maximum_fusion.1), channel_id=1, source_target_pairs={{0,16},{8,24},{16,0},{24,8},{1,17},{9,25},{17,1},{25,9},{2,18},{10... | collective-permute-start | bytes 294920 | tf_op jit(solution)/shard_map/ppermute | solution.py:373
  8.4 3.1 %collective-permute-done.4 = f32[12,16,128]{2,1,0:T(8,128)S(1)} collective-permute-done((f32[12,16,128]{2,1,0:T(8,128)S(1)}, f32[12,16,128]{2,1,0:T(8,128)S(1)}, u32[]{:S(2)}, u32[]{:S(2)}) %collective-permute-start.4) | collective-permute-done | bytes 98336 | tf_op jit(solution)/shard_map/ppermute | solution.py:373
  11.6 1.3 %collective-permute-start.6 = (f32[512,128]{1,0:T(8,128)S(1)}, f32[512,128]{1,0:T(8,128)S(1)}, u32[]{:S(2)}, u32[]{:S(2)}) collective-permute-start(f32[512,128]{1,0:T(8,128)S(1)} %constant_dynamic-update-slice_fusion.5), channel_id=1, source_target_pairs={{1,0},{2,1},{3,2},{4,3},{5,4},{6,5},{7,6},{9,8},{10,9},{11,10},{12... | collective-permute-start | bytes 786440 | tf_op jit(solution)/shard_map/ppermute | solution.py:387
  12.9 3.0 %collective-permute-start.5 = (f32[512,128]{1,0:T(8,128)S(1)}, f32[512,128]{1,0:T(8,128)S(1)}, u32[]{:S(2)}, u32[]{:S(2)}) collective-permute-start(f32[512,128]{1,0:T(8,128)S(1)} %constant_dynamic-update-slice_fusion), channel_id=1, source_target_pairs={{0,1},{1,2},{2,3},{3,4},{4,5},{5,6},{6,7},{8,9},{9,10},{10,11},{11... | collective-permute-start | bytes 786440 | tf_op jit(solution)/shard_map/ppermute | solution.py:386
  16.0 2.1 %collective-permute-start = (f32[26,16,128]{2,1,0:T(8,128)S(1)}, f32[26,16,128]{2,1,0:T(8,128)S(1)}, u32[]{:S(2)}, u32[]{:S(2)}) collective-permute-start(f32[26,16,128]{2,1,0:T(8,128)S(1)} %get-tuple-element.37), channel_id=1, source_target_pairs={{0,8},{8,0},{16,24},{24,16},{1,9},{9,1},{17,25},{25,17},{2,10},{10... | collective-permute-start | bytes 638984 | tf_op jit(solution)/shard_map/ppermute | solution.py:373
  18.1 1.4 %collective-permute-start.1 = (f32[26,16,128]{2,1,0:T(8,128)S(1)}, f32[26,16,128]{2,1,0:T(8,128)S(1)}, u32[]{:S(2)}, u32[]{:S(2)}) collective-permute-start(f32[26,16,128]{2,1,0:T(8,128)S(1)} %get-tuple-element.37), channel_id=1, source_target_pairs={{0,16},{8,24},{16,0},{24,8},{1,17},{9,25},{17,1},{25,9},{2,18},{10... | collective-permute-start | bytes 638984 | tf_op jit(solution)/shard_map/ppermute | solution.py:373
  19.5 0.5 collective-permute-start.2
  20.7 0.0 copy-done.3
  20.7 0.0 copy-done.1
  20.7 0.0 copy-done.7
  20.7 0.0 copy-done.8
  20.7 0.0 copy-done.9
  20.7 2.4 %shard_map.114 = (f32[2432,128]{1,0:T(8,128)S(1)}, f32[2432,128]{1,0:T(8,128)S(1)}, f32[2432,128]{1,0:T(8,128)S(1)}, f32[2048,128]{1,0:T(8,128)S(1)}, f32[2432,1...) custom-call(f32[3]{0:T(128)S(1)} %copy-done.7, ...), custom_call_target="tpu_custom_call" | custom-call | tf_op jit(solution)/shard_map/pallas_call | solution.py:416
  23.1 0.0 collective-permute-done.6.from_high
  23.1 0.0 collective-permute-done.5.from_low
  23.1 0.0 copy-start.6
  23.2 1.5 %shard_map.115 = (f32[2432,128]{1,0:T(8,128)S(1)}, f32[2432,128]{1,0:T(8,128)S(1)}, f32[2432,128]{1,0:T(8,128)S(1)}, f32[2432,128]{1,0:T(8,128)S(1)}, f32[2176,1...) custom-call(f32[3]{0:T(128)S(1)} %copy-done.7, ...), custom_call_target="tpu_custom_call", output_to_operand_aliasing={{0}: (10, {}), {1}: (11, {}), {2}: (12, {}), {3}: (13, {}),... | custom-call | tf_op jit(solution)/shard_map/pallas_call | solution.py:416
  24.6 3.0 %collective-permute-done.refs_0_ = f32[26,16,128]{2,1,0:T(8,128)S(1)} collective-permute-done((f32[26,16,128]{2,1,0:T(8,128)S(1)}, f32[26,16,128]{2,1,0:T(8,128)S(1)}, u32[]{:S(2)}, u32[]{:S(2)}) %collective-permute-start) | collective-permute-done | bytes 213024 | tf_op jit(solution)/shard_map/ppermute | solution.py:373
  27.7 6.5 %collective-permute-done.1.refs_1_ = f32[26,16,128]{2,1,0:T(8,128)S(1)} collective-permute-done((f32[26,16,128]{2,1,0:T(8,128)S(1)}, f32[26,16,128]{2,1,0:T(8,128)S(1)}, u32[]{:S(2)}, u32[]{:S(2)}) %collective-permute-start.1) | collective-permute-done | bytes 213024 | tf_op jit(solution)/shard_map/ppermute | solution.py:373
  34.2 5.5 %collective-permute-done.2.refs_2_ = f32[26,16,128]{2,1,0:T(8,128)S(1)} collective-permute-done((f32[26,16,128]{2,1,0:T(8,128)S(1)}, f32[26,16,128]{2,1,0:T(8,128)S(1)}, u32[]{:S(2)}, u32[]{:S(2)}) %collective-permute-start.2) | collective-permute-done | bytes 213024 | tf_op jit(solution)/shard_map/ppermute | solution.py:373
  39.7 0.0 copy-done.6
  39.7 2.2 %shard_map.116 = (f32[2432,128]{1,0:T(8,128)S(1)}, f32[2432,128]{1,0:T(8,128)S(1)}, f32[2432,128]{1,0:T(8,128)S(1)}, f32[2432,128]{1,0:T(8,128)S(1)}, f32[8,128]{1,0:T(8,128)S(1)}) custom-call(f32[32,16,128]{2,1,0:T(8,128)S(1)} %copy-done.6, ...), custom_call_target="tpu_custom_call", output_to_operand_aliasing={{0}: (11, {}), {1}: (12, {}), {2}: (13, {}), {3}: (14, {})} | custom-call | tf_op jit(solution)/shard_map/pallas_call | solution.py:416
  42.0 0.0 copy-start.4
  42.0 0.2 collective-permute-start.7
  42.2 1.1 %collective-permute-done.7 = f32[8,128]{1,0:T(8,128)S(1)} collective-permute-done((f32[8,128]{1,0:T(8,128)S(1)}, f32[8,128]{1,0:T(8,128)S(1)}, u32[]{:S(2)}, u32[]{:S(2)}) %collective-permute-start.7) | collective-permute-done | bytes 4128 | tf_op jit(solution)/shard_map/ppermute | solution.py:373
  43.2 1.1 %collective-permute-start.8 = (f32[8,128]{1,0:T(8,128)S(1)}, f32[8,128]{1,0:T(8,128)S(1)}, u32[]{:S(2)}, u32[]{:S(2)}) collective-permute-start(f32[8,128]{1,0:T(8,128)S(1)} %add.6), channel_id=1, source_target_pairs={{0,2},{1,3},{2,0},{3,1},{4,6},{5,7},{6,4},{7,5},{8,10},{9,11},{10,... | collective-permute-start | bytes 12296 | tf_op jit(solution)/shard_map/ppermute | solution.py:373
  44.3 2.5 %collective-permute-done.8 = f32[8,128]{1,0:T(8,128)S(1)} collective-permute-done((f32[8,128]{1,0:T(8,128)S(1)}, f32[8,128]{1,0:T(8,128)S(1)}, u32[]{:S(2)}, u32[]{:S(2)}) %collective-permute-start.8) | collective-permute-done | bytes 4128 | tf_op jit(solution)/shard_map/ppermute | solution.py:373
  46.8 1.5 %collective-permute-start.9 = (f32[8,128]{1,0:T(8,128)S(1)}, f32[8,128]{1,0:T(8,128)S(1)}, u32[]{:S(2)}, u32[]{:S(2)}) collective-permute-start(f32[8,128]{1,0:T(8,128)S(1)} %add.7.mine), channel_id=1, source_target_pairs={{0,4},{1,5},{2,6},{3,7},{4,0},{5,1},{6,2},{7,3},{8,12},{9,13},{10,... | collective-permute-start | bytes 12296 | tf_op jit(solution)/shard_map/ppermute | solution.py:373
  49.0 1.7 %shard_map.117 = (f32[2176,128]{1,0:T(8,128)S(1)}, f32[2176,128]{1,0:T(8,128)S(1)}) custom-call(f32[2304,128]{1,0:T(8,128)S(1)} %get-tuple-element.65.wide), custom_call_target="tpu_custom_call" | custom-call | tf_op jit(solution)/shard_map/pallas_call | solution.py:416
  50.7 0.0 collective-permute-done.9.theirs
  50.7 0.0 copy-done.4
  50.7 5.6 %shard_map.118 = (f32[512,128]{1,0:T(8,128)}, f32[2048,128]{1,0:T(8,128)}, f32[2048,128]{1,0:T(8,128)}) custom-call(f32[1]{0:T(128)S(6)} %copy.40.hinder_t, f32[1]{0:T(128)S(6)} %copy.41.diffuse_t, f32[8,128]{1,0:T(8,128)S(1)} %add.7.mine, f32[8,128]{1,0:T(8,128)S(1)} %collective-permute-done.9.theirs, f32[2432,128]{1,0:T(8,128)S(1)} %get-tuple-element.59.p0, ...), custom_call_target="tpu_custom_call" | custom-call | tf_op jit(solution)/shard_map/pallas_call | solution.py:416
  (19 shorter events, 0.2 us)
Async XLA Ops:
  0.6 1.0 %copy-start.5 = (f32[32,16,128]{2,1,0:T(8,128)S(1)}, f32[32,16,128]{2,1,0:T(8,128)}, u32[]{:S(2)}) copy-start(f32[32,16,128]{2,1,0:T(8,128)} %vp.3) | copy-start | bytes 786436
  1.6 4.2 %collective-permute-start.3 = (f32[6,16,128]{2,1,0:T(8,128)S(1)}, f32[6,16,128]{2,1,0:T(8,128)S(1)}, u32[]{:S(2)}, u32[]{:S(2)}) collective-permute-start(f32[6,16,128]{2,1,0:T(8,128)S(1)} %get-tuple-element.38), channel_id=1, source_target_pairs={{0,8},{8,0},{16,24},{24,16},{1,9},{9,1},{17,25},{25,17},{2,10},{10... | collective-permute-start | bytes 147464 | tf_op jit(solution)/shard_map/ppermute | solution.py:373
  1.7 1.2 %copy-start = (s32[32,64,128]{2,1,0:T(8,128)S(1)}, s32[32,64,128]{2,1,0:T(8,128)}, u32[]{:S(2)}) copy-start(s32[32,64,128]{2,1,0:T(8,128)} %tissue.1) | copy-start | bytes 3145732
  2.9 1.2 %copy-start.2 = (f32[1,32,64,128]{3,2,1,0:T(8,128)S(1)}, f32[1,32,64,128]{3,2,1,0:T(8,128)}, u32[]{:S(2)}) copy-start(f32[1,32,64,128]{3,2,1,0:T(8,128)} %param.16) | copy-start | bytes 3145732
  4.2 16.5 %copy-start.3 = (f32[1,32,64,128]{3,2,1,0:T(8,128)S(1)}, f32[1,32,64,128]{3,2,1,0:T(8,128)}, u32[]{:S(2)}) copy-start(f32[1,32,64,128]{3,2,1,0:T(8,128)} %param.16) | copy-start | bytes 3145732
  4.2 16.5 %copy-start.1 = (s32[32,64,128]{2,1,0:T(8,128)S(1)}, s32[32,64,128]{2,1,0:T(8,128)}, u32[]{:S(2)}) copy-start(s32[32,64,128]{2,1,0:T(8,128)} %tissue.1) | copy-start | bytes 3145732
  4.2 16.5 %copy-start.7 = (f32[3]{0:T(128)S(1)}, f32[3]{0:T(128)}, u32[]{:S(2)}) copy-start(f32[3]{0:T(128)} %cond_t.3) | copy-start | bytes 40
  4.2 16.5 %copy-start.8 = (f32[3]{0:T(128)S(1)}, f32[3]{0:T(128)}, u32[]{:S(2)}) copy-start(f32[3]{0:T(128)} %leak_t.3) | copy-start | bytes 40
  4.2 16.5 %copy-start.9 = (f32[1,3]{1,0:T(1,128)S(1)}, f32[1,3]{1,0:T(1,128)}, u32[]{:S(2)}) copy-start(f32[1,3]{1,0:T(1,128)} %bind_t.3) | copy-start | bytes 40
  5.8 5.8 %collective-permute-start.4 = (f32[12,16,128]{2,1,0:T(8,128)S(1)}, f32[12,16,128]{2,1,0:T(8,128)S(1)}, u32[]{:S(2)}, u32[]{:S(2)}) collective-permute-start(f32[12,16,128]{2,1,0:T(8,128)S(1)} %pad_maximum_fusion.1), channel_id=1, source_target_pairs={{0,16},{8,24},{16,0},{24,8},{1,17},{9,25},{17,1},{25,9},{2,18},{10... | collective-permute-start | bytes 294920 | tf_op jit(solution)/shard_map/ppermute | solution.py:373
  11.6 11.5 %collective-permute-start.6 = (f32[512,128]{1,0:T(8,128)S(1)}, f32[512,128]{1,0:T(8,128)S(1)}, u32[]{:S(2)}, u32[]{:S(2)}) collective-permute-start(f32[512,128]{1,0:T(8,128)S(1)} %constant_dynamic-update-slice_fusion.5), channel_id=1, source_target_pairs={{1,0},{2,1},{3,2},{4,3},{5,4},{6,5},{7,6},{9,8},{10,9},{11,10},{12... | collective-permute-start | bytes 786440 | tf_op jit(solution)/shard_map/ppermute | solution.py:387
  12.9 10.2 %collective-permute-start.5 = (f32[512,128]{1,0:T(8,128)S(1)}, f32[512,128]{1,0:T(8,128)S(1)}, u32[]{:S(2)}, u32[]{:S(2)}) collective-permute-start(f32[512,128]{1,0:T(8,128)S(1)} %constant_dynamic-update-slice_fusion), channel_id=1, source_target_pairs={{0,1},{1,2},{2,3},{3,4},{4,5},{5,6},{6,7},{8,9},{9,10},{10,11},{11... | collective-permute-start | bytes 786440 | tf_op jit(solution)/shard_map/ppermute | solution.py:386
  16.0 11.7 %collective-permute-start = (f32[26,16,128]{2,1,0:T(8,128)S(1)}, f32[26,16,128]{2,1,0:T(8,128)S(1)}, u32[]{:S(2)}, u32[]{:S(2)}) collective-permute-start(f32[26,16,128]{2,1,0:T(8,128)S(1)} %get-tuple-element.37), channel_id=1, source_target_pairs={{0,8},{8,0},{16,24},{24,16},{1,9},{9,1},{17,25},{25,17},{2,10},{10... | collective-permute-start | bytes 638984 | tf_op jit(solution)/shard_map/ppermute | solution.py:373
  18.1 16.1 %collective-permute-start.1 = (f32[26,16,128]{2,1,0:T(8,128)S(1)}, f32[26,16,128]{2,1,0:T(8,128)S(1)}, u32[]{:S(2)}, u32[]{:S(2)}) collective-permute-start(f32[26,16,128]{2,1,0:T(8,128)S(1)} %get-tuple-element.37), channel_id=1, source_target_pairs={{0,16},{8,24},{16,0},{24,8},{1,17},{9,25},{17,1},{25,9},{2,18},{10... | collective-permute-start | bytes 638984 | tf_op jit(solution)/shard_map/ppermute | solution.py:373
  19.5 20.2 %collective-permute-start.2 = (f32[26,16,128]{2,1,0:T(8,128)S(1)}, f32[26,16,128]{2,1,0:T(8,128)S(1)}, u32[]{:S(2)}, u32[]{:S(2)}) collective-permute-start(f32[26,16,128]{2,1,0:T(8,128)S(1)} %get-tuple-element.37), channel_id=1, source_target_pairs={{0,24},{8,16},{16,8},{24,0},{1,25},{9,17},{17,9},{25,1},{2,26},{10... | collective-permute-start | bytes 638984 | tf_op jit(solution)/shard_map/ppermute | solution.py:373
  23.1 16.6 %copy-start.6 = (f32[32,16,128]{2,1,0:T(8,128)S(1)}, f32[32,16,128]{2,1,0:T(8,128)}, u32[]{:S(2)}) copy-start(f32[32,16,128]{2,1,0:T(8,128)} %vp.3) | copy-start | bytes 786436
  42.0 8.7 %copy-start.4 = (f32[1,32,64,128]{3,2,1,0:T(8,128)S(1)}, f32[1,32,64,128]{3,2,1,0:T(8,128)}, u32[]{:S(2)}) copy-start(f32[1,32,64,128]{3,2,1,0:T(8,128)} %param.17) | copy-start | bytes 3145732
  42.0 1.2 %collective-permute-start.7 = (f32[8,128]{1,0:T(8,128)S(1)}, f32[8,128]{1,0:T(8,128)S(1)}, u32[]{:S(2)}, u32[]{:S(2)}) collective-permute-start(f32[8,128]{1,0:T(8,128)S(1)} %get-tuple-element.58), channel_id=1, source_target_pairs={{0,1},{1,0},{2,3},{3,2},{4,5},{5,4},{6,7},{7,6},{8,9},{9,8},{10,11... | collective-permute-start | bytes 12296 | tf_op jit(solution)/shard_map/ppermute | solution.py:373
  43.2 3.6 %collective-permute-start.8 = (f32[8,128]{1,0:T(8,128)S(1)}, f32[8,128]{1,0:T(8,128)S(1)}, u32[]{:S(2)}, u32[]{:S(2)}) collective-permute-start(f32[8,128]{1,0:T(8,128)S(1)} %add.6), channel_id=1, source_target_pairs={{0,2},{1,3},{2,0},{3,1},{4,6},{5,7},{6,4},{7,5},{8,10},{9,11},{10,... | collective-permute-start | bytes 12296 | tf_op jit(solution)/shard_map/ppermute | solution.py:373
  46.8 3.9 %collective-permute-start.9 = (f32[8,128]{1,0:T(8,128)S(1)}, f32[8,128]{1,0:T(8,128)S(1)}, u32[]{:S(2)}, u32[]{:S(2)}) collective-permute-start(f32[8,128]{1,0:T(8,128)S(1)} %add.7.mine), channel_id=1, source_target_pairs={{0,4},{1,5},{2,6},{3,7},{4,0},{5,1},{6,2},{7,3},{8,12},{9,13},{10,... | collective-permute-start | bytes 12296 | tf_op jit(solution)/shard_map/ppermute | solution.py:373

commit v3 on v2

--- a/solution.py
+++ b/solution.py
@@ -10,6 +10,7 @@
 TSTEPS = 2
 HALO = TSTEPS + 1
 DT = 0.1
+EARLY = 8
 
 
 def select(labels, values):
@@ -72,22 +73,30 @@
     return tuple(a + t.reshape(-1, 8, t.shape[-1]).sum(0) for a, t in zip(totals, terms))
 
 
-def split_kernel(rim, vp, rims, inner):
+def split_kernel(rim, early, vp, rims, inner, ahead, rest):
     layers = vp.shape[0]
     rims[:rim] = vp[:rim]
     rims[rim:] = vp[layers - rim :]
     inner[...] = vp[rim : layers - rim]
-
-
-def border_kernel(tissue, conc, low, high):
+    ahead[...] = vp[rim : rim + early]
+    rest[...] = vp[rim + early : layers - rim]
+
+
+def border_kernel(tissue, conc, low, high, labels, sems):
     layers, rows, _ = tissue.shape
-    for j in range(HALO):
-        low[j * rows : (j + 1) * rows, :] = tissue[j].astype(jnp.float32)
-        high[j * rows : (j + 1) * rows, :] = tissue[layers - HALO + j].astype(jnp.float32)
-    for j in range(TSTEPS):
-        at = (HALO + j) * rows
-        low[at : at + rows, :] = conc[j]
-        high[at : at + rows, :] = conc[layers - TSTEPS + j]
+    copies = []
+    for side, out, first, start in ((0, low, 0, 0), (1, high, layers - HALO, layers - TSTEPS)):
+        copies.append(pltpu.make_async_copy(tissue.at[pl.ds(first, HALO)], labels.at[side], sems.at[side, 0]))
+        for j in range(TSTEPS):
+            spot = pl.ds((HALO + j) * rows, rows)
+            copies.append(pltpu.make_async_copy(conc.at[start + j], out.at[spot, :], sems.at[side, 1 + j]))
+    for copy in copies:
+        copy.start()
+    for copy in copies:
+        copy.wait()
+    for side, out in ((0, low), (1, high)):
+        for j in range(HALO):
+            out[j * rows : (j + 1) * rows, :] = labels[side, j].astype(jnp.float32)
 
 
 def constants(cond_t, leak_t):
@@ -137,8 +146,11 @@
     lax.fori_loop(0, layers, own, jnp.zeros(shape, jnp.float32), unroll=2)
 
 
-def rim_kernel(parts, rim, width, rows, cond_t, leak_t, bind_t, diffuse_t, blocks, from_low, from_high, tissue, diag, ratio, *refs):
-    kx, ky, kz, inverse, keep, wide, p0, u0, p_next, u_next, sums = refs[6:]
+def rim_kernel(parts, rim, width, rows, cond_t, leak_t, bind_t, diffuse_t, blocks, near, far, tissue, diag, ratio, *refs):
+    kx, ky, kz, inverse, keep, wide, p0, u0, p_next, u_next, sums, from_low, from_high = refs[6:]
+    odd = is_odd()
+    from_low[...] = jnp.where(odd, near[...], far[...])
+    from_high[...] = jnp.where(odd, far[...], near[...])
     lanes = tissue.shape[1]
     layers = tissue.shape[0] // rows
     me = lax.axis_index("size")
@@ -212,22 +224,23 @@
 
 
 def core_kernel(parts, rim, rows, vp, *refs):
-    inner = refs[: parts - 1]
-    refs = refs[parts - 1 :]
+    inner, refs = refs[:parts], refs[parts:]
     kx, ky, kz, diag, inverse, ratio, part = refs[:7]
     p0, u0, p_next, u_next, sums = refs[11:]
     layers, width, _ = vp.shape
     me = lax.axis_index("size")
-    for k in range(parts):
+    sources = [[vp.at[rim : layers - rim]], [inner[0]], [inner[1], inner[2]]] + [[ref] for ref in inner[3:]]
+    for k, pieces in enumerate(sources):
         column = pl.multiple_of((me ^ k) * width, width)
-        source = vp if k == 0 else inner[k - 1]
-        start = rim if k == 0 else 0
 
         def spot(layer):
             return pl.ds(pl.multiple_of(layer * rows + column, width), width)
 
-        for i in range(layers - 2 * rim):
-            p0[spot(i + (rim + HALO)), :] = source[i + start] * ratio[spot(i + rim), :]
+        layer = rim
+        for piece in pieces:
+            for i in range(piece.shape[0]):
+                p0[spot(layer + HALO), :] = piece[i] * ratio[spot(layer), :]
+                layer += 1
 
     faces = (kx, ky, kz)
     first = rim + HALO - 1
@@ -381,11 +394,17 @@
     return array
 
 
+def is_odd():
+    return lax.rem(lax.axis_index("gz"), 2) == 1
+
+
 def across(low, high):
     count = lax.axis_size("gz")
-    from_low = lax.ppermute(high, "gz", [(i, i + 1) for i in range(count - 1)])
-    from_high = lax.ppermute(low, "gz", [(i + 1, i) for i in range(count - 1)])
-    return from_low, from_high
+    pairs = [(i, i ^ 1) for i in range(count)]
+    near = lax.ppermute(jnp.where(is_odd(), low, high), "gz", pairs)
+    pairs = [(i, i + 1) for i in range(1, count - 1, 2)]
+    far = lax.ppermute(jnp.where(is_odd(), high, low), "gz", pairs + [(j, i) for i, j in pairs])
+    return near, far
 
 
 def total_over(array, axis):
@@ -434,22 +453,34 @@
     extended = f32((layers + 2 * HALO) * rows, lanes)
     stepped = f32((layers + 2) * rows, lanes)
     wider = f32((layers + 2 * TSTEPS) * rows, lanes)
-    rims, middle = call(
-        functools.partial(split_kernel, rim),
-        [f32(2 * rim, width, lanes), f32(layers - 2 * rim, width, lanes)],
+    count = layers - 2 * rim
+    early = EARLY * count // 32
+    rims, middle, ahead, rest = call(
+        functools.partial(split_kernel, rim, early),
+        [f32(2 * rim, width, lanes), f32(count, width, lanes), f32(early, width, lanes), f32(count - early, width, lanes)],
         [],
         [vessel_pressure],
     )
     blocks = butterfly(rims, "size")
-    inner = [swapped(middle, "size", k) for k in range(1, parts)]
+    inner = [(swapped(middle, "size", k),) for k in range(1, parts)]
+    inner[1] = (swapped(ahead, "size", 2), swapped(rest, "size", 2))
+    inner = [piece for pieces in inner for piece in pieces]
     border = f32((HALO + TSTEPS) * rows, lanes)
-    border_low, border_high = call(border_kernel, [border] * 2, [], [tissue, conc])
+    border_low, border_high = pl.pallas_call(
+        border_kernel,
+        out_shape=(border,) * 2,
+        in_specs=[pl.BlockSpec(memory_space=pltpu.HBM)] * 2,
+        out_specs=(vmem(),) * 2,
+        scratch_shapes=[pltpu.VMEM((2, HALO, rows, lanes), jnp.int32), pltpu.SemaphoreType.DMA((2, 1 + TSTEPS))],
+        compiler_params=pltpu.CompilerParams(vmem_limit_bytes=8 << 20),
+        name="border",
+    )(pltpu.with_memory_space_constraint(tissue, pltpu.HBM), pltpu.with_memory_space_constraint(conc, pltpu.HBM))
 
     def payload(first, border):
         pieces = [blocks[k * 2 * rim + first : k * 2 * rim + first + HALO] for k in range(parts)] + [border]
         return jnp.concatenate([a.reshape(-1, lanes) for a in pieces], 0)
 
-    from_low, from_high = across(payload(0, border_low), payload(2 * rim - HALO, border_high))
+    near, far = across(payload(0, border_low), payload(2 * rim - HALO, border_high))
     tissue, conc, bound = (a.reshape(-1, lanes) for a in (tissue, conc, bound))
     kx, ky, kz, diag, inverse, ratio, rate, keep, wide = call(
         functools.partial(prepare_kernel, rows),
@@ -461,7 +492,8 @@
         functools.partial(rim_kernel, parts, rim, width, rows),
         [extended] * 4 + [stepped, wider] + [extended] * 4 + [f32(4, 8, lanes)],
         [cond_table, leak_table, bind_table, diffusivity],
-        [blocks, from_low, from_high, tissue, diag, ratio, kx, ky, kz, inverse, keep, wide],
+        [blocks, near, far, tissue, diag, ratio, kx, ky, kz, inverse, keep, wide],
+        scratch=[f32(*near.shape)] * 2,
         aliases={10 + i: i for i in range(6)},
     )
     p0, u0, p_next, u_next, sums = call(
@@ -469,7 +501,7 @@
         [extended] * 4 + [f32(8, lanes)],
         [],
         [vessel_pressure, *inner, kx, ky, kz, diag, inverse, ratio, part, p0, u0, p_next, u_next],
-        aliases={parts + 7 + i: i for i in range(4)},
+        aliases={parts + 8 + i: i for i in range(4)},
     )
     wide_low, wide_high = call(functools.partial(slide_kernel, rows), [stepped] * 2, [], [wide])
     mine, theirs = total_over(sums, "gz")

time: 56.6 us -> 57.4 us (1.014)
  the two profiles are of different devices: /device:TPU:8 before, /device:TPU:0 now
where the time goes in v3:
time: 57.4 us; the launch traced here: 57.2 us
  starting transfers between devices  22.5 us (39%)
  waiting for transfers between devices  16.8 us (29%)
  Pallas kernels  14.5 us (25%)
  between operations  2.2 us (4%)
  local copies, waits for them, and re-layouts  1.07 us (2%)
    ppermute x9, starting transfers between devices, swapped(): return lax.ppermute(array, axis, [(i, i ^ bit) for i in range(count)])  21.8 us
    ppermute x9, waiting for transfers between devices, swapped(): return lax.ppermute(array, axis, [(i, i ^ bit) for i in range(count)])  16.8 us
    pallas_call x6, Pallas kernels, call(): pl.pallas_call(kernel, out_shape=tuple(outs), in_specs=[smem()] * len(sca...  13.5 us
  transfers between devices with their start and end apart: 11, of which 5 were waited for; matrix products, arithmetic and copies ran while one was open for 0% of the time, Pallas kernels for 12%

profile of v3, /device:TPU:0, one launch (start us, length us, event | category | flops | bytes accessed | tf_op | source)
XLA Modules:
  0.0 57.2 jit_solution(9256033541988814704)
XLA Ops:
  0.6 0.0 copy-start.3
  0.6 0.9 %copy-done.3 = f32[32,16,128]{2,1,0:T(8,128)S(1)} copy-done((f32[32,16,128]{2,1,0:T(8,128)S(1)}, f32[32,16,128]{2,1,0:T(8,128)}, u32[]{:S(2)}) %copy-start.3) | copy-done | bytes 262168
  1.6 3.1 %collective-permute-start.4 = (f32[6,16,128]{2,1,0:T(8,128)S(1)}, f32[6,16,128]{2,1,0:T(8,128)S(1)}, u32[]{:S(2)}, u32[]{:S(2)}) collective-permute-start(f32[6,16,128]{2,1,0:T(8,128)S(1)} %get-tuple-element.42), channel_id=1, source_target_pairs={{0,8},{8,0},{16,24},{24,16},{1,9},{9,1},{17,25},{25,17},{2,10},{10... | collective-permute-start | bytes 147464 | tf_op jit(solution)/shard_map/ppermute | solution.py:386
  4.8 1.1 %border.1 = (f32[320,128]{1,0:T(8,128)S(1)}, f32[320,128]{1,0:T(8,128)S(1)}) custom-call(s32[32,64,128]{2,1,0:T(8,128)} %tissue.1, f32[32,64,128]{2,1,0:T(8,128)} %bitcast.17), custom_call_target="tpu_custom_call" | custom-call | tf_op jit(solution)/shard_map/border/pallas_call | solution.py:469
  5.8 0.0 copy-start
  5.8 0.0 copy-start.1
  5.8 0.0 copy-start.5
  5.9 0.0 copy-start.6
  5.9 0.0 copy-start.7
  5.9 0.9 %collective-permute-done.4 = f32[6,16,128]{2,1,0:T(8,128)S(1)} collective-permute-done((f32[6,16,128]{2,1,0:T(8,128)S(1)}, f32[6,16,128]{2,1,0:T(8,128)S(1)}, u32[]{:S(2)}, u32[]{:S(2)}) %collective-permute-start.4) | collective-permute-done | bytes 49184 | tf_op jit(solution)/shard_map/ppermute | solution.py:386
  6.8 3.1 %collective-permute-start.5 = (f32[12,16,128]{2,1,0:T(8,128)S(1)}, f32[12,16,128]{2,1,0:T(8,128)S(1)}, u32[]{:S(2)}, u32[]{:S(2)}) collective-permute-start(f32[12,16,128]{2,1,0:T(8,128)S(1)} %pad_maximum_fusion.1), channel_id=1, source_target_pairs={{0,16},{8,24},{16,0},{24,8},{1,17},{9,25},{17,1},{25,9},{2,18},{10... | collective-permute-start | bytes 294920 | tf_op jit(solution)/shard_map/ppermute | solution.py:386
  9.9 2.7 %collective-permute-done.5 = f32[12,16,128]{2,1,0:T(8,128)S(1)} collective-permute-done((f32[12,16,128]{2,1,0:T(8,128)S(1)}, f32[12,16,128]{2,1,0:T(8,128)S(1)}, u32[]{:S(2)}, u32[]{:S(2)}) %collective-permute-start.5) | collective-permute-done | bytes 98336 | tf_op jit(solution)/shard_map/ppermute | solution.py:386
  12.8 0.1 collective-permute-start.6
  12.8 0.7 %collective-permute-start.7 = (f32[512,128]{1,0:T(8,128)S(1)}, f32[512,128]{1,0:T(8,128)S(1)}, u32[]{:S(2)}, u32[]{:S(2)}) collective-permute-start(f32[512,128]{1,0:T(8,128)S(1)} %get-tuple-element.75), channel_id=1, source_target_pairs={{1,2},{3,4},{5,6},{2,1},{4,3},{6,5},{9,10},{11,12},{13,14},{10,9},... | collective-permute-start | bytes 786440 | tf_op jit(solution)/shard_map/ppermute | solution.py:406
  13.5 2.0 %collective-permute-start = (f32[26,16,128]{2,1,0:T(8,128)S(1)}, f32[26,16,128]{2,1,0:T(8,128)S(1)}, u32[]{:S(2)}, u32[]{:S(2)}) collective-permute-start(f32[26,16,128]{2,1,0:T(8,128)S(1)} %get-tuple-element.39), channel_id=1, source_target_pairs={{0,8},{8,0},{16,24},{24,16},{1,9},{9,1},{17,25},{25,17},{2,10},{10... | collective-permute-start | bytes 638984 | tf_op jit(solution)/shard_map/ppermute | solution.py:386
  15.5 2.9 %collective-permute-start.3 = (f32[26,16,128]{2,1,0:T(8,128)S(1)}, f32[26,16,128]{2,1,0:T(8,128)S(1)}, u32[]{:S(2)}, u32[]{:S(2)}) collective-permute-start(f32[26,16,128]{2,1,0:T(8,128)S(1)} %get-tuple-element.39), channel_id=1, source_target_pairs={{0,24},{8,16},{16,8},{24,0},{1,25},{9,17},{17,9},{25,1},{2,26},{10... | collective-permute-start | bytes 638984 | tf_op jit(solution)/shard_map/ppermute | solution.py:386
  18.4 0.5 collective-permute-start.2
  19.6 0.0 copy-done
  19.6 0.0 copy-done.1
  19.6 0.0 copy-done.5
  19.6 0.0 copy-done.6
  19.6 0.0 copy-done.7
  19.6 2.4 %shard_map.113 = (f32[2432,128]{1,0:T(8,128)S(1)}, f32[2432,128]{1,0:T(8,128)S(1)}, f32[2432,128]{1,0:T(8,128)S(1)}, f32[2048,128]{1,0:T(8,128)S(1)}, f32[2432,1...) custom-call(f32[3]{0:T(128)S(1)} %copy-done.5, ...), custom_call_target="tpu_custom_call" | custom-call | tf_op jit(solution)/shard_map/pallas_call | solution.py:435
  22.0 0.0 collective-permute-done.6.near
  22.0 2.5 %collective-permute-start.1 = (f32[6,16,128]{2,1,0:T(8,128)S(1)}, f32[6,16,128]{2,1,0:T(8,128)S(1)}, u32[]{:S(2)}, u32[]{:S(2)}) collective-permute-start(f32[6,16,128]{2,1,0:T(8,128)S(1)} %get-tuple-element.40), channel_id=1, source_target_pairs={{0,16},{8,24},{16,0},{24,8},{1,17},{9,25},{17,1},{25,9},{2,18},{10... | collective-permute-start | bytes 147464 | tf_op jit(solution)/shard_map/ppermute | solution.py:386
  24.5 0.0 collective-permute-done.7.far
  24.5 0.0 copy-start.4
  24.5 1.5 %shard_map.114 = (f32[2432,128]{1,0:T(8,128)S(1)}, f32[2432,128]{1,0:T(8,128)S(1)}, f32[2432,128]{1,0:T(8,128)S(1)}, f32[2432,128]{1,0:T(8,128)S(1)}, f32[2176,1...) custom-call(f32[3]{0:T(128)S(1)} %copy-done.5, ...), custom_call_target="tpu_custom_call", output_to_operand_aliasing={{0}: (10, {}), {1}: (11, {}), {2}: (12, {}), {3}: (13, {}),... | custom-call | tf_op jit(solution)/shard_map/pallas_call | solution.py:435
  26.1 10.8 %collective-permute-done.1.refs_1_ = f32[6,16,128]{2,1,0:T(8,128)S(1)} collective-permute-done((f32[6,16,128]{2,1,0:T(8,128)S(1)}, f32[6,16,128]{2,1,0:T(8,128)S(1)}, u32[]{:S(2)}, u32[]{:S(2)}) %collective-permute-start.1) | collective-permute-done | bytes 49184 | tf_op jit(solution)/shard_map/ppermute | solution.py:386
  36.9 0.0 collective-permute-done.2.refs_2_
  36.9 0.0 collective-permute-done.refs_0_
  36.9 0.0 collective-permute-done.3.refs_3_
  36.9 0.0 copy-done.4
  36.9 2.3 %shard_map.115 = (f32[2432,128]{1,0:T(8,128)S(1)}, f32[2432,128]{1,0:T(8,128)S(1)}, f32[2432,128]{1,0:T(8,128)S(1)}, f32[2432,128]{1,0:T(8,128)S(1)}, f32[8,128]{1,0:T(8,128)S(1)}) custom-call(f32[32,16,128]{2,1,0:T(8,128)S(1)} %copy-done.4, ...), custom_call_target="tpu_custom_call", output_to_operand_aliasing={{0}: (12, {}), {1}: (13, {}), {2}: (14, {}), {3}: (15, {})} | custom-call | tf_op jit(solution)/shard_map/pallas_call | solution.py:435
  39.1 0.0 copy-start.2
  39.1 1.8 %collective-permute-start.8 = (f32[8,128]{1,0:T(8,128)S(1)}, f32[8,128]{1,0:T(8,128)S(1)}, u32[]{:S(2)}, u32[]{:S(2)}) collective-permute-start(f32[8,128]{1,0:T(8,128)S(1)} %get-tuple-element.62), channel_id=1, source_target_pairs={{0,1},{1,0},{2,3},{3,2},{4,5},{5,4},{6,7},{7,6},{8,9},{9,8},{10,11... | collective-permute-start | bytes 12296 | tf_op jit(solution)/shard_map/ppermute | solution.py:386
  40.9 0.8 %collective-permute-done.8 = f32[8,128]{1,0:T(8,128)S(1)} collective-permute-done((f32[8,128]{1,0:T(8,128)S(1)}, f32[8,128]{1,0:T(8,128)S(1)}, u32[]{:S(2)}, u32[]{:S(2)}) %collective-permute-start.8) | collective-permute-done | bytes 4128 | tf_op jit(solution)/shard_map/ppermute | solution.py:386
  41.7 3.9 %collective-permute-start.9 = (f32[8,128]{1,0:T(8,128)S(1)}, f32[8,128]{1,0:T(8,128)S(1)}, u32[]{:S(2)}, u32[]{:S(2)}) collective-permute-start(f32[8,128]{1,0:T(8,128)S(1)} %add.6), channel_id=1, source_target_pairs={{0,2},{1,3},{2,0},{3,1},{4,6},{5,7},{6,4},{7,5},{8,10},{9,11},{10,... | collective-permute-start | bytes 12296 | tf_op jit(solution)/shard_map/ppermute | solution.py:386
  45.6 1.6 %collective-permute-done.9 = f32[8,128]{1,0:T(8,128)S(1)} collective-permute-done((f32[8,128]{1,0:T(8,128)S(1)}, f32[8,128]{1,0:T(8,128)S(1)}, u32[]{:S(2)}, u32[]{:S(2)}) %collective-permute-start.9) | collective-permute-done | bytes 4128 | tf_op jit(solution)/shard_map/ppermute | solution.py:386
  47.2 2.1 %collective-permute-start.10 = (f32[8,128]{1,0:T(8,128)S(1)}, f32[8,128]{1,0:T(8,128)S(1)}, u32[]{:S(2)}, u32[]{:S(2)}) collective-permute-start(f32[8,128]{1,0:T(8,128)S(1)} %add.7.mine), channel_id=1, source_target_pairs={{0,4},{1,5},{2,6},{3,7},{4,0},{5,1},{6,2},{7,3},{8,12},{9,13},{10,... | collective-permute-start | bytes 12296 | tf_op jit(solution)/shard_map/ppermute | solution.py:386
  49.9 1.7 %shard_map.116 = (f32[2176,128]{1,0:T(8,128)S(1)}, f32[2176,128]{1,0:T(8,128)S(1)}) custom-call(f32[2304,128]{1,0:T(8,128)S(1)} %get-tuple-element.69.wide), custom_call_target="tpu_custom_call" | custom-call | tf_op jit(solution)/shard_map/pallas_call | solution.py:435
  51.6 0.0 collective-permute-done.10.theirs
  51.6 0.0 copy-done.2
  51.6 5.6 %shard_map.117 = (f32[512,128]{1,0:T(8,128)}, f32[2048,128]{1,0:T(8,128)}, f32[2048,128]{1,0:T(8,128)}) custom-call(f32[1]{0:T(128)S(6)} %copy.40.hinder_t, f32[1]{0:T(128)S(6)} %copy.41.diffuse_t, f32[8,128]{1,0:T(8,128)S(1)} %add.7.mine, f32[8,128]{1,0:T(8,128)S(1)} %collective-permute-done.10.theirs, f32[2432,128]{1,0:T(8,128)S(1)} %get-tuple-element.63.p0, ...), custom_call_target="tpu_custom_call" | custom-call | tf_op jit(solution)/shard_map/pallas_call | solution.py:435
  (18 shorter events, 0.2 us)
Async XLA Ops:
  0.6 1.0 %copy-start.3 = (f32[32,16,128]{2,1,0:T(8,128)S(1)}, f32[32,16,128]{2,1,0:T(8,128)}, u32[]{:S(2)}) copy-start(f32[32,16,128]{2,1,0:T(8,128)} %vp.3) | copy-start | bytes 786436
  1.6 5.2 %collective-permute-start.4 = (f32[6,16,128]{2,1,0:T(8,128)S(1)}, f32[6,16,128]{2,1,0:T(8,128)S(1)}, u32[]{:S(2)}, u32[]{:S(2)}) collective-permute-start(f32[6,16,128]{2,1,0:T(8,128)S(1)} %get-tuple-element.42), channel_id=1, source_target_pairs={{0,8},{8,0},{16,24},{24,16},{1,9},{9,1},{17,25},{25,17},{2,10},{10... | collective-permute-start | bytes 147464 | tf_op jit(solution)/shard_map/ppermute | solution.py:386
  5.8 13.8 %copy-start = (s32[32,64,128]{2,1,0:T(8,128)S(1)}, s32[32,64,128]{2,1,0:T(8,128)}, u32[]{:S(2)}) copy-start(s32[32,64,128]{2,1,0:T(8,128)} %tissue.1) | copy-start | bytes 3145732
  5.8 13.8 %copy-start.1 = (f32[1,32,64,128]{3,2,1,0:T(8,128)S(1)}, f32[1,32,64,128]{3,2,1,0:T(8,128)}, u32[]{:S(2)}) copy-start(f32[1,32,64,128]{3,2,1,0:T(8,128)} %param.16) | copy-start | bytes 3145732
  5.8 13.8 %copy-start.5 = (f32[3]{0:T(128)S(1)}, f32[3]{0:T(128)}, u32[]{:S(2)}) copy-start(f32[3]{0:T(128)} %cond_t.3) | copy-start | bytes 40
  5.9 13.8 %copy-start.6 = (f32[3]{0:T(128)S(1)}, f32[3]{0:T(128)}, u32[]{:S(2)}) copy-start(f32[3]{0:T(128)} %leak_t.3) | copy-start | bytes 40
  5.9 13.8 %copy-start.7 = (f32[1,3]{1,0:T(1,128)S(1)}, f32[1,3]{1,0:T(1,128)}, u32[]{:S(2)}) copy-start(f32[1,3]{1,0:T(1,128)} %bind_t.3) | copy-start | bytes 40
  6.8 5.8 %collective-permute-start.5 = (f32[12,16,128]{2,1,0:T(8,128)S(1)}, f32[12,16,128]{2,1,0:T(8,128)S(1)}, u32[]{:S(2)}, u32[]{:S(2)}) collective-permute-start(f32[12,16,128]{2,1,0:T(8,128)S(1)} %pad_maximum_fusion.1), channel_id=1, source_target_pairs={{0,16},{8,24},{16,0},{24,8},{1,17},{9,25},{17,1},{25,9},{2,18},{10... | collective-permute-start | bytes 294920 | tf_op jit(solution)/shard_map/ppermute | solution.py:386
  12.8 9.2 %collective-permute-start.6 = (f32[512,128]{1,0:T(8,128)S(1)}, f32[512,128]{1,0:T(8,128)S(1)}, u32[]{:S(2)}, u32[]{:S(2)}) collective-permute-start(f32[512,128]{1,0:T(8,128)S(1)} %get-tuple-element.76), channel_id=1, source_target_pairs={{0,1},{1,0},{2,3},{3,2},{4,5},{5,4},{6,7},{7,6},{8,9},{9,8},{10,11... | collective-permute-start | bytes 786440 | tf_op jit(solution)/shard_map/ppermute | solution.py:404
  12.8 11.7 %collective-permute-start.7 = (f32[512,128]{1,0:T(8,128)S(1)}, f32[512,128]{1,0:T(8,128)S(1)}, u32[]{:S(2)}, u32[]{:S(2)}) collective-permute-start(f32[512,128]{1,0:T(8,128)S(1)} %get-tuple-element.75), channel_id=1, source_target_pairs={{1,2},{3,4},{5,6},{2,1},{4,3},{6,5},{9,10},{11,12},{13,14},{10,9},... | collective-permute-start | bytes 786440 | tf_op jit(solution)/shard_map/ppermute | solution.py:406
  13.5 23.3 %collective-permute-start = (f32[26,16,128]{2,1,0:T(8,128)S(1)}, f32[26,16,128]{2,1,0:T(8,128)S(1)}, u32[]{:S(2)}, u32[]{:S(2)}) collective-permute-start(f32[26,16,128]{2,1,0:T(8,128)S(1)} %get-tuple-element.39), channel_id=1, source_target_pairs={{0,8},{8,0},{16,24},{24,16},{1,9},{9,1},{17,25},{25,17},{2,10},{10... | collective-permute-start | bytes 638984 | tf_op jit(solution)/shard_map/ppermute | solution.py:386
  15.5 21.3 %collective-permute-start.3 = (f32[26,16,128]{2,1,0:T(8,128)S(1)}, f32[26,16,128]{2,1,0:T(8,128)S(1)}, u32[]{:S(2)}, u32[]{:S(2)}) collective-permute-start(f32[26,16,128]{2,1,0:T(8,128)S(1)} %get-tuple-element.39), channel_id=1, source_target_pairs={{0,24},{8,16},{16,8},{24,0},{1,25},{9,17},{17,9},{25,1},{2,26},{10... | collective-permute-start | bytes 638984 | tf_op jit(solution)/shard_map/ppermute | solution.py:386
  18.4 18.4 %collective-permute-start.2 = (f32[20,16,128]{2,1,0:T(8,128)S(1)}, f32[20,16,128]{2,1,0:T(8,128)S(1)}, u32[]{:S(2)}, u32[]{:S(2)}) collective-permute-start(f32[20,16,128]{2,1,0:T(8,128)S(1)} %get-tuple-element.41), channel_id=1, source_target_pairs={{0,16},{8,24},{16,0},{24,8},{1,17},{9,25},{17,1},{25,9},{2,18},{10... | collective-permute-start | bytes 491528 | tf_op jit(solution)/shard_map/ppermute | solution.py:386
  22.0 14.9 %collective-permute-start.1 = (f32[6,16,128]{2,1,0:T(8,128)S(1)}, f32[6,16,128]{2,1,0:T(8,128)S(1)}, u32[]{:S(2)}, u32[]{:S(2)}) collective-permute-start(f32[6,16,128]{2,1,0:T(8,128)S(1)} %get-tuple-element.40), channel_id=1, source_target_pairs={{0,16},{8,24},{16,0},{24,8},{1,17},{9,25},{17,1},{25,9},{2,18},{10... | collective-permute-start | bytes 147464 | tf_op jit(solution)/shard_map/ppermute | solution.py:386
  24.5 12.3 %copy-start.4 = (f32[32,16,128]{2,1,0:T(8,128)S(1)}, f32[32,16,128]{2,1,0:T(8,128)}, u32[]{:S(2)}) copy-start(f32[32,16,128]{2,1,0:T(8,128)} %vp.3) | copy-start | bytes 786436
  39.1 12.5 %copy-start.2 = (f32[1,32,64,128]{3,2,1,0:T(8,128)S(1)}, f32[1,32,64,128]{3,2,1,0:T(8,128)}, u32[]{:S(2)}) copy-start(f32[1,32,64,128]{3,2,1,0:T(8,128)} %param.17) | copy-start | bytes 3145732
  39.1 2.6 %collective-permute-start.8 = (f32[8,128]{1,0:T(8,128)S(1)}, f32[8,128]{1,0:T(8,128)S(1)}, u32[]{:S(2)}, u32[]{:S(2)}) collective-permute-start(f32[8,128]{1,0:T(8,128)S(1)} %get-tuple-element.62), channel_id=1, source_target_pairs={{0,1},{1,0},{2,3},{3,2},{4,5},{5,4},{6,7},{7,6},{8,9},{9,8},{10,11... | collective-permute-start | bytes 12296 | tf_op jit(solution)/shard_map/ppermute | solution.py:386
  41.7 5.4 %collective-permute-start.9 = (f32[8,128]{1,0:T(8,128)S(1)}, f32[8,128]{1,0:T(8,128)S(1)}, u32[]{:S(2)}, u32[]{:S(2)}) collective-permute-start(f32[8,128]{1,0:T(8,128)S(1)} %add.6), channel_id=1, source_target_pairs={{0,2},{1,3},{2,0},{3,1},{4,6},{5,7},{6,4},{7,5},{8,10},{9,11},{10,... | collective-permute-start | bytes 12296 | tf_op jit(solution)/shard_map/ppermute | solution.py:386
  47.2 4.4 %collective-permute-start.10 = (f32[8,128]{1,0:T(8,128)S(1)}, f32[8,128]{1,0:T(8,128)S(1)}, u32[]{:S(2)}, u32[]{:S(2)}) collective-permute-start(f32[8,128]{1,0:T(8,128)S(1)} %add.7.mine), channel_id=1, source_target_pairs={{0,4},{1,5},{2,6},{3,7},{4,0},{5,1},{6,2},{7,3},{8,12},{9,13},{10,... | collective-permute-start | bytes 12296 | tf_op jit(solution)/shard_map/ppermute | solution.py:386

commit v4 on v3

--- a/solution.py
+++ b/solution.py
@@ -329,10 +329,9 @@
     rising = jnp.where(lane == lanes - 1, 0.0, diffuse)
     falling = jnp.where(lane == 0, 0.0, diffuse)
 
-    def advance(i):
+    def advance(i, z_out, z_back):
         e = i + TSTEPS
         here, conc = near(press, e), near(wide, i + 1)
-        z_out, z_back = near(zo, i), near(zb, i)
         z_up, z_down = halves(near(kz, e) * (here - near(press, e + 1)), diffuse)
         stay = near(keep, i) - z_up - z_back
         moved = z_out * near(wide, i) + z_down * near(wide, i + 2)
@@ -345,11 +344,11 @@
         y_into, y_low = halves(preceding(flow, 1), falling)
         stay = stay - out - y_low
         moved = moved + y_into * near(wide_low, i) + y_back * near(wide_high, i)
-        drive(e + 2)
         for ref, value in ((zo, z_up), (zb, z_down), (xo, into), (xb, back), (yo, y_into), (yb, y_back), (kept, stay)):
             store(ref, i + 1, value)
         valid = jnp.where(i == 0, has_low, jnp.where(i == layers + 1, has_high, 1.0))
         store(first, i + 1, (stay * conc + moved) * valid)
+        return z_up, z_down
 
     def finish(i):
         here = near(first, i + 1)
@@ -360,25 +359,36 @@
         gain = near(rate, i - 1) * (near(wide, i + 1) + here)
         store(bound_out, i - 1, near(bound, i - 1) + gain)
 
-    for e in range(TSTEPS - 1, TSTEPS + 2):
+    for e in range(TSTEPS - 1, TSTEPS + 3):
         drive(e)
     z_out, z_back = halves(near(kz, TSTEPS - 1) * (near(press, TSTEPS - 1) - near(press, TSTEPS)), diffuse)
     store(zo, 0, z_out)
     store(zb, 0, z_back)
 
-    def begin(i, carry):
-        advance(i)
+    def two(i):
+        z_out, z_back = advance(i, near(zo, i), near(zb, i))
+        advance(i + 1, z_out, z_back)
+        for step in range(TSTEPS + 3, TSTEPS + 5):
+            drive(jnp.minimum(i + step, layers + 2 * TSTEPS))
+
+    def begin(j, carry):
+        two(2 * j)
         return carry
 
-    lax.fori_loop(0, 3, begin, 0)
-
-    def body(i, carry):
-        finish(i - 2)
-        advance(i)
+    lax.fori_loop(0, 2, begin, 0)
+
+    def body(j, carry):
+        finish(2 * j - 3)
+        finish(2 * j - 2)
+        two(2 * j)
         return carry
 
-    lax.fori_loop(3, layers + 2, body, 0)
-    finish(layers)
+    pairs = (layers + 2) // 2
+    lax.fori_loop(2, pairs, body, 0)
+    for i in range(2 * pairs, layers + 2):
+        advance(i, near(zo, i), near(zb, i))
+    for i in range(2 * pairs - 3, layers + 1):
+        finish(i)
 
 
 def swapped(array, axis, bit):

time: 57.4 us -> 56.5 us (0.984)
  Pallas kernels: 14.5 us -> 13.6 us
    pallas_call x6, Pallas kernels: 13.5 us -> 12.5 us  [call(): pl.pallas_call(kernel, out_shape=tuple(outs), in_specs=[smem()] * len(sca...]
where the time goes in v4:
time: 56.5 us; the launch traced here: 56.3 us
  starting transfers between devices  22.5 us (40%)
  waiting for transfers between devices  16.8 us (30%)
  Pallas kernels  13.6 us (24%)
  between operations  2.2 us (4%)
  local copies, waits for them, and re-layouts  1.07 us (2%)
    ppermute x9, starting transfers between devices, swapped(): return lax.ppermute(array, axis, [(i, i ^ bit) for i in range(count)])  21.8 us
    ppermute x9, waiting for transfers between devices, swapped(): return lax.ppermute(array, axis, [(i, i ^ bit) for i in range(count)])  16.8 us
    pallas_call x6, Pallas kernels, call(): pl.pallas_call(kernel, out_shape=tuple(outs), in_specs=[smem()] * len(sca...  12.5 us
  transfers between devices with their start and end apart: 11, of which 5 were waited for; matrix products, arithmetic and copies ran while one was open for 0% of the time, Pallas kernels for 12%

profile of v4, /device:TPU:0, one launch (start us, length us, event | category | flops | bytes accessed | tf_op | source)
XLA Modules:
  0.0 56.3 jit_solution(6073102795050687186)
XLA Ops:
  0.6 0.0 copy-start.3
  0.6 0.9 %copy-done.3 = f32[32,16,128]{2,1,0:T(8,128)S(1)} copy-done((f32[32,16,128]{2,1,0:T(8,128)S(1)}, f32[32,16,128]{2,1,0:T(8,128)}, u32[]{:S(2)}) %copy-start.3) | copy-done | bytes 262168
  1.6 3.1 %collective-permute-start.4 = (f32[6,16,128]{2,1,0:T(8,128)S(1)}, f32[6,16,128]{2,1,0:T(8,128)S(1)}, u32[]{:S(2)}, u32[]{:S(2)}) collective-permute-start(f32[6,16,128]{2,1,0:T(8,128)S(1)} %get-tuple-element.42), channel_id=1, source_target_pairs={{0,8},{8,0},{16,24},{24,16},{1,9},{9,1},{17,25},{25,17},{2,10},{10... | collective-permute-start | bytes 147464 | tf_op jit(solution)/shard_map/ppermute | solution.py:396
  4.8 1.1 %border.1 = (f32[320,128]{1,0:T(8,128)S(1)}, f32[320,128]{1,0:T(8,128)S(1)}) custom-call(s32[32,64,128]{2,1,0:T(8,128)} %tissue.1, f32[32,64,128]{2,1,0:T(8,128)} %bitcast.17), custom_call_target="tpu_custom_call" | custom-call | tf_op jit(solution)/shard_map/border/pallas_call | solution.py:479
  5.8 0.0 copy-start
  5.8 0.0 copy-start.1
  5.8 0.0 copy-start.5
  5.9 0.0 copy-start.6
  5.9 0.0 copy-start.7
  5.9 0.9 %collective-permute-done.4 = f32[6,16,128]{2,1,0:T(8,128)S(1)} collective-permute-done((f32[6,16,128]{2,1,0:T(8,128)S(1)}, f32[6,16,128]{2,1,0:T(8,128)S(1)}, u32[]{:S(2)}, u32[]{:S(2)}) %collective-permute-start.4) | collective-permute-done | bytes 49184 | tf_op jit(solution)/shard_map/ppermute | solution.py:396
  6.8 3.1 %collective-permute-start.5 = (f32[12,16,128]{2,1,0:T(8,128)S(1)}, f32[12,16,128]{2,1,0:T(8,128)S(1)}, u32[]{:S(2)}, u32[]{:S(2)}) collective-permute-start(f32[12,16,128]{2,1,0:T(8,128)S(1)} %pad_maximum_fusion.1), channel_id=1, source_target_pairs={{0,16},{8,24},{16,0},{24,8},{1,17},{9,25},{17,1},{25,9},{2,18},{10... | collective-permute-start | bytes 294920 | tf_op jit(solution)/shard_map/ppermute | solution.py:396
  9.9 2.7 %collective-permute-done.5 = f32[12,16,128]{2,1,0:T(8,128)S(1)} collective-permute-done((f32[12,16,128]{2,1,0:T(8,128)S(1)}, f32[12,16,128]{2,1,0:T(8,128)S(1)}, u32[]{:S(2)}, u32[]{:S(2)}) %collective-permute-start.5) | collective-permute-done | bytes 98336 | tf_op jit(solution)/shard_map/ppermute | solution.py:396
  12.8 0.1 collective-permute-start.6
  12.8 0.7 %collective-permute-start.7 = (f32[512,128]{1,0:T(8,128)S(1)}, f32[512,128]{1,0:T(8,128)S(1)}, u32[]{:S(2)}, u32[]{:S(2)}) collective-permute-start(f32[512,128]{1,0:T(8,128)S(1)} %get-tuple-element.75), channel_id=1, source_target_pairs={{1,2},{3,4},{5,6},{2,1},{4,3},{6,5},{9,10},{11,12},{13,14},{10,9},... | collective-permute-start | bytes 786440 | tf_op jit(solution)/shard_map/ppermute | solution.py:416
  13.5 2.0 %collective-permute-start = (f32[26,16,128]{2,1,0:T(8,128)S(1)}, f32[26,16,128]{2,1,0:T(8,128)S(1)}, u32[]{:S(2)}, u32[]{:S(2)}) collective-permute-start(f32[26,16,128]{2,1,0:T(8,128)S(1)} %get-tuple-element.39), channel_id=1, source_target_pairs={{0,8},{8,0},{16,24},{24,16},{1,9},{9,1},{17,25},{25,17},{2,10},{10... | collective-permute-start | bytes 638984 | tf_op jit(solution)/shard_map/ppermute | solution.py:396
  15.5 2.9 %collective-permute-start.3 = (f32[26,16,128]{2,1,0:T(8,128)S(1)}, f32[26,16,128]{2,1,0:T(8,128)S(1)}, u32[]{:S(2)}, u32[]{:S(2)}) collective-permute-start(f32[26,16,128]{2,1,0:T(8,128)S(1)} %get-tuple-element.39), channel_id=1, source_target_pairs={{0,24},{8,16},{16,8},{24,0},{1,25},{9,17},{17,9},{25,1},{2,26},{10... | collective-permute-start | bytes 638984 | tf_op jit(solution)/shard_map/ppermute | solution.py:396
  18.4 0.5 collective-permute-start.2
  19.6 0.0 copy-done
  19.6 0.0 copy-done.1
  19.6 0.0 copy-done.5
  19.6 0.0 copy-done.6
  19.6 0.0 copy-done.7
  19.6 2.4 %shard_map.113 = (f32[2432,128]{1,0:T(8,128)S(1)}, f32[2432,128]{1,0:T(8,128)S(1)}, f32[2432,128]{1,0:T(8,128)S(1)}, f32[2048,128]{1,0:T(8,128)S(1)}, f32[2432,1...) custom-call(f32[3]{0:T(128)S(1)} %copy-done.5, ...), custom_call_target="tpu_custom_call" | custom-call | tf_op jit(solution)/shard_map/pallas_call | solution.py:445
  22.0 0.0 collective-permute-done.6.near
  22.0 2.5 %collective-permute-start.1 = (f32[6,16,128]{2,1,0:T(8,128)S(1)}, f32[6,16,128]{2,1,0:T(8,128)S(1)}, u32[]{:S(2)}, u32[]{:S(2)}) collective-permute-start(f32[6,16,128]{2,1,0:T(8,128)S(1)} %get-tuple-element.40), channel_id=1, source_target_pairs={{0,16},{8,24},{16,0},{24,8},{1,17},{9,25},{17,1},{25,9},{2,18},{10... | collective-permute-start | bytes 147464 | tf_op jit(solution)/shard_map/ppermute | solution.py:396
  24.5 0.0 collective-permute-done.7.far
  24.5 0.0 copy-start.4
  24.5 1.5 %shard_map.114 = (f32[2432,128]{1,0:T(8,128)S(1)}, f32[2432,128]{1,0:T(8,128)S(1)}, f32[2432,128]{1,0:T(8,128)S(1)}, f32[2432,128]{1,0:T(8,128)S(1)}, f32[2176,1...) custom-call(f32[3]{0:T(128)S(1)} %copy-done.5, ...), custom_call_target="tpu_custom_call", output_to_operand_aliasing={{0}: (10, {}), {1}: (11, {}), {2}: (12, {}), {3}: (13, {}),... | custom-call | tf_op jit(solution)/shard_map/pallas_call | solution.py:445
  26.1 10.8 %collective-permute-done.1.refs_1_ = f32[6,16,128]{2,1,0:T(8,128)S(1)} collective-permute-done((f32[6,16,128]{2,1,0:T(8,128)S(1)}, f32[6,16,128]{2,1,0:T(8,128)S(1)}, u32[]{:S(2)}, u32[]{:S(2)}) %collective-permute-start.1) | collective-permute-done | bytes 49184 | tf_op jit(solution)/shard_map/ppermute | solution.py:396
  36.9 0.0 collective-permute-done.2.refs_2_
  36.9 0.0 collective-permute-done.refs_0_
  36.9 0.0 collective-permute-done.3.refs_3_
  36.9 0.0 copy-done.4
  36.9 2.3 %shard_map.115 = (f32[2432,128]{1,0:T(8,128)S(1)}, f32[2432,128]{1,0:T(8,128)S(1)}, f32[2432,128]{1,0:T(8,128)S(1)}, f32[2432,128]{1,0:T(8,128)S(1)}, f32[8,128]{1,0:T(8,128)S(1)}) custom-call(f32[32,16,128]{2,1,0:T(8,128)S(1)} %copy-done.4, ...), custom_call_target="tpu_custom_call", output_to_operand_aliasing={{0}: (12, {}), {1}: (13, {}), {2}: (14, {}), {3}: (15, {})} | custom-call | tf_op jit(solution)/shard_map/pallas_call | solution.py:445
  39.1 0.0 copy-start.2
  39.1 1.8 %collective-permute-start.8 = (f32[8,128]{1,0:T(8,128)S(1)}, f32[8,128]{1,0:T(8,128)S(1)}, u32[]{:S(2)}, u32[]{:S(2)}) collective-permute-start(f32[8,128]{1,0:T(8,128)S(1)} %get-tuple-element.62), channel_id=1, source_target_pairs={{0,1},{1,0},{2,3},{3,2},{4,5},{5,4},{6,7},{7,6},{8,9},{9,8},{10,11... | collective-permute-start | bytes 12296 | tf_op jit(solution)/shard_map/ppermute | solution.py:396
  40.9 0.8 %collective-permute-done.8 = f32[8,128]{1,0:T(8,128)S(1)} collective-permute-done((f32[8,128]{1,0:T(8,128)S(1)}, f32[8,128]{1,0:T(8,128)S(1)}, u32[]{:S(2)}, u32[]{:S(2)}) %collective-permute-start.8) | collective-permute-done | bytes 4128 | tf_op jit(solution)/shard_map/ppermute | solution.py:396
  41.7 3.9 %collective-permute-start.9 = (f32[8,128]{1,0:T(8,128)S(1)}, f32[8,128]{1,0:T(8,128)S(1)}, u32[]{:S(2)}, u32[]{:S(2)}) collective-permute-start(f32[8,128]{1,0:T(8,128)S(1)} %add.6), channel_id=1, source_target_pairs={{0,2},{1,3},{2,0},{3,1},{4,6},{5,7},{6,4},{7,5},{8,10},{9,11},{10,... | collective-permute-start | bytes 12296 | tf_op jit(solution)/shard_map/ppermute | solution.py:396
  45.6 1.6 %collective-permute-done.9 = f32[8,128]{1,0:T(8,128)S(1)} collective-permute-done((f32[8,128]{1,0:T(8,128)S(1)}, f32[8,128]{1,0:T(8,128)S(1)}, u32[]{:S(2)}, u32[]{:S(2)}) %collective-permute-start.9) | collective-permute-done | bytes 4128 | tf_op jit(solution)/shard_map/ppermute | solution.py:396
  47.2 2.1 %collective-permute-start.10 = (f32[8,128]{1,0:T(8,128)S(1)}, f32[8,128]{1,0:T(8,128)S(1)}, u32[]{:S(2)}, u32[]{:S(2)}) collective-permute-start(f32[8,128]{1,0:T(8,128)S(1)} %add.7.mine), channel_id=1, source_target_pairs={{0,4},{1,5},{2,6},{3,7},{4,0},{5,1},{6,2},{7,3},{8,12},{9,13},{10,... | collective-permute-start | bytes 12296 | tf_op jit(solution)/shard_map/ppermute | solution.py:396
  49.9 1.7 %shard_map.116 = (f32[2176,128]{1,0:T(8,128)S(1)}, f32[2176,128]{1,0:T(8,128)S(1)}) custom-call(f32[2304,128]{1,0:T(8,128)S(1)} %get-tuple-element.69.wide), custom_call_target="tpu_custom_call" | custom-call | tf_op jit(solution)/shard_map/pallas_call | solution.py:445
  51.6 0.0 collective-permute-done.10.theirs
  51.6 0.0 copy-done.2
  51.6 4.6 %shard_map.117 = (f32[512,128]{1,0:T(8,128)}, f32[2048,128]{1,0:T(8,128)}, f32[2048,128]{1,0:T(8,128)}) custom-call(f32[1]{0:T(128)S(6)} %copy.40.hinder_t, f32[1]{0:T(128)S(6)} %copy.41.diffuse_t, f32[8,128]{1,0:T(8,128)S(1)} %add.7.mine, f32[8,128]{1,0:T(8,128)S(1)} %collective-permute-done.10.theirs, f32[2432,128]{1,0:T(8,128)S(1)} %get-tuple-element.63.p0, ...), custom_call_target="tpu_custom_call" | custom-call | tf_op jit(solution)/shard_map/pallas_call | solution.py:445
  (18 shorter events, 0.2 us)
Async XLA Ops:
  0.6 1.0 %copy-start.3 = (f32[32,16,128]{2,1,0:T(8,128)S(1)}, f32[32,16,128]{2,1,0:T(8,128)}, u32[]{:S(2)}) copy-start(f32[32,16,128]{2,1,0:T(8,128)} %vp.3) | copy-start | bytes 786436
  1.6 5.2 %collective-permute-start.4 = (f32[6,16,128]{2,1,0:T(8,128)S(1)}, f32[6,16,128]{2,1,0:T(8,128)S(1)}, u32[]{:S(2)}, u32[]{:S(2)}) collective-permute-start(f32[6,16,128]{2,1,0:T(8,128)S(1)} %get-tuple-element.42), channel_id=1, source_target_pairs={{0,8},{8,0},{16,24},{24,16},{1,9},{9,1},{17,25},{25,17},{2,10},{10... | collective-permute-start | bytes 147464 | tf_op jit(solution)/shard_map/ppermute | solution.py:396
  5.8 13.8 %copy-start = (s32[32,64,128]{2,1,0:T(8,128)S(1)}, s32[32,64,128]{2,1,0:T(8,128)}, u32[]{:S(2)}) copy-start(s32[32,64,128]{2,1,0:T(8,128)} %tissue.1) | copy-start | bytes 3145732
  5.8 13.8 %copy-start.1 = (f32[1,32,64,128]{3,2,1,0:T(8,128)S(1)}, f32[1,32,64,128]{3,2,1,0:T(8,128)}, u32[]{:S(2)}) copy-start(f32[1,32,64,128]{3,2,1,0:T(8,128)} %param.16) | copy-start | bytes 3145732
  5.8 13.8 %copy-start.5 = (f32[3]{0:T(128)S(1)}, f32[3]{0:T(128)}, u32[]{:S(2)}) copy-start(f32[3]{0:T(128)} %cond_t.3) | copy-start | bytes 40
  5.9 13.8 %copy-start.6 = (f32[3]{0:T(128)S(1)}, f32[3]{0:T(128)}, u32[]{:S(2)}) copy-start(f32[3]{0:T(128)} %leak_t.3) | copy-start | bytes 40
  5.9 13.8 %copy-start.7 = (f32[1,3]{1,0:T(1,128)S(1)}, f32[1,3]{1,0:T(1,128)}, u32[]{:S(2)}) copy-start(f32[1,3]{1,0:T(1,128)} %bind_t.3) | copy-start | bytes 40
  6.8 5.8 %collective-permute-start.5 = (f32[12,16,128]{2,1,0:T(8,128)S(1)}, f32[12,16,128]{2,1,0:T(8,128)S(1)}, u32[]{:S(2)}, u32[]{:S(2)}) collective-permute-start(f32[12,16,128]{2,1,0:T(8,128)S(1)} %pad_maximum_fusion.1), channel_id=1, source_target_pairs={{0,16},{8,24},{16,0},{24,8},{1,17},{9,25},{17,1},{25,9},{2,18},{10... | collective-permute-start | bytes 294920 | tf_op jit(solution)/shard_map/ppermute | solution.py:396
  12.8 9.2 %collective-permute-start.6 = (f32[512,128]{1,0:T(8,128)S(1)}, f32[512,128]{1,0:T(8,128)S(1)}, u32[]{:S(2)}, u32[]{:S(2)}) collective-permute-start(f32[512,128]{1,0:T(8,128)S(1)} %get-tuple-element.76), channel_id=1, source_target_pairs={{0,1},{1,0},{2,3},{3,2},{4,5},{5,4},{6,7},{7,6},{8,9},{9,8},{10,11... | collective-permute-start | bytes 786440 | tf_op jit(solution)/shard_map/ppermute | solution.py:414
  12.8 11.7 %collective-permute-start.7 = (f32[512,128]{1,0:T(8,128)S(1)}, f32[512,128]{1,0:T(8,128)S(1)}, u32[]{:S(2)}, u32[]{:S(2)}) collective-permute-start(f32[512,128]{1,0:T(8,128)S(1)} %get-tuple-element.75), channel_id=1, source_target_pairs={{1,2},{3,4},{5,6},{2,1},{4,3},{6,5},{9,10},{11,12},{13,14},{10,9},... | collective-permute-start | bytes 786440 | tf_op jit(solution)/shard_map/ppermute | solution.py:416
  13.5 23.3 %collective-permute-start = (f32[26,16,128]{2,1,0:T(8,128)S(1)}, f32[26,16,128]{2,1,0:T(8,128)S(1)}, u32[]{:S(2)}, u32[]{:S(2)}) collective-permute-start(f32[26,16,128]{2,1,0:T(8,128)S(1)} %get-tuple-element.39), channel_id=1, source_target_pairs={{0,8},{8,0},{16,24},{24,16},{1,9},{9,1},{17,25},{25,17},{2,10},{10... | collective-permute-start | bytes 638984 | tf_op jit(solution)/shard_map/ppermute | solution.py:396
  15.5 21.3 %collective-permute-start.3 = (f32[26,16,128]{2,1,0:T(8,128)S(1)}, f32[26,16,128]{2,1,0:T(8,128)S(1)}, u32[]{:S(2)}, u32[]{:S(2)}) collective-permute-start(f32[26,16,128]{2,1,0:T(8,128)S(1)} %get-tuple-element.39), channel_id=1, source_target_pairs={{0,24},{8,16},{16,8},{24,0},{1,25},{9,17},{17,9},{25,1},{2,26},{10... | collective-permute-start | bytes 638984 | tf_op jit(solution)/shard_map/ppermute | solution.py:396
  18.4 18.4 %collective-permute-start.2 = (f32[20,16,128]{2,1,0:T(8,128)S(1)}, f32[20,16,128]{2,1,0:T(8,128)S(1)}, u32[]{:S(2)}, u32[]{:S(2)}) collective-permute-start(f32[20,16,128]{2,1,0:T(8,128)S(1)} %get-tuple-element.41), channel_id=1, source_target_pairs={{0,16},{8,24},{16,0},{24,8},{1,17},{9,25},{17,1},{25,9},{2,18},{10... | collective-permute-start | bytes 491528 | tf_op jit(solution)/shard_map/ppermute | solution.py:396
  22.0 14.9 %collective-permute-start.1 = (f32[6,16,128]{2,1,0:T(8,128)S(1)}, f32[6,16,128]{2,1,0:T(8,128)S(1)}, u32[]{:S(2)}, u32[]{:S(2)}) collective-permute-start(f32[6,16,128]{2,1,0:T(8,128)S(1)} %get-tuple-element.40), channel_id=1, source_target_pairs={{0,16},{8,24},{16,0},{24,8},{1,17},{9,25},{17,1},{25,9},{2,18},{10... | collective-permute-start | bytes 147464 | tf_op jit(solution)/shard_map/ppermute | solution.py:396
  24.5 12.3 %copy-start.4 = (f32[32,16,128]{2,1,0:T(8,128)S(1)}, f32[32,16,128]{2,1,0:T(8,128)}, u32[]{:S(2)}) copy-start(f32[32,16,128]{2,1,0:T(8,128)} %vp.3) | copy-start | bytes 786436
  39.1 12.5 %copy-start.2 = (f32[1,32,64,128]{3,2,1,0:T(8,128)S(1)}, f32[1,32,64,128]{3,2,1,0:T(8,128)}, u32[]{:S(2)}) copy-start(f32[1,32,64,128]{3,2,1,0:T(8,128)} %param.17) | copy-start | bytes 3145732
  39.1 2.6 %collective-permute-start.8 = (f32[8,128]{1,0:T(8,128)S(1)}, f32[8,128]{1,0:T(8,128)S(1)}, u32[]{:S(2)}, u32[]{:S(2)}) collective-permute-start(f32[8,128]{1,0:T(8,128)S(1)} %get-tuple-element.62), channel_id=1, source_target_pairs={{0,1},{1,0},{2,3},{3,2},{4,5},{5,4},{6,7},{7,6},{8,9},{9,8},{10,11... | collective-permute-start | bytes 12296 | tf_op jit(solution)/shard_map/ppermute | solution.py:396
  41.7 5.4 %collective-permute-start.9 = (f32[8,128]{1,0:T(8,128)S(1)}, f32[8,128]{1,0:T(8,128)S(1)}, u32[]{:S(2)}, u32[]{:S(2)}) collective-permute-start(f32[8,128]{1,0:T(8,128)S(1)} %add.6), channel_id=1, source_target_pairs={{0,2},{1,3},{2,0},{3,1},{4,6},{5,7},{6,4},{7,5},{8,10},{9,11},{10,... | collective-permute-start | bytes 12296 | tf_op jit(solution)/shard_map/ppermute | solution.py:396
  47.2 4.4 %collective-permute-start.10 = (f32[8,128]{1,0:T(8,128)S(1)}, f32[8,128]{1,0:T(8,128)S(1)}, u32[]{:S(2)}, u32[]{:S(2)}) collective-permute-start(f32[8,128]{1,0:T(8,128)S(1)} %add.7.mine), channel_id=1, source_target_pairs={{0,4},{1,5},{2,6},{3,7},{4,0},{5,1},{6,2},{7,3},{8,12},{9,13},{10,... | collective-permute-start | bytes 12296 | tf_op jit(solution)/shard_map/ppermute | solution.py:396

commit v5 on v4

--- a/solution.py
+++ b/solution.py
@@ -10,7 +10,7 @@
 TSTEPS = 2
 HALO = TSTEPS + 1
 DT = 0.1
-EARLY = 8
+EARLY = 10
 
 
 def select(labels, values):
@@ -143,7 +143,7 @@
         put(kz, e - 1, before * c)
         return c
 
-    lax.fori_loop(0, layers, own, jnp.zeros(shape, jnp.float32), unroll=2)
+    lax.fori_loop(0, layers, own, jnp.zeros(shape, jnp.float32), unroll=4)
 
 
 def rim_kernel(parts, rim, width, rows, cond_t, leak_t, bind_t, diffuse_t, blocks, near, far, tissue, diag, ratio, *refs):
@@ -201,20 +201,16 @@
 
     faces = (kx, ky, kz)
 
-    def both(e, carry):
+    for e in range(1, rim + HALO - 1):
         image(e, rows, faces, inverse, p0, u0, p_next)
         image(layers + 2 * HALO - 1 - e, rows, faces, inverse, p0, u0, p_next)
-        return carry
-
-    lax.fori_loop(1, rim + HALO - 1, both, 0)
     for e in (HALO - 1, layers + HALO):
         put(u_next, e, following(at(u0, e, rows), 1))
 
     def sum_over(first, count, totals):
-        def body(i, carry):
-            return products(i + HALO, rows, carry, faces, diag, p0, u0, u_next)
-
-        return lax.fori_loop(first, first + count, body, totals)
+        for i in range(first, first + count):
+            totals = products(i + HALO, rows, totals, faces, diag, p0, u0, u_next)
+        return totals
 
     zero = jnp.zeros((8, lanes), jnp.float32)
     totals = sum_over(0, rim - 2, (zero,) * 4)
@@ -278,10 +274,10 @@
         put(high, i, following(conc, 1))
         return carry
 
-    lax.fori_loop(0, low.shape[0] // rows, body, 0, unroll=2)
-
-
-def transport_kernel(width, rows, hinder_t, diffuse_t, mine, theirs, p0, u0, p_next, u_next, kx, ky, kz, rate, keep, wide, wide_low, wide_high, bound, pressure, free_out, bound_out, press, first, kept, zo, zb, xo, xb, yo, yb):
+    lax.fori_loop(0, low.shape[0] // rows, body, 0, unroll=math.gcd(low.shape[0] // rows, 17))
+
+
+def transport_kernel(width, rows, hinder_t, diffuse_t, mine, theirs, p0, u0, p_next, u_next, kx, ky, kz, rate, keep, wide, wide_low, wide_high, bound, pressure_hbm, free_hbm, bound_hbm, press, first, kept, zo, zb, xo, xb, yo, yb, pressure, free_out, bound_out, sems):
     lanes = bound.shape[1]
     layers = bound.shape[0] // rows
     me = lax.axis_index("size")
@@ -384,11 +380,32 @@
         return carry
 
     pairs = (layers + 2) // 2
-    lax.fori_loop(2, pairs, body, 0)
+    chunk = layers // 4
+    copies = [pltpu.make_async_copy(pressure, pressure_hbm, sems.at[0])]
+    copies[0].start()
+
+    def send(first, count):
+        span = pl.ds(first * rows, count * rows)
+        for here, there in ((free_out, free_hbm), (bound_out, bound_hbm)):
+            copy = pltpu.make_async_copy(here.at[span, :], there.at[span, :], sems.at[len(copies)])
+            copy.start()
+            copies.append(copy)
+
+    done, sent = 2, 0
+    for c in range(1, 4):
+        until = (c * chunk + 2) // 2 + 1
+        lax.fori_loop(done, until, body, 0)
+        ready = 2 * until - 4
+        send(sent, ready - sent)
+        done, sent = until, ready
+    lax.fori_loop(done, pairs, body, 0)
     for i in range(2 * pairs, layers + 2):
         advance(i, near(zo, i), near(zb, i))
     for i in range(2 * pairs - 3, layers + 1):
         finish(i)
+    send(sent, layers - sent)
+    for copy in copies:
+        copy.wait()
 
 
 def swapped(array, axis, bit):
@@ -515,13 +532,19 @@
     )
     wide_low, wide_high = call(functools.partial(slide_kernel, rows), [stepped] * 2, [], [wide])
     mine, theirs = total_over(sums, "gz")
-    pressure, free, bound = call(
+    operands = [mine, theirs, p0, u0, p_next, u_next, kx, ky, kz, rate, keep, wide, wide_low, wide_high, bound]
+    outs = (f32(layers * width, lanes), slab, slab)
+    held = [f32((layers + 2 * HALO + 1) * rows, lanes)] + [wider] * 8 + list(outs)
+    size = sum(4 * math.prod(a.shape) for a in operands + held)
+    pressure, free, bound = pl.pallas_call(
         functools.partial(transport_kernel, width, rows),
-        [f32(layers * width, lanes), slab, slab],
-        [hindrance, diffusivity],
-        [mine, theirs, p0, u0, p_next, u_next, kx, ky, kz, rate, keep, wide, wide_low, wide_high, bound],
-        scratch=[f32((layers + 2 * HALO + 1) * rows, lanes)] + [wider] * 8,
-    )
+        out_shape=outs,
+        in_specs=[smem()] * 2 + [vmem()] * len(operands),
+        out_specs=(pl.BlockSpec(memory_space=pltpu.HBM),) * 3,
+        scratch_shapes=[pltpu.VMEM(a.shape, a.dtype) for a in held] + [pltpu.SemaphoreType.DMA((9,))],
+        compiler_params=pltpu.CompilerParams(vmem_limit_bytes=size + (4 << 20)),
+        name="transport",
+    )(hindrance, diffusivity, *operands)
     shape = (1, layers, rows, lanes)
     return pressure.reshape(layers, width, lanes), free.reshape(shape), bound.reshape(shape)
 

time: 56.5 us -> 55.2 us (0.977)
  Pallas kernels: 13.6 us -> 11.1 us
  waiting for transfers between devices: 16.8 us -> 18 us
    pallas_call x6 -> x5, Pallas kernels: 12.5 us -> 5.88 us  [call(): pl.pallas_call(kernel, out_shape=tuple(outs), in_specs=[smem()] * len(sca...]
    pallas_call x0 -> x1, Pallas kernels: none -> 4.18 us  [program(): pl.pallas_call(functools.partial(transport_kernel, width, rows), out_shap...]
    ppermute x9, waiting for transfers between devices: 16.8 us -> 18 us  [swapped(): return lax.ppermute(array, axis, [(i, i ^ bit) for i in range(count)])]
  transfers between devices with their start and end apart: 11 -> 11, of which waited for: 5 -> 6; matrix products, arithmetic and copies ran while one was open for 0% -> 0% of each run, Pallas kernels for 12% -> 8%
where the time goes in v5:
time: 55.2 us; the launch traced here: 55 us
  starting transfers between devices  22.5 us (41%)
  waiting for transfers between devices  18 us (33%)
  Pallas kernels  11.1 us (20%)
  between operations  2.18 us (4%)
  local copies, waits for them, and re-layouts  1.07 us (2%)
    ppermute x9, starting transfers between devices, swapped(): return lax.ppermute(array, axis, [(i, i ^ bit) for i in range(count)])  21.8 us
    ppermute x9, waiting for transfers between devices, swapped(): return lax.ppermute(array, axis, [(i, i ^ bit) for i in range(count)])  18 us
    pallas_call x5, Pallas kernels, call(): pl.pallas_call(kernel, out_shape=tuple(outs), in_specs=[smem()] * len(sca...  5.88 us
    pallas_call x1, Pallas kernels, program(): pl.pallas_call(functools.partial(transport_kernel, width, rows), out_shap...  4.18 us
  transfers between devices with their start and end apart: 11, of which 6 were waited for; matrix products, arithmetic and copies ran while one was open for 0% of the time, Pallas kernels for 8%

profile of v5, /device:TPU:0, one launch (start us, length us, event | category | flops | bytes accessed | tf_op | source)
XLA Modules:
  0.0 55.0 jit_solution(5289812670674604796)
XLA Ops:
  0.6 0.0 copy-start.3
  0.6 0.9 %copy-done.3 = f32[32,16,128]{2,1,0:T(8,128)S(1)} copy-done((f32[32,16,128]{2,1,0:T(8,128)S(1)}, f32[32,16,128]{2,1,0:T(8,128)}, u32[]{:S(2)}) %copy-start.3) | copy-done | bytes 262168
  1.6 3.1 %collective-permute-start.4 = (f32[6,16,128]{2,1,0:T(8,128)S(1)}, f32[6,16,128]{2,1,0:T(8,128)S(1)}, u32[]{:S(2)}, u32[]{:S(2)}) collective-permute-start(f32[6,16,128]{2,1,0:T(8,128)S(1)} %get-tuple-element.42), channel_id=1, source_target_pairs={{0,8},{8,0},{16,24},{24,16},{1,9},{9,1},{17,25},{25,17},{2,10},{10... | collective-permute-start | bytes 147464 | tf_op jit(solution)/shard_map/ppermute | solution.py:413
  4.8 1.1 %border.1 = (f32[320,128]{1,0:T(8,128)S(1)}, f32[320,128]{1,0:T(8,128)S(1)}) custom-call(s32[32,64,128]{2,1,0:T(8,128)} %tissue.1, f32[32,64,128]{2,1,0:T(8,128)} %bitcast.17), custom_call_target="tpu_custom_call" | custom-call | tf_op jit(solution)/shard_map/border/pallas_call | solution.py:496
  5.8 0.0 copy-start
  5.8 0.0 copy-start.1
  5.8 0.0 copy-start.5
  5.9 0.0 copy-start.6
  5.9 0.0 copy-start.7
  5.9 0.9 %collective-permute-done.4 = f32[6,16,128]{2,1,0:T(8,128)S(1)} collective-permute-done((f32[6,16,128]{2,1,0:T(8,128)S(1)}, f32[6,16,128]{2,1,0:T(8,128)S(1)}, u32[]{:S(2)}, u32[]{:S(2)}) %collective-permute-start.4) | collective-permute-done | bytes 49184 | tf_op jit(solution)/shard_map/ppermute | solution.py:413
  6.8 3.1 %collective-permute-start.5 = (f32[12,16,128]{2,1,0:T(8,128)S(1)}, f32[12,16,128]{2,1,0:T(8,128)S(1)}, u32[]{:S(2)}, u32[]{:S(2)}) collective-permute-start(f32[12,16,128]{2,1,0:T(8,128)S(1)} %pad_maximum_fusion.1), channel_id=1, source_target_pairs={{0,16},{8,24},{16,0},{24,8},{1,17},{9,25},{17,1},{25,9},{2,18},{10... | collective-permute-start | bytes 294920 | tf_op jit(solution)/shard_map/ppermute | solution.py:413
  9.9 2.7 %collective-permute-done.5 = f32[12,16,128]{2,1,0:T(8,128)S(1)} collective-permute-done((f32[12,16,128]{2,1,0:T(8,128)S(1)}, f32[12,16,128]{2,1,0:T(8,128)S(1)}, u32[]{:S(2)}, u32[]{:S(2)}) %collective-permute-start.5) | collective-permute-done | bytes 98336 | tf_op jit(solution)/shard_map/ppermute | solution.py:413
  12.8 0.1 collective-permute-start.6
  12.8 0.7 %collective-permute-start.7 = (f32[512,128]{1,0:T(8,128)S(1)}, f32[512,128]{1,0:T(8,128)S(1)}, u32[]{:S(2)}, u32[]{:S(2)}) collective-permute-start(f32[512,128]{1,0:T(8,128)S(1)} %get-tuple-element.75), channel_id=1, source_target_pairs={{1,2},{3,4},{5,6},{2,1},{4,3},{6,5},{9,10},{11,12},{13,14},{10,9},... | collective-permute-start | bytes 786440 | tf_op jit(solution)/shard_map/ppermute | solution.py:433
  13.5 2.0 %collective-permute-start = (f32[26,16,128]{2,1,0:T(8,128)S(1)}, f32[26,16,128]{2,1,0:T(8,128)S(1)}, u32[]{:S(2)}, u32[]{:S(2)}) collective-permute-start(f32[26,16,128]{2,1,0:T(8,128)S(1)} %get-tuple-element.39), channel_id=1, source_target_pairs={{0,8},{8,0},{16,24},{24,16},{1,9},{9,1},{17,25},{25,17},{2,10},{10... | collective-permute-start | bytes 638984 | tf_op jit(solution)/shard_map/ppermute | solution.py:413
  15.5 2.9 %collective-permute-start.3 = (f32[26,16,128]{2,1,0:T(8,128)S(1)}, f32[26,16,128]{2,1,0:T(8,128)S(1)}, u32[]{:S(2)}, u32[]{:S(2)}) collective-permute-start(f32[26,16,128]{2,1,0:T(8,128)S(1)} %get-tuple-element.39), channel_id=1, source_target_pairs={{0,24},{8,16},{16,8},{24,0},{1,25},{9,17},{17,9},{25,1},{2,26},{10... | collective-permute-start | bytes 638984 | tf_op jit(solution)/shard_map/ppermute | solution.py:413
  18.4 0.5 collective-permute-start.2
  19.6 0.0 copy-done
  19.6 0.0 copy-done.1
  19.6 0.0 copy-done.5
  19.6 0.0 copy-done.6
  19.6 0.0 copy-done.7
  19.6 1.8 %shard_map.113 = (f32[2432,128]{1,0:T(8,128)S(1)}, f32[2432,128]{1,0:T(8,128)S(1)}, f32[2432,128]{1,0:T(8,128)S(1)}, f32[2048,128]{1,0:T(8,128)S(1)}, f32[2432,1...) custom-call(f32[3]{0:T(128)S(1)} %copy-done.5, ...), custom_call_target="tpu_custom_call" | custom-call | tf_op jit(solution)/shard_map/pallas_call | solution.py:462
  21.4 0.0 collective-permute-done.6.near
  21.4 2.5 %collective-permute-start.1 = (f32[8,16,128]{2,1,0:T(8,128)S(1)}, f32[8,16,128]{2,1,0:T(8,128)S(1)}, u32[]{:S(2)}, u32[]{:S(2)}) collective-permute-start(f32[8,16,128]{2,1,0:T(8,128)S(1)} %get-tuple-element.40), channel_id=1, source_target_pairs={{0,16},{8,24},{16,0},{24,8},{1,17},{9,25},{17,1},{25,9},{2,18},{10... | collective-permute-start | bytes 196616 | tf_op jit(solution)/shard_map/ppermute | solution.py:413
  23.9 0.0 collective-permute-done.7.far
  23.9 0.0 copy-start.4
  24.0 1.1 %shard_map.114 = (f32[2432,128]{1,0:T(8,128)S(1)}, f32[2432,128]{1,0:T(8,128)S(1)}, f32[2432,128]{1,0:T(8,128)S(1)}, f32[2432,128]{1,0:T(8,128)S(1)}, f32[2176,1...) custom-call(f32[3]{0:T(128)S(1)} %copy-done.5, ...), custom_call_target="tpu_custom_call", output_to_operand_aliasing={{0}: (10, {}), {1}: (11, {}), {2}: (12, {}), {3}: (13, {}),... | custom-call | tf_op jit(solution)/shard_map/pallas_call | solution.py:462
  25.1 11.8 %collective-permute-done.1.refs_1_ = f32[8,16,128]{2,1,0:T(8,128)S(1)} collective-permute-done((f32[8,16,128]{2,1,0:T(8,128)S(1)}, f32[8,16,128]{2,1,0:T(8,128)S(1)}, u32[]{:S(2)}, u32[]{:S(2)}) %collective-permute-start.1) | collective-permute-done | bytes 65568 | tf_op jit(solution)/shard_map/ppermute | solution.py:413
  36.9 0.0 collective-permute-done.2.refs_2_
  36.9 0.0 collective-permute-done.refs_0_
  36.9 0.0 collective-permute-done.3.refs_3_
  36.9 0.0 copy-done.4
  36.9 2.3 %shard_map.115 = (f32[2432,128]{1,0:T(8,128)S(1)}, f32[2432,128]{1,0:T(8,128)S(1)}, f32[2432,128]{1,0:T(8,128)S(1)}, f32[2432,128]{1,0:T(8,128)S(1)}, f32[8,128]{1,0:T(8,128)S(1)}) custom-call(f32[32,16,128]{2,1,0:T(8,128)S(1)} %copy-done.4, ...), custom_call_target="tpu_custom_call", output_to_operand_aliasing={{0}: (12, {}), {1}: (13, {}), {2}: (14, {}), {3}: (15, {})} | custom-call | tf_op jit(solution)/shard_map/pallas_call | solution.py:462
  39.1 0.0 copy-start.2
  39.1 1.8 %collective-permute-start.8 = (f32[8,128]{1,0:T(8,128)S(1)}, f32[8,128]{1,0:T(8,128)S(1)}, u32[]{:S(2)}, u32[]{:S(2)}) collective-permute-start(f32[8,128]{1,0:T(8,128)S(1)} %get-tuple-element.62), channel_id=1, source_target_pairs={{0,1},{1,0},{2,3},{3,2},{4,5},{5,4},{6,7},{7,6},{8,9},{9,8},{10,11... | collective-permute-start | bytes 12296 | tf_op jit(solution)/shard_map/ppermute | solution.py:413
  40.9 0.8 %collective-permute-done.8 = f32[8,128]{1,0:T(8,128)S(1)} collective-permute-done((f32[8,128]{1,0:T(8,128)S(1)}, f32[8,128]{1,0:T(8,128)S(1)}, u32[]{:S(2)}, u32[]{:S(2)}) %collective-permute-start.8) | collective-permute-done | bytes 4128 | tf_op jit(solution)/shard_map/ppermute | solution.py:413
  41.7 3.9 %collective-permute-start.9 = (f32[8,128]{1,0:T(8,128)S(1)}, f32[8,128]{1,0:T(8,128)S(1)}, u32[]{:S(2)}, u32[]{:S(2)}) collective-permute-start(f32[8,128]{1,0:T(8,128)S(1)} %add.6), channel_id=1, source_target_pairs={{0,2},{1,3},{2,0},{3,1},{4,6},{5,7},{6,4},{7,5},{8,10},{9,11},{10,... | collective-permute-start | bytes 12296 | tf_op jit(solution)/shard_map/ppermute | solution.py:413
  45.6 1.6 %collective-permute-done.9 = f32[8,128]{1,0:T(8,128)S(1)} collective-permute-done((f32[8,128]{1,0:T(8,128)S(1)}, f32[8,128]{1,0:T(8,128)S(1)}, u32[]{:S(2)}, u32[]{:S(2)}) %collective-permute-start.9) | collective-permute-done | bytes 4128 | tf_op jit(solution)/shard_map/ppermute | solution.py:413
  47.2 2.1 %collective-permute-start.10 = (f32[8,128]{1,0:T(8,128)S(1)}, f32[8,128]{1,0:T(8,128)S(1)}, u32[]{:S(2)}, u32[]{:S(2)}) collective-permute-start(f32[8,128]{1,0:T(8,128)S(1)} %add.7.mine), channel_id=1, source_target_pairs={{0,4},{1,5},{2,6},{3,7},{4,0},{5,1},{6,2},{7,3},{8,12},{9,13},{10,... | collective-permute-start | bytes 12296 | tf_op jit(solution)/shard_map/ppermute | solution.py:413
  49.9 0.7 %shard_map.116 = (f32[2176,128]{1,0:T(8,128)S(1)}, f32[2176,128]{1,0:T(8,128)S(1)}) custom-call(f32[2304,128]{1,0:T(8,128)S(1)} %get-tuple-element.69.wide), custom_call_target="tpu_custom_call" | custom-call | tf_op jit(solution)/shard_map/pallas_call | solution.py:462
  50.6 0.2 collective-permute-done.10.theirs
  50.8 0.0 copy-done.2
  50.8 4.2 %transport.1 = (f32[512,128]{1,0:T(8,128)}, f32[2048,128]{1,0:T(8,128)}, f32[2048,128]{1,0:T(8,128)}) custom-call(f32[1]{0:T(128)S(6)} %copy.40.hinder_t, f32[1]{0:T(128)S(6)} %copy.41.diffuse_t, f32[8,128]{1,0:T(8,128)S(1)} %add.7.mine, f32[8,128]{1,0:T(8,128)S(1)} %collective-permute-done.10.theirs, f32[2432,128]{1,0:T(8,128)S(1)} %get-tuple-element.63.p0, ...), custom_call_target="tpu_custom_call" | custom-call | tf_op jit(solution)/shard_map/transport/pallas_call | solution.py:539
  (18 shorter events, 0.2 us)
Async XLA Ops:
  0.6 1.0 %copy-start.3 = (f32[32,16,128]{2,1,0:T(8,128)S(1)}, f32[32,16,128]{2,1,0:T(8,128)}, u32[]{:S(2)}) copy-start(f32[32,16,128]{2,1,0:T(8,128)} %vp.3) | copy-start | bytes 786436
  1.6 5.2 %collective-permute-start.4 = (f32[6,16,128]{2,1,0:T(8,128)S(1)}, f32[6,16,128]{2,1,0:T(8,128)S(1)}, u32[]{:S(2)}, u32[]{:S(2)}) collective-permute-start(f32[6,16,128]{2,1,0:T(8,128)S(1)} %get-tuple-element.42), channel_id=1, source_target_pairs={{0,8},{8,0},{16,24},{24,16},{1,9},{9,1},{17,25},{25,17},{2,10},{10... | collective-permute-start | bytes 147464 | tf_op jit(solution)/shard_map/ppermute | solution.py:413
  5.8 13.8 %copy-start = (s32[32,64,128]{2,1,0:T(8,128)S(1)}, s32[32,64,128]{2,1,0:T(8,128)}, u32[]{:S(2)}) copy-start(s32[32,64,128]{2,1,0:T(8,128)} %tissue.1) | copy-start | bytes 3145732
  5.8 13.8 %copy-start.1 = (f32[1,32,64,128]{3,2,1,0:T(8,128)S(1)}, f32[1,32,64,128]{3,2,1,0:T(8,128)}, u32[]{:S(2)}) copy-start(f32[1,32,64,128]{3,2,1,0:T(8,128)} %param.16) | copy-start | bytes 3145732
  5.8 13.8 %copy-start.5 = (f32[3]{0:T(128)S(1)}, f32[3]{0:T(128)}, u32[]{:S(2)}) copy-start(f32[3]{0:T(128)} %cond_t.3) | copy-start | bytes 40
  5.9 13.8 %copy-start.6 = (f32[3]{0:T(128)S(1)}, f32[3]{0:T(128)}, u32[]{:S(2)}) copy-start(f32[3]{0:T(128)} %leak_t.3) | copy-start | bytes 40
  5.9 13.8 %copy-start.7 = (f32[1,3]{1,0:T(1,128)S(1)}, f32[1,3]{1,0:T(1,128)}, u32[]{:S(2)}) copy-start(f32[1,3]{1,0:T(1,128)} %bind_t.3) | copy-start | bytes 40
  6.8 5.8 %collective-permute-start.5 = (f32[12,16,128]{2,1,0:T(8,128)S(1)}, f32[12,16,128]{2,1,0:T(8,128)S(1)}, u32[]{:S(2)}, u32[]{:S(2)}) collective-permute-start(f32[12,16,128]{2,1,0:T(8,128)S(1)} %pad_maximum_fusion.1), channel_id=1, source_target_pairs={{0,16},{8,24},{16,0},{24,8},{1,17},{9,25},{17,1},{25,9},{2,18},{10... | collective-permute-start | bytes 294920 | tf_op jit(solution)/shard_map/ppermute | solution.py:413
  12.8 8.6 %collective-permute-start.6 = (f32[512,128]{1,0:T(8,128)S(1)}, f32[512,128]{1,0:T(8,128)S(1)}, u32[]{:S(2)}, u32[]{:S(2)}) collective-permute-start(f32[512,128]{1,0:T(8,128)S(1)} %get-tuple-element.76), channel_id=1, source_target_pairs={{0,1},{1,0},{2,3},{3,2},{4,5},{5,4},{6,7},{7,6},{8,9},{9,8},{10,11... | collective-permute-start | bytes 786440 | tf_op jit(solution)/shard_map/ppermute | solution.py:431
  12.8 11.1 %collective-permute-start.7 = (f32[512,128]{1,0:T(8,128)S(1)}, f32[512,128]{1,0:T(8,128)S(1)}, u32[]{:S(2)}, u32[]{:S(2)}) collective-permute-start(f32[512,128]{1,0:T(8,128)S(1)} %get-tuple-element.75), channel_id=1, source_target_pairs={{1,2},{3,4},{5,6},{2,1},{4,3},{6,5},{9,10},{11,12},{13,14},{10,9},... | collective-permute-start | bytes 786440 | tf_op jit(solution)/shard_map/ppermute | solution.py:433
  13.5 23.3 %collective-permute-start = (f32[26,16,128]{2,1,0:T(8,128)S(1)}, f32[26,16,128]{2,1,0:T(8,128)S(1)}, u32[]{:S(2)}, u32[]{:S(2)}) collective-permute-start(f32[26,16,128]{2,1,0:T(8,128)S(1)} %get-tuple-element.39), channel_id=1, source_target_pairs={{0,8},{8,0},{16,24},{24,16},{1,9},{9,1},{17,25},{25,17},{2,10},{10... | collective-permute-start | bytes 638984 | tf_op jit(solution)/shard_map/ppermute | solution.py:413
  15.5 21.3 %collective-permute-start.3 = (f32[26,16,128]{2,1,0:T(8,128)S(1)}, f32[26,16,128]{2,1,0:T(8,128)S(1)}, u32[]{:S(2)}, u32[]{:S(2)}) collective-permute-start(f32[26,16,128]{2,1,0:T(8,128)S(1)} %get-tuple-element.39), channel_id=1, source_target_pairs={{0,24},{8,16},{16,8},{24,0},{1,25},{9,17},{17,9},{25,1},{2,26},{10... | collective-permute-start | bytes 638984 | tf_op jit(solution)/shard_map/ppermute | solution.py:413
  18.4 18.4 %collective-permute-start.2 = (f32[18,16,128]{2,1,0:T(8,128)S(1)}, f32[18,16,128]{2,1,0:T(8,128)S(1)}, u32[]{:S(2)}, u32[]{:S(2)}) collective-permute-start(f32[18,16,128]{2,1,0:T(8,128)S(1)} %get-tuple-element.41), channel_id=1, source_target_pairs={{0,16},{8,24},{16,0},{24,8},{1,17},{9,25},{17,1},{25,9},{2,18},{10... | collective-permute-start | bytes 442376 | tf_op jit(solution)/shard_map/ppermute | solution.py:413
  21.4 15.4 %collective-permute-start.1 = (f32[8,16,128]{2,1,0:T(8,128)S(1)}, f32[8,16,128]{2,1,0:T(8,128)S(1)}, u32[]{:S(2)}, u32[]{:S(2)}) collective-permute-start(f32[8,16,128]{2,1,0:T(8,128)S(1)} %get-tuple-element.40), channel_id=1, source_target_pairs={{0,16},{8,24},{16,0},{24,8},{1,17},{9,25},{17,1},{25,9},{2,18},{10... | collective-permute-start | bytes 196616 | tf_op jit(solution)/shard_map/ppermute | solution.py:413
  23.9 12.9 %copy-start.4 = (f32[32,16,128]{2,1,0:T(8,128)S(1)}, f32[32,16,128]{2,1,0:T(8,128)}, u32[]{:S(2)}) copy-start(f32[32,16,128]{2,1,0:T(8,128)} %vp.3) | copy-start | bytes 786436
  39.1 11.7 %copy-start.2 = (f32[1,32,64,128]{3,2,1,0:T(8,128)S(1)}, f32[1,32,64,128]{3,2,1,0:T(8,128)}, u32[]{:S(2)}) copy-start(f32[1,32,64,128]{3,2,1,0:T(8,128)} %param.17) | copy-start | bytes 3145732
  39.1 2.6 %collective-permute-start.8 = (f32[8,128]{1,0:T(8,128)S(1)}, f32[8,128]{1,0:T(8,128)S(1)}, u32[]{:S(2)}, u32[]{:S(2)}) collective-permute-start(f32[8,128]{1,0:T(8,128)S(1)} %get-tuple-element.62), channel_id=1, source_target_pairs={{0,1},{1,0},{2,3},{3,2},{4,5},{5,4},{6,7},{7,6},{8,9},{9,8},{10,11... | collective-permute-start | bytes 12296 | tf_op jit(solution)/shard_map/ppermute | solution.py:413
  41.7 5.4 %collective-permute-start.9 = (f32[8,128]{1,0:T(8,128)S(1)}, f32[8,128]{1,0:T(8,128)S(1)}, u32[]{:S(2)}, u32[]{:S(2)}) collective-permute-start(f32[8,128]{1,0:T(8,128)S(1)} %add.6), channel_id=1, source_target_pairs={{0,2},{1,3},{2,0},{3,1},{4,6},{5,7},{6,4},{7,5},{8,10},{9,11},{10,... | collective-permute-start | bytes 12296 | tf_op jit(solution)/shard_map/ppermute | solution.py:413
  47.2 3.7 %collective-permute-start.10 = (f32[8,128]{1,0:T(8,128)S(1)}, f32[8,128]{1,0:T(8,128)S(1)}, u32[]{:S(2)}, u32[]{:S(2)}) collective-permute-start(f32[8,128]{1,0:T(8,128)S(1)} %add.7.mine), channel_id=1, source_target_pairs={{0,4},{1,5},{2,6},{3,7},{4,0},{5,1},{6,2},{7,3},{8,12},{9,13},{10,... | collective-permute-start | bytes 12296 | tf_op jit(solution)/shard_map/ppermute | solution.py:413
